TPU v7x, 128 devices: a whole 4x4x4 slice. The times are simulated.
128 devices in a mesh: xline: 16 (over z, x), iline: 8 (over y, core).
Axes of the slice: x: 4, y: 4, z: 4, core: 2. Of those that a mesh axis runs over, the one named last changes fastest.
Arguments:
- traces: bfloat16 [65536, 1536], P(('xline', 'iline')), may hold values from -16 to 16
- trace_offset: bfloat16 [65536], P(('xline', 'iline')), may hold values from 0 to 1
- trace_owner: int32 [65536], P(('xline', 'iline')), may hold values from 0 to 127, as said below
- trace_cell: int32 [65536], P(('xline', 'iline')), may hold values from 0 to 7
- slowness: float32 [32, 32, 1536], P('xline', 'iline'), may hold values from 1 to 36
- band_start: int32 [1536], replicated, may hold values from 0 to 1528, as said below
- dip_shift: int32 [9, 32, 32], P(None, 'xline', 'iline'), may hold values from -4 to 4
Outputs:
- smoothed: float32 [32, 32, 1536], P('xline', 'iline')
Inputs may be any that keep to these rules, and one draw needn't show every extreme that they name: `trace_owner`: at most 5 traces of one device (one aligned block of 512 rows) share a bin block, and one particular bin block receives exactly 5 traces from every device. band_start[t] - t lies between -(7) and 0 for every t.
All inputs are finite; a program needn't handle non-finite values.
Results may differ from a plain program's by a relative error of at most 0.0003.
Values may be sent and summed in bfloat16 or wider, within the bound.
No kernel may reach another device: no remote copies, remote signals or barrier semaphores. Data moves between devices by JAX's collectives and lax.ppermute only.
A program may use at most 64 MiB of HBM per device.

v0:
```python
import jax
import jax.numpy as jnp
from jax import lax
from jax.sharding import PartitionSpec as P

BAND = 8
DIP = 4


CENTER_WEIGHT = 0.5
SIDE_WEIGHT = 0.0625


def with_halo(value, sides, width):
    for axis, dim in sides:
        size, length = (lax.axis_size(axis), value.shape[dim])
        up = [(i, (i + 1) % size) for i in range(size - 1)]
        down = [(j, i) for i, j in up]
        last = lax.slice_in_dim(value, length - width, length, axis=dim)
        initial = lax.slice_in_dim(value, 0, width, axis=dim)
        before = lax.ppermute(last, axis, up)
        after = lax.ppermute(initial, axis, down)
        value = jnp.concatenate([before, value, after], axis=dim)
    return value


def corrected_rows(trace_rows, offset_rows, slow_rows, band_start):
    samples = trace_rows.shape[1]
    reach = BAND - 1
    sample_ints = jnp.arange(samples, dtype=jnp.int32)
    sample_times = sample_ints.astype(jnp.float32)
    moveout = jnp.sqrt(
        sample_times[None, :] * sample_times[None, :]
        + (offset_rows * offset_rows)[:, None] * slow_rows
    )
    lead = band_start - sample_ints
    widened = jnp.pad(trace_rows, ((0, 0), (reach, reach)))
    numerator = jnp.zeros(moveout.shape, jnp.float32)
    denominator = jnp.zeros(moveout.shape, jnp.float32)
    for step_ahead in range(-reach, reach + 1):
        inside = (step_ahead >= lead) & (step_ahead <= lead + reach)
        picked = widened[:, reach + step_ahead : reach + step_ahead + samples].astype(jnp.float32)
        distance = (sample_times + float(step_ahead))[None, :] - moveout
        weight = jnp.where(inside[None, :], 1.0 / (1.0 + distance * distance), 0.0)
        numerator = numerator + weight * picked
        denominator = denominator + weight
    return numerator / denominator


def smooth_bins(padded, dip_shift, rows_x, rows_y):
    samples = padded.shape[2]
    result = jnp.zeros((rows_x, rows_y, samples), jnp.float32)
    for neighbour in range(9):
        shift_x = neighbour // 3
        shift_y = neighbour % 3
        window = padded[shift_x : shift_x + rows_x, shift_y : shift_y + rows_y, :]
        widened = jnp.pad(window, ((0, 0), (0, 0), (DIP, DIP)))
        shifted = jnp.zeros((rows_x, rows_y, samples), jnp.float32)
        for lag in range(-DIP, DIP + 1):
            chosen = (dip_shift[neighbour] == lag)[:, :, None]
            shifted = shifted + jnp.where(
                chosen, widened[:, :, DIP + lag : DIP + lag + samples], 0.0
            )
        factor = CENTER_WEIGHT if neighbour == 4 else SIDE_WEIGHT
        result = result + factor * shifted
    return result


def body(traces, trace_offset, trace_owner, trace_cell, slowness, band_start, dip_shift):
    owners = lax.axis_size(("xline", "iline"))
    row_count = traces.shape[0]
    samples = traces.shape[1]
    capacity = max(2, 5 * row_count // (4 * owners))
    rows_x = slowness.shape[0]
    rows_y = slowness.shape[1]
    cell_count = rows_x * rows_y
    row_ids = jnp.arange(row_count, dtype=jnp.int32)
    same_owner = (trace_owner[:, None] == trace_owner[None, :]) & (
        row_ids[None, :] < row_ids[:, None]
    )
    owner_rank = jnp.sum(same_owner.astype(jnp.int32), axis=1)
    slot_index = trace_owner * capacity + owner_rank
    send_traces = jnp.zeros((owners * capacity, samples), jnp.bfloat16).at[slot_index].set(traces)
    send_offsets = jnp.zeros((owners * capacity,), jnp.bfloat16).at[slot_index].set(trace_offset)
    send_cells = (
        jnp.zeros((owners * capacity,), jnp.bfloat16)
        .at[slot_index]
        .set((trace_cell + 1).astype(jnp.bfloat16))
    )
    slow_table = slowness.reshape(cell_count, samples)
    cell_ids = jnp.arange(cell_count, dtype=jnp.int32)
    shaped = (
        send_traces.reshape(owners, capacity, samples),
        send_offsets.reshape(owners, capacity),
        send_cells.reshape(owners, capacity),
    )
    got_traces = lax.all_to_all(
        shaped[0], ("xline", "iline"), split_axis=0, concat_axis=0, tiled=True
    )
    got_offsets = lax.all_to_all(
        shaped[1], ("xline", "iline"), split_axis=0, concat_axis=0, tiled=True
    )
    got_cells = lax.all_to_all(
        shaped[2], ("xline", "iline"), split_axis=0, concat_axis=0, tiled=True
    )
    sources = got_offsets.shape[0]
    item_count = got_offsets.shape[1]
    flat_cells = got_cells.reshape(sources * item_count).astype(jnp.int32) - 1
    picker = (flat_cells[:, None] == cell_ids[None, :]).astype(jnp.float32)
    slow_rows = jnp.dot(picker, slow_table, precision=lax.Precision.HIGHEST)
    moved = corrected_rows(
        got_traces.reshape(sources * item_count, samples),
        got_offsets.reshape(sources * item_count).astype(jnp.float32),
        slow_rows,
        band_start,
    )
    moved_out = moved.reshape(sources, item_count, samples)
    stacked_cells = got_cells.reshape(owners * capacity).astype(jnp.int32) - 1
    members = (cell_ids[:, None] == stacked_cells[None, :]).astype(jnp.float32)
    bin_sums = jnp.dot(
        members, moved_out.reshape(owners * capacity, samples), precision=lax.Precision.HIGHEST
    )
    fold_count = jnp.sum(members, axis=1)
    bin_stack = (bin_sums / jnp.maximum(fold_count, 1.0)[:, None]).reshape(rows_x, rows_y, samples)
    padded = with_halo(bin_stack, (("xline", 0), ("iline", 1)), 1)
    return smooth_bins(padded, dip_shift, rows_x, rows_y)


def solution(mesh):
    return jax.shard_map(
        body,
        mesh=mesh,
        in_specs=(
            P(("xline", "iline"), None),
            P(("xline", "iline")),
            P(("xline", "iline")),
            P(("xline", "iline")),
            P("xline", "iline", None),
            P(),
            P(None, "xline", "iline"),
        ),
        out_specs=P("xline", "iline", None),
        check_vma=False,
    )
```

profile of v0, /device:TPU:7, one launch (start us, length us, event | category | flops | bytes accessed | tf_op | source)
XLA Modules:
  0.0 149.2 jit_solution(11189174244762532904)
XLA Ops:
  0.0 1.0 convert_reduce_fusion
  1.0 0.7 compare_select_fusion
  1.7 3.8 %scatter_custom_fusion = bf16[640]{0:T(1024)(128)(2,1)S(1)} fusion(s32[512]{0:T(512)S(1)} %get-tuple-element.160, bf16[512]{0:T(512)(128)(2,1)S(1)} %get-tuple-element.161, bf16[]{:T(256)} %constant.35.clone.1), kind=kCustom, calls=%fused_computation.272 | custom fusion | bytes 1282 | tf_op jit(solution)/shard_map/scatter | solution.py:88
  5.5 0.9 all_to_all.20
  6.4 10.8 %all-to-all-start = ((bf16[128,1,5]{2,1,0:T(2,128)(2,1)}), bf16[128,1,5]{2,1,0:T(2,128)(2,1)S(1)}, u32[]{:S(2)}, u32[]{:S(2)}) async-start(bf16[128,1,5]{2,1,0:T(2,128)(2,1)} %all_to_all.20), calls=%async_computation | async-start | bytes 131072 | tf_op jit(solution)/shard_map/all_to_all | solution.py:103
  17.1 3.9 %scatter_custom_fusion.1 = bf16[640]{0:T(1024)(128)(2,1)S(1)} fusion(s32[512]{0:T(512)S(1)} %get-tuple-element.160, bf16[512]{0:T(512)(128)(2,1)} %param.8, bf16[]{:T(256)} %constant.35.clone.1), kind=kCustom, calls=%fused_computation.270 | custom fusion | bytes 1792 | tf_op jit(solution)/shard_map/scatter | solution.py:84
  21.0 0.9 all_to_all.21
  21.9 3.2 %all-to-all-done = bf16[128,1,5]{2,1,0:T(2,128)(2,1)S(1)} async-done(((bf16[128,1,5]{2,1,0:T(2,128)(2,1)}), bf16[128,1,5]{2,1,0:T(2,128)(2,1)S(1)}, u32[]{:S(2)}, u32[]{:S(2)}) %all-to-all-start) | async-done | bytes 1312 | tf_op jit(solution)/shard_map/all_to_all | solution.py:103
  25.1 6.6 %all-to-all-start.1 = ((bf16[128,1,5]{2,1,0:T(2,128)(2,1)}), bf16[128,1,5]{2,1,0:T(2,128)(2,1)S(1)}, u32[]{:S(2)}, u32[]{:S(2)}) async-start(bf16[128,1,5]{2,1,0:T(2,128)(2,1)} %all_to_all.21), calls=%async_computation.1 | async-start | bytes 131072 | tf_op jit(solution)/shard_map/all_to_all | solution.py:100
  31.7 4.6 %scatter_custom_fusion.2 = bf16[640,1536]{1,0:T(8,128)(2,1)S(1)} fusion(s32[512]{0:T(512)S(1)} %get-tuple-element.160, bf16[512,1536]{1,0:T(8,128)(2,1)} %param.7, bf16[]{:T(256)} %constant.35.clone.1), kind=kCustom, calls=%fused_computation.58 | custom fusion | bytes 1966592 | tf_op jit(solution)/shard_map/scatter | solution.py:83
  36.3 2.5 %reshape.689 = bf16[128,5,1536]{2,1,0:T(8,128)(2,1)} reshape(bf16[640,1536]{1,0:T(8,128)(2,1)S(1)} %scatter_custom_fusion.2) | data formatting | bytes 3932160 | tf_op jit(solution)/shard_map/reshape | solution.py:93
  38.8 0.9 all-to-all-done.1
  39.7 8.8 %all-to-all-start.2 = ((bf16[128,5,1536]{2,1,0:T(8,128)(2,1)}), bf16[128,5,1536]{2,1,0:T(8,128)(2,1)S(1)}, u32[]{:S(2)}, u32[]{:S(2)}) async-start(bf16[128,5,1536]{2,1,0:T(8,128)(2,1)} %reshape.689), calls=%async_computation.2 | async-start | bytes 6291456 | tf_op jit(solution)/shard_map/all_to_all | solution.py:97
  48.6 0.0 copy-done.1
  48.7 0.0 copy-done.2
  48.7 0.6 compare_and_fusion.14
  49.3 0.2 add_reduce_fusion
  49.6 0.2 sub.130
  49.8 0.2 multiply_reduce_fusion
  50.0 0.2 mul.150
  50.2 0.1 convert_reduce_fusion.1
  50.3 0.0 copy-start.4
  50.3 0.0 copy-start.5
  50.3 0.0 copy-start.6
  50.3 0.0 copy-start.7
  50.3 0.0 copy-start.8
  50.4 0.0 copy-start.9
  50.4 0.0 copy-start.10
  50.4 3.6 %fusion.48 = f32[640,1536]{1,0:T(8,128)} fusion(f32[8,1536]{1,0:T(8,128)S(1)} %reshape.688, s32[640]{0:T(1024)S(1)} %sub.130), kind=kOutput, calls=%fused_computation.61 | convolution fusion | flops 94376960 | bytes 3983872 | tf_op jit(solution)/shard_map/dot_general | solution.py:110
  54.0 34.3 %all-to-all-done.2 = bf16[128,5,1536]{2,1,0:T(8,128)(2,1)S(1)} async-done(((bf16[128,5,1536]{2,1,0:T(8,128)(2,1)}), bf16[128,5,1536]{2,1,0:T(8,128)(2,1)S(1)}, u32[]{:S(2)}, u32[]{:S(2)}) %all-to-all-start.2) | async-done | bytes 1966112 | tf_op jit(solution)/shard_map/all_to_all | solution.py:97
  88.3 2.2 %reshape.690 = bf16[640,1536]{1,0:T(8,128)(2,1)} reshape(bf16[128,5,1536]{2,1,0:T(8,128)(2,1)S(1)} %all-to-all-done.2) | data formatting | bytes 3932160 | tf_op jit(solution)/shard_map/reshape | solution.py:112
  90.5 0.0 copy-done.3
  90.5 0.0 copy-done.4
  90.5 0.0 copy-done.5
  90.6 0.0 copy-start
  90.6 34.1 %fusion.1 = f32[8,1536]{1,0:T(8,128)S(1)} fusion(bf16[640,1536]{1,0:T(8,128)(2,1)} %reshape.690, f32[640,1536]{1,0:T(8,128)} %fusion.48, f32[1536]{0:T(1024)S(1)} %get-tuple-element.162, f32[1536]{0:T(1024)S(1)} %get-tuple-element.163, f32[1536]{0:T(1024)S(1)} %get-tuple-element.164, f32[1536]{0:T(1024)S(1)} %get-tuple-element.165, ...), kind=kOutput, calls=%fused_computation.5 | convolution fusion | flops 228082688 | bytes 6073888 | tf_op jit(solution)/shard_map/dot_general | solution.py:120
  124.7 3.5 %collective-permute-start = (f32[1,4,1536]{2,1,0:T(4,128)S(1)}, f32[1,4,1536]{2,1,0:T(4,128)S(1)}, u32[]{:S(2)}, u32[]{:S(2)}) collective-permute-start(f32[1,4,1536]{2,1,0:T(4,128)S(1)} %get-tuple-element.101), channel_id=1, source_target_pairs={{0,8},{8,16},{16,24},{24,32},{32,40},{40,48},{48,56},{56,64},{64,7... | collective-permute-start | bytes 73736 | tf_op jit(solution)/shard_map/ppermute | solution.py:21
  128.3 2.3 %compare_reduce_fusion.80 = (pred[2,4]{1,0:T(4,128)(4,1)S(1)}, pred[2,4]{1,0:T(4,128)(4,1)S(1)}, pred[2,4]{1,0:T(4,128)(4,1)S(1)}, pred[2,4]{1,0:T(4,128)(4,1)S(...) fusion(s32[9,2,4]{0,2,1:T(4,128)S(1)} %copy-done), kind=kLoop, calls=%fused_computation.268 | loop fusion | flops 496 | bytes 784 | tf_op jit(solution)/shard_map/eq | solution.py:60
  130.6 1.9 %collective-permute-start.1 = (f32[1,4,1536]{2,1,0:T(4,128)S(1)}, f32[1,4,1536]{2,1,0:T(4,128)S(1)}, u32[]{:S(2)}, u32[]{:S(2)}) collective-permute-start(f32[1,4,1536]{2,1,0:T(4,128)S(1)} %get-tuple-element.100), channel_id=1, source_target_pairs={{8,0},{16,8},{24,16},{32,24},{40,32},{48,40},{56,48},{64,56},{72,6... | collective-permute-start | bytes 73736 | tf_op jit(solution)/shard_map/ppermute | solution.py:22
  132.6 0.0 collective-permute-done
  132.6 4.7 %collective-permute-done.1 = f32[1,4,1536]{2,1,0:T(4,128)S(1)} collective-permute-done((f32[1,4,1536]{2,1,0:T(4,128)S(1)}, f32[1,4,1536]{2,1,0:T(4,128)S(1)}, u32[]{:S(2)}, u32[]{:S(2)}) %collective-permute-start.1) | collective-permute-done | bytes 24608 | tf_op jit(solution)/shard_map/ppermute | solution.py:22
  137.4 3.6 %collective-permute-start.2 = (f32[4,1,1536]{2,1,0:T(1,128)S(1)}, f32[4,1,1536]{2,1,0:T(1,128)S(1)}, u32[]{:S(2)}, u32[]{:S(2)}) collective-permute-start(f32[4,1,1536]{2,1,0:T(1,128)S(1)} %get-tuple-element.95), channel_id=1, source_target_pairs={{0,1},{1,2},{2,3},{3,4},{4,5},{5,6},{6,7},{8,9},{9,10},{10,11},{11... | collective-permute-start | bytes 73736 | tf_op jit(solution)/shard_map/ppermute | solution.py:21
  141.0 2.6 %collective-permute-start.3 = (f32[4,1,1536]{2,1,0:T(1,128)S(1)}, f32[4,1,1536]{2,1,0:T(1,128)S(1)}, u32[]{:S(2)}, u32[]{:S(2)}) collective-permute-start(f32[4,1,1536]{2,1,0:T(1,128)S(1)} %get-tuple-element.96), channel_id=1, source_target_pairs={{1,0},{2,1},{3,2},{4,3},{5,4},{6,5},{7,6},{9,8},{10,9},{11,10},{12... | collective-permute-start | bytes 73736 | tf_op jit(solution)/shard_map/ppermute | solution.py:22
  143.6 0.8 compare_reduce_fusion.53
  144.4 0.0 collective-permute-done.2
  144.4 1.7 %collective-permute-done.3 = f32[4,1,1536]{2,1,0:T(1,128)S(1)} collective-permute-done((f32[4,1,1536]{2,1,0:T(1,128)S(1)}, f32[4,1,1536]{2,1,0:T(1,128)S(1)}, u32[]{:S(2)}, u32[]{:S(2)}) %collective-permute-start.3) | collective-permute-done | bytes 24608 | tf_op jit(solution)/shard_map/ppermute | solution.py:22
  146.1 0.1 pad_maximum_fusion.7
  146.2 2.9 %multiply_add_fusion = f32[2,4,1536]{2,1,0:T(4,128)} fusion(f32[2,4,1536]{2,1,0:T(4,128)S(1)} %get-tuple-element.92, f32[2,4,1536]{2,1,0:T(4,128)S(1)} %get-tuple-element.98, f32[2,4,1536]{2,1,0:T(4,128)S(1)} %get-tuple-element.88, f32[2,4,1536]{2,1,0:T(4,128)S(1)} %get-tuple-element.93, f32[2,4,1536]{2,1,0:T(4,128)S(1)} %reshape.691, ...), kind=kLoop, calls=%fused_computation.73 | loop fusion | flops 2052096 | bytes 492168 | tf_op jit(solution)/shard_map/add | solution.py:65
  (26 shorter events, 0.2 us)
Async XLA Ops:
  6.4 18.8 %all-to-all-start = ((bf16[128,1,5]{2,1,0:T(2,128)(2,1)}), bf16[128,1,5]{2,1,0:T(2,128)(2,1)S(1)}, u32[]{:S(2)}, u32[]{:S(2)}) async-start(bf16[128,1,5]{2,1,0:T(2,128)(2,1)} %all_to_all.20), calls=%async_computation | async-start | bytes 131072 | tf_op jit(solution)/shard_map/all_to_all | solution.py:103
  25.1 14.6 %all-to-all-start.1 = ((bf16[128,1,5]{2,1,0:T(2,128)(2,1)}), bf16[128,1,5]{2,1,0:T(2,128)(2,1)S(1)}, u32[]{:S(2)}, u32[]{:S(2)}) async-start(bf16[128,1,5]{2,1,0:T(2,128)(2,1)} %all_to_all.21), calls=%async_computation.1 | async-start | bytes 131072 | tf_op jit(solution)/shard_map/all_to_all | solution.py:100
  38.8 9.8 %copy-start.1 = (f32[2,4,1536]{2,1,0:T(4,128)S(1)}, f32[2,4,1536]{2,1,0:T(4,128)}, u32[]{:S(2)}) copy-start(f32[2,4,1536]{2,1,0:T(4,128)} %param.11) | copy-start | bytes 147460
  38.8 9.9 %copy-start.2 = (s32[1536]{0:T(1024)S(1)}, s32[1536]{0:T(1024)}, u32[]{:S(2)}) copy-start(s32[1536]{0:T(1024)} %param.12) | copy-start | bytes 18436
  39.7 48.6 %all-to-all-start.2 = ((bf16[128,5,1536]{2,1,0:T(8,128)(2,1)}), bf16[128,5,1536]{2,1,0:T(8,128)(2,1)S(1)}, u32[]{:S(2)}, u32[]{:S(2)}) async-start(bf16[128,5,1536]{2,1,0:T(8,128)(2,1)} %reshape.689), calls=%async_computation.2 | async-start | bytes 6291456 | tf_op jit(solution)/shard_map/all_to_all | solution.py:97
  50.3 40.2 %copy-start.3 = (pred[1536]{0:T(1024)(128)(4,1)S(1)}, pred[1536]{0:T(1024)(128)(4,1)}, u32[]{:S(2)}) copy-start(pred[1536]{0:T(1024)(128)(4,1)} %get-tuple-element.109) | copy-start | bytes 4612
  50.3 40.2 %copy-start.4 = (pred[1536]{0:T(1024)(128)(4,1)S(1)}, pred[1536]{0:T(1024)(128)(4,1)}, u32[]{:S(2)}) copy-start(pred[1536]{0:T(1024)(128)(4,1)} %get-tuple-element.110) | copy-start | bytes 4612
  50.3 40.2 %copy-start.5 = (pred[1536]{0:T(1024)(128)(4,1)S(1)}, pred[1536]{0:T(1024)(128)(4,1)}, u32[]{:S(2)}) copy-start(pred[1536]{0:T(1024)(128)(4,1)} %get-tuple-element.111) | copy-start | bytes 4612
  50.3 40.2 %copy-start.6 = (pred[1536]{0:T(1024)(128)(4,1)S(1)}, pred[1536]{0:T(1024)(128)(4,1)}, u32[]{:S(2)}) copy-start(pred[1536]{0:T(1024)(128)(4,1)} %get-tuple-element.112) | copy-start | bytes 4612
  50.3 40.2 %copy-start.7 = (pred[1536]{0:T(1024)(128)(4,1)S(1)}, pred[1536]{0:T(1024)(128)(4,1)}, u32[]{:S(2)}) copy-start(pred[1536]{0:T(1024)(128)(4,1)} %get-tuple-element.113) | copy-start | bytes 4612
  50.3 40.2 %copy-start.8 = (pred[1536]{0:T(1024)(128)(4,1)S(1)}, pred[1536]{0:T(1024)(128)(4,1)}, u32[]{:S(2)}) copy-start(pred[1536]{0:T(1024)(128)(4,1)} %get-tuple-element.114) | copy-start | bytes 4612
  50.4 40.2 %copy-start.9 = (pred[1536]{0:T(1024)(128)(4,1)S(1)}, pred[1536]{0:T(1024)(128)(4,1)}, u32[]{:S(2)}) copy-start(pred[1536]{0:T(1024)(128)(4,1)} %get-tuple-element.115) | copy-start | bytes 4612
  50.4 40.2 %copy-start.10 = (pred[1536]{0:T(1024)(128)(4,1)S(1)}, pred[1536]{0:T(1024)(128)(4,1)}, u32[]{:S(2)}) copy-start(pred[1536]{0:T(1024)(128)(4,1)} %get-tuple-element.116) | copy-start | bytes 4612
  90.6 37.7 %copy-start = (s32[9,2,4]{0,2,1:T(4,128)S(1)}, s32[9,2,4]{0,2,1:T(4,128)}, u32[]{:S(2)}) copy-start(s32[9,2,4]{0,2,1:T(4,128)} %param.13) | copy-start | bytes 868
  124.7 7.8 %collective-permute-start = (f32[1,4,1536]{2,1,0:T(4,128)S(1)}, f32[1,4,1536]{2,1,0:T(4,128)S(1)}, u32[]{:S(2)}, u32[]{:S(2)}) collective-permute-start(f32[1,4,1536]{2,1,0:T(4,128)S(1)} %get-tuple-element.101), channel_id=1, source_target_pairs={{0,8},{8,16},{16,24},{24,32},{32,40},{40,48},{48,56},{56,64},{64,7... | collective-permute-start | bytes 73736 | tf_op jit(solution)/shard_map/ppermute | solution.py:21
  130.6 6.7 %collective-permute-start.1 = (f32[1,4,1536]{2,1,0:T(4,128)S(1)}, f32[1,4,1536]{2,1,0:T(4,128)S(1)}, u32[]{:S(2)}, u32[]{:S(2)}) collective-permute-start(f32[1,4,1536]{2,1,0:T(4,128)S(1)} %get-tuple-element.100), channel_id=1, source_target_pairs={{8,0},{16,8},{24,16},{32,24},{40,32},{48,40},{56,48},{64,56},{72,6... | collective-permute-start | bytes 73736 | tf_op jit(solution)/shard_map/ppermute | solution.py:22
  137.4 7.0 %collective-permute-start.2 = (f32[4,1,1536]{2,1,0:T(1,128)S(1)}, f32[4,1,1536]{2,1,0:T(1,128)S(1)}, u32[]{:S(2)}, u32[]{:S(2)}) collective-permute-start(f32[4,1,1536]{2,1,0:T(1,128)S(1)} %get-tuple-element.95), channel_id=1, source_target_pairs={{0,1},{1,2},{2,3},{3,4},{4,5},{5,6},{6,7},{8,9},{9,10},{10,11},{11... | collective-permute-start | bytes 73736 | tf_op jit(solution)/shard_map/ppermute | solution.py:21
  141.0 5.1 %collective-permute-start.3 = (f32[4,1,1536]{2,1,0:T(1,128)S(1)}, f32[4,1,1536]{2,1,0:T(1,128)S(1)}, u32[]{:S(2)}, u32[]{:S(2)}) collective-permute-start(f32[4,1,1536]{2,1,0:T(1,128)S(1)} %get-tuple-element.96), channel_id=1, source_target_pairs={{1,0},{2,1},{3,2},{4,3},{5,4},{6,5},{7,6},{9,8},{10,9},{11,10},{12... | collective-permute-start | bytes 73736 | tf_op jit(solution)/shard_map/ppermute | solution.py:22
where the time goes:
time: 150 us; the launch traced here: 149 us
  waiting for transfers between devices  44.9 us (30%)
  starting transfers between devices  37.7 us (25%)
  matrix products  37.7 us (25%)
  local copies, waits for them, and re-layouts  19.3 us (13%)
  other arithmetic  9.19 us (6%)
    all_to_all x1, waiting for transfers between devices, body(): lax.all_to_all(shaped[0], ('xline', 'iline'), split_axis=0, concat_axis=0...  34.3 us
    dot_general x1, matrix products, body(): jnp.dot(members, moved_out.reshape(owners * capacity, samples), precision...  34.1 us
    all_to_all x1, starting transfers between devices, body(): lax.all_to_all(shaped[2], ('xline', 'iline'), split_axis=0, concat_axis=0...  10.8 us
    all_to_all x1, starting transfers between devices, body(): lax.all_to_all(shaped[0], ('xline', 'iline'), split_axis=0, concat_axis=0...  8.85 us
    ppermute x2, starting transfers between devices, with_halo(): before = lax.ppermute(last, axis, up)  7.09 us
    all_to_all x1, starting transfers between devices, body(): lax.all_to_all(shaped[1], ('xline', 'iline'), split_axis=0, concat_axis=0...  6.56 us
    ppermute x2, waiting for transfers between devices, with_halo(): after = lax.ppermute(initial, axis, down)  6.46 us
    scatter x1, local copies, waits for them, and re-layouts, body(): jnp.zeros((owners * capacity, samples), jnp.bfloat16).at[slot_index]  4.61 us
  transfers between devices with their start and end apart: 7, of which 5 were waited for; matrix products, arithmetic and copies ran while one was open for 13% of the time, Pallas kernels for 0%

commit v1 on v0

v1 whole, which is shorter than its diff:
```python
import functools

import jax
import jax.numpy as jnp
from jax import lax
from jax.experimental import pallas as pl
from jax.experimental.pallas import tpu as pltpu
from jax.sharding import PartitionSpec as P

BAND = 8
DIP = 4
REACH = BAND - 1
LANES = 128
CAP = 5
ROWS = 64
HALVES = (0.5, 1.5, 2.5, 3.5)

CENTER_WEIGHT = 0.5
SIDE_WEIGHT = 0.0625

AXES = ("xline", "iline")
F32 = jnp.float32
BF16 = jnp.bfloat16


def iota(shape, dim):
    return lax.broadcasted_iota(jnp.int32, shape, dim)


def dispatch_kernel(owners, traces_ref, owner_ref, cell_ref, offset_ref, out_ref, stage):
    rows, samples = traces_ref.shape
    blocks = samples // LANES
    owner = owner_ref[...]
    is_owner = iota((owners, rows), 0) == owner
    hot = is_owner.astype(F32)
    earlier = (iota((rows, rows), 0) < iota((rows, rows), 1)).astype(F32).astype(BF16)
    counts = jnp.dot(hot.astype(BF16), earlier, preferred_element_type=F32)
    rank = jnp.sum(hot * counts, axis=0, keepdims=True)
    picks = [jnp.where(rank == float(k), hot, 0.0).astype(BF16) for k in range(CAP)]
    pick = jnp.concatenate(picks, axis=0)
    meta = jnp.zeros((owners, LANES), F32)
    line = iota((LANES, rows), 0)
    offset = offset_ref[...]
    cell = (cell_ref[...] + 1).astype(F32)
    for k in range(CAP):
        source = jnp.where(line == 8 * k, offset, jnp.where(line == 8 * k + 1, cell, 0.0))
        meta = meta + lax.dot_general(
            picks[k], source.astype(BF16), (((1,), (1,)), ((), ())), preferred_element_type=F32
        )
    stage[pl.ds(CAP * blocks, owners, stride=ROWS), :] = meta
    for row in range(CAP * blocks + 1, ROWS):
        stage[pl.ds(row, owners, stride=ROWS), :] = jnp.zeros((owners, LANES), F32)
    placed = jnp.dot(pick, traces_ref[...], preferred_element_type=F32)
    placed = pltpu.roll(placed, REACH, 1)
    for k in range(CAP):
        for block in range(blocks):
            stage[pl.ds(k * blocks + block, owners, stride=ROWS), :] = placed[
                k * owners : (k + 1) * owners, block * LANES : (block + 1) * LANES
            ]
    out_ref[...] = stage[...].astype(BF16)


def dispatch(traces, owner, cell, offset, owners):
    rows, samples = traces.shape
    return pl.pallas_call(
        functools.partial(dispatch_kernel, owners),
        out_shape=jax.ShapeDtypeStruct((owners * ROWS, LANES), BF16),
        scratch_shapes=[pltpu.VMEM((owners * ROWS, LANES), F32)],
        name="dispatch",
    )(traces, owner.reshape(1, rows), cell.reshape(1, rows), offset.astype(F32).reshape(1, rows))


def bands_kernel(start_ref, out_ref):
    block = pl.program_id(0)
    first = start_ref[...] + (REACH - block * LANES)
    place = iota((2 * LANES, LANES), 0) - first
    for i, half in enumerate(HALVES):
        low = (place == int(3.5 - half)).astype(F32)
        high = (place == int(3.5 + half)).astype(F32)
        out_ref[0, :, i * LANES : (i + 1) * LANES] = (0.5 * (low + high)).astype(BF16)
        out_ref[0, :, (4 + i) * LANES : (5 + i) * LANES] = (half * (low - high)).astype(BF16)


def bands(band_start):
    samples = band_start.shape[0]
    blocks = samples // LANES
    return pl.pallas_call(
        bands_kernel,
        grid=(blocks,),
        in_specs=[pl.BlockSpec((1, LANES), lambda b: (0, b))],
        out_specs=pl.BlockSpec((1, 2 * LANES, BAND * LANES), lambda b: (b, 0, 0)),
        out_shape=jax.ShapeDtypeStruct((blocks, 2 * LANES, BAND * LANES), BF16),
        name="bands",
    )(band_start.reshape(1, samples))


def split3(value):
    high = value.astype(BF16)
    rest = value - high.astype(F32)
    middle = rest.astype(BF16)
    low = (rest - middle.astype(F32)).astype(BF16)
    return high, middle, low


def correct(lag, pairs):
    square = lag * lag
    fourth = square * square
    near = [square + (1.0 + h * h) for h in HALVES]
    prod = [(fourth + (1.0 + h * h) ** 2) + (2.0 - 2.0 * h * h) * square for h in HALVES]
    top = [pairs[i] * near[i] + pairs[4 + i] * lag for i in range(4)]
    left, right = prod[0] * prod[1], prod[2] * prod[3]
    num = (top[0] * prod[1] + top[1] * prod[0]) * right + (top[2] * prod[3] + top[3] * prod[2]) * left
    den = (near[0] * prod[1] + near[1] * prod[0]) * right + (near[2] * prod[3] + near[3] * prod[2]) * left
    return num / den


def stack_kernel(got_ref, bands_ref, start_ref, slow_ref, out_ref, stage, window, scaled, member, fold, pairs, moved):
    block = pl.program_id(0)
    blocks = pl.num_programs(0)
    bins = slow_ref.shape[0]
    sources = got_ref.shape[0] // ROWS
    items = CAP * sources

    @pl.when(block == 0)
    def _():
        stage[...] = got_ref[...].astype(F32)
        for k in range(CAP):
            for b in range(window.shape[0] - 1):
                rows = stage[pl.ds(k * (window.shape[0] - 1) + b, sources, stride=ROWS), :].astype(BF16)
                window[b, k * sources : (k + 1) * sources, :] = rows
                if b == 0:
                    window[window.shape[0] - 1, k * sources : (k + 1) * sources, :] = rows
        meta = stage[pl.ds(CAP * (window.shape[0] - 1), sources, stride=ROWS), :]
        across = meta.T
        lane = iota((sources, LANES), 1)
        total = jnp.zeros((bins, 1), F32)
        for k in range(CAP):
            offset = meta[:, 8 * k : 8 * k + 1]
            cell = meta[:, 8 * k + 1 : 8 * k + 2] - 1.0
            square = offset * offset
            high = square.astype(BF16).astype(F32)
            low = square - high
            part = jnp.where(lane < 3 * bins, high, low)
            keep = ((lane % bins).astype(F32) == cell) & (lane < 6 * bins)
            scaled[k * sources : (k + 1) * sources, :] = jnp.where(keep, part, 0.0).astype(BF16)
            same = across[8 * k + 1 : 8 * k + 2, :] == (iota((bins, sources), 0) + 1).astype(F32)
            ones = same.astype(F32)
            total = total + jnp.sum(ones, axis=1, keepdims=True)
            member[:, k * sources : (k + 1) * sources] = ones.astype(BF16)
        fold[...] = jnp.broadcast_to(jnp.maximum(total, 1.0), fold.shape)

    wide = jnp.concatenate([window[block], window[block + 1]], axis=1)
    pairs[...] = jnp.dot(wide, bands_ref[0], preferred_element_type=F32)
    parts = list(split3(slow_ref[...]))
    table = jnp.concatenate([p.astype(F32) for p in parts + parts] + [jnp.zeros((LANES - 6 * bins, LANES), F32)], axis=0)
    added = jnp.dot(scaled[...], table.astype(BF16), preferred_element_type=F32)
    time = (iota((1, LANES), 1) + block * LANES).astype(F32)
    start = start_ref[...].astype(F32) + 3.5
    step = 32
    for row in range(0, items, step):
        here = slice(row, row + step)
        lag = start - jnp.sqrt(time * time + added[here, :])
        got = [pairs[here, i * LANES : (i + 1) * LANES] for i in range(BAND)]
        value = correct(lag, got)
        high = value.astype(BF16)
        moved[here, :] = high
        moved[items + row : items + row + step, :] = (value - high.astype(F32)).astype(BF16)
    sums = jnp.dot(member[...], moved[:items, :], preferred_element_type=F32) + jnp.dot(
        member[...], moved[items:, :], preferred_element_type=F32
    )
    out_ref[...] = sums / fold[...]


def stack(got, picks, band_start, slowness):
    bins, samples = slowness.shape
    blocks = samples // LANES
    sources = got.shape[0] // ROWS
    items = CAP * sources
    return pl.pallas_call(
        stack_kernel,
        grid=(blocks,),
        in_specs=[
            pl.BlockSpec(got.shape, lambda b: (0, 0)),
            pl.BlockSpec((1, 2 * LANES, BAND * LANES), lambda b: (b, 0, 0)),
            pl.BlockSpec((1, LANES), lambda b: (0, b)),
            pl.BlockSpec((bins, LANES), lambda b: (0, b)),
        ],
        out_specs=pl.BlockSpec((bins, LANES), lambda b: (0, b)),
        out_shape=jax.ShapeDtypeStruct((bins, samples), F32),
        scratch_shapes=[
            pltpu.VMEM(got.shape, F32),
            pltpu.VMEM((blocks + 1, items, LANES), BF16),
            pltpu.VMEM((items, LANES), BF16),
            pltpu.VMEM((bins, items), BF16),
            pltpu.VMEM((bins, LANES), F32),
            pltpu.VMEM((items, BAND * LANES), F32),
            pltpu.VMEM((2 * items, LANES), BF16),
        ],
        name="stack",
    )(got, picks, band_start.reshape(1, samples), slowness)


def smooth_kernel(rows_x, rows_y, padded_ref, dip_ref, out_ref):
    bins = rows_x * rows_y
    samples = padded_ref.shape[2]
    near = []
    for n in range(9):
        dx, dy = n // 3, n % 3
        near.append(
            jnp.concatenate([padded_ref[dx + x, dy : dy + rows_y, :] for x in range(rows_x)], axis=0)
        )
    time = iota((bins, samples), 1)
    result = jnp.zeros((bins, samples), F32)
    for lag in range(-DIP, DIP + 1):
        part = jnp.zeros((bins, samples), F32)
        for n in range(9):
            factor = CENTER_WEIGHT if n == 4 else SIDE_WEIGHT
            weight = jnp.where(dip_ref[:, n : n + 1] == lag, factor, 0.0)
            part = part + weight * near[n]
        if lag:
            part = pltpu.roll(part, (-lag) % samples, 1)
            part = jnp.where((time + lag >= 0) & (time + lag < samples), part, 0.0)
        result = result + part
    out_ref[...] = result


def smooth(padded, dip, rows_x, rows_y):
    samples = padded.shape[2]
    return pl.pallas_call(
        functools.partial(smooth_kernel, rows_x, rows_y),
        out_shape=jax.ShapeDtypeStruct((rows_x * rows_y, samples), F32),
        name="smooth",
    )(padded, dip)


def with_halo(value, sides, width):
    for axis, dim in sides:
        size, length = (lax.axis_size(axis), value.shape[dim])
        up = [(i, (i + 1) % size) for i in range(size - 1)]
        down = [(j, i) for i, j in up]
        last = lax.slice_in_dim(value, length - width, length, axis=dim)
        initial = lax.slice_in_dim(value, 0, width, axis=dim)
        before = lax.ppermute(last, axis, up)
        after = lax.ppermute(initial, axis, down)
        value = jnp.concatenate([before, value, after], axis=dim)
    return value


def body(traces, trace_offset, trace_owner, trace_cell, slowness, band_start, dip_shift):
    owners = lax.axis_size(AXES)
    rows_x, rows_y, samples = slowness.shape
    bins = rows_x * rows_y
    send = dispatch(traces, trace_owner, trace_cell, trace_offset, owners)
    got = lax.all_to_all(send.reshape(owners, ROWS, LANES), AXES, split_axis=0, concat_axis=0, tiled=True)
    picks = bands(band_start)
    stacked = stack(got.reshape(owners * ROWS, LANES), picks, band_start, slowness.reshape(bins, samples))
    padded = with_halo(stacked.reshape(rows_x, rows_y, samples), (("xline", 0), ("iline", 1)), 1)
    dip = jnp.pad(dip_shift.reshape(9, bins).T, ((0, 0), (0, LANES - 9)))
    return smooth(padded, dip, rows_x, rows_y).reshape(rows_x, rows_y, samples)


def solution(mesh):
    return jax.shard_map(
        body,
        mesh=mesh,
        in_specs=(
            P(AXES, None),
            P(AXES),
            P(AXES),
            P(AXES),
            P("xline", "iline", None),
            P(),
            P(None, "xline", "iline"),
        ),
        out_specs=P("xline", "iline", None),
        check_vma=False,
    )
```

time: 150 us -> 96.8 us (0.65)
  the two profiles are of different devices: /device:TPU:7 before, /device:TPU:14 now
where the time goes in v1:
time: 96.8 us; the launch traced here: 96.1 us
  Pallas kernels  39.5 us (41%)
  waiting for transfers between devices  27.6 us (29%)
  starting transfers between devices  20.6 us (21%)
  local copies, waits for them, and re-layouts  6.39 us (7%)
  other arithmetic  2 us (2%)
    pallas_call x1, Pallas kernels, stack(): pl.pallas_call(stack_kernel, grid=(blocks,), in_specs=[pl.BlockSpec(got.s...  22.5 us
    all_to_all x1, waiting for transfers between devices, body(): lax.all_to_all(send.reshape(owners, ROWS, LANES), AXES, split_axis=0, con...  18.5 us
    all_to_all x1, starting transfers between devices, body(): lax.all_to_all(send.reshape(owners, ROWS, LANES), AXES, split_axis=0, con...  10.4 us
    pallas_call x1, Pallas kernels, bands(): pl.pallas_call(bands_kernel, grid=(blocks,), in_specs=[pl.BlockSpec((1, L...  7.61 us
    pallas_call x1, Pallas kernels, dispatch(): pl.pallas_call(functools.partial(dispatch_kernel, owners), out_shape=jax....  7.29 us
    ppermute x2, waiting for transfers between devices, with_halo(): after = lax.ppermute(initial, axis, down)  5.43 us
    ppermute x2, starting transfers between devices, with_halo(): before = lax.ppermute(last, axis, up)  5.41 us
    ppermute x2, starting transfers between devices, with_halo(): after = lax.ppermute(initial, axis, down)  4.81 us
  transfers between devices with their start and end apart: 5, of which 3 were waited for; matrix products, arithmetic and copies ran while one was open for 3% of the time, Pallas kernels for 8%

profile of v1, /device:TPU:14, one launch (start us, length us, event | category | flops | bytes accessed | tf_op | source)
XLA Modules:
  0.0 96.1 jit_solution(12835744636877943889)
XLA Ops:
  0.0 1.3 %reshape.46 = f32[512]{0:T(512)} convert(bf16[512]{0:T(512)(128)(2,1)} %param.8) | non-fusion elementwise | flops 512 | bytes 3072 | tf_op jit(solution)/shard_map/reshape | solution.py:70
  1.3 7.3 %dispatch.1 = bf16[8192,128]{1,0:T(8,128)(2,1)} custom-call(bf16[512,1536]{1,0:T(8,128)(2,1)} %traces_ref.1, s32[1,512]{1,0:T(1,128)} %bitcast.16, s32[1,512]{1,0:T(1,128)} %bitcast.17, f32[1,512]{1,0:T(1,128)} %bitcast.14), custom_call_target="tpu_custom_call" | custom-call | tf_op jit(solution)/shard_map/dispatch/pallas_call | solution.py:65
  8.5 0.0 copy-start.2
  8.6 10.4 %all-to-all-start = ((bf16[128,64,128]{2,1,0:T(8,128)(2,1)}), bf16[128,64,128]{2,1,0:T(8,128)(2,1)S(1)}, u32[]{:S(2)}, u32[]{:S(2)}) async-start(bf16[128,64,128]{2,1,0:T(8,128)(2,1)} %bitcast.12), calls=%async_computation | async-start | bytes 4194304 | tf_op jit(solution)/shard_map/all_to_all | solution.py:254
  18.9 0.0 copy-done.2
  18.9 0.6 reshape.41.start_ref
  19.5 0.0 copy-start.1
  19.5 7.6 %bands.1.bands_ref = bf16[12,256,1024]{2,1,0:T(8,128)(2,1)} custom-call(s32[1,1536]{1,0:T(1,128)} %reshape.41.start_ref), custom_call_target="tpu_custom_call" | custom-call | tf_op jit(solution)/shard_map/bands/pallas_call | solution.py:87
  27.2 0.0 copy-done.1
  27.2 0.6 reshape.42.slow_ref
  27.8 18.5 %all-to-all-done = bf16[128,64,128]{2,1,0:T(8,128)(2,1)S(1)} async-done(((bf16[128,64,128]{2,1,0:T(8,128)(2,1)}), bf16[128,64,128]{2,1,0:T(8,128)(2,1)S(1)}, u32[]{:S(2)}, u32[]{:S(2)}) %all-to-all-start) | async-done | bytes 2097184 | tf_op jit(solution)/shard_map/all_to_all | solution.py:254
  46.3 0.0 copy-start
  46.3 1.3 %copy-done = bf16[128,64,128]{2,1,0:T(8,128)(2,1)} copy-done((bf16[128,64,128]{2,1,0:T(8,128)(2,1)}, bf16[128,64,128]{2,1,0:T(8,128)(2,1)S(1)}, u32[]{:S(2)}) %copy-start) | copy-done | bytes 2097176
  47.6 0.0 copy-start.3
  47.6 22.5 %stack.1 = f32[8,1536]{1,0:T(8,128)} custom-call(bf16[8192,128]{1,0:T(8,128)(2,1)} %bitcast.13, bf16[12,256,1024]{2,1,0:T(8,128)(2,1)} %bands.1.bands_ref, s32[1,1536]{1,0:T(1,128)} %reshape.41.start_ref, f32[8,1536]{1,0:T(8,128)} %reshape.42.slow_ref), custom_call_target="tpu_custom_call" | custom-call | tf_op jit(solution)/shard_map/stack/pallas_call | solution.py:179
  70.1 0.9 slice_bitcast_fusion
  71.0 3.5 %collective-permute-start = (f32[1,4,1536]{2,1,0:T(4,128)S(1)}, f32[1,4,1536]{2,1,0:T(4,128)S(1)}, u32[]{:S(2)}, u32[]{:S(2)}) collective-permute-start(f32[1,4,1536]{2,1,0:T(4,128)S(1)} %get-tuple-element.8), channel_id=1, source_target_pairs={{0,8},{8,16},{16,24},{24,32},{32,40},{40,48},{48,56},{56,64},{64,7... | collective-permute-start | bytes 73736 | tf_op jit(solution)/shard_map/ppermute | solution.py:243
  74.5 0.8 reshape.43
  75.3 2.4 %collective-permute-start.1 = (f32[1,4,1536]{2,1,0:T(4,128)S(1)}, f32[1,4,1536]{2,1,0:T(4,128)S(1)}, u32[]{:S(2)}, u32[]{:S(2)}) collective-permute-start(f32[1,4,1536]{2,1,0:T(4,128)S(1)} %get-tuple-element.7), channel_id=1, source_target_pairs={{8,0},{16,8},{24,16},{32,24},{40,32},{48,40},{56,48},{64,56},{72,6... | collective-permute-start | bytes 73736 | tf_op jit(solution)/shard_map/ppermute | solution.py:244
  77.7 0.0 collective-permute-done
  77.7 5.4 %collective-permute-done.1 = f32[1,4,1536]{2,1,0:T(4,128)S(1)} collective-permute-done((f32[1,4,1536]{2,1,0:T(4,128)S(1)}, f32[1,4,1536]{2,1,0:T(4,128)S(1)}, u32[]{:S(2)}, u32[]{:S(2)}) %collective-permute-start.1) | collective-permute-done | bytes 24608 | tf_op jit(solution)/shard_map/ppermute | solution.py:244
  83.2 2.5 %collective-permute-start.3 = (f32[4,1,1536]{2,1,0:T(1,128)S(1)}, f32[4,1,1536]{2,1,0:T(1,128)S(1)}, u32[]{:S(2)}, u32[]{:S(2)}) collective-permute-start(f32[4,1,1536]{2,1,0:T(1,128)S(1)} %get-tuple-element.6), channel_id=1, source_target_pairs={{1,0},{2,1},{3,2},{4,3},{5,4},{6,5},{7,6},{9,8},{10,9},{11,10},{12... | collective-permute-start | bytes 73736 | tf_op jit(solution)/shard_map/ppermute | solution.py:244
  85.7 1.9 %collective-permute-start.2 = (f32[4,1,1536]{2,1,0:T(1,128)S(1)}, f32[4,1,1536]{2,1,0:T(1,128)S(1)}, u32[]{:S(2)}, u32[]{:S(2)}) collective-permute-start(f32[4,1,1536]{2,1,0:T(1,128)S(1)} %get-tuple-element.5), channel_id=1, source_target_pairs={{0,1},{1,2},{2,3},{3,4},{4,5},{5,6},{6,7},{8,9},{9,10},{10,11},{11... | collective-permute-start | bytes 73736 | tf_op jit(solution)/shard_map/ppermute | solution.py:243
  87.6 0.0 copy-done.3
  87.6 0.6 pad.4.dip_ref
  88.2 0.0 collective-permute-done.3
  88.2 3.7 %collective-permute-done.2 = f32[4,1,1536]{2,1,0:T(1,128)S(1)} collective-permute-done((f32[4,1,1536]{2,1,0:T(1,128)S(1)}, f32[4,1,1536]{2,1,0:T(1,128)S(1)}, u32[]{:S(2)}, u32[]{:S(2)}) %collective-permute-start.2) | collective-permute-done | bytes 24608 | tf_op jit(solution)/shard_map/ppermute | solution.py:243
  91.9 0.7 pad_maximum_fusion.padded_ref
  92.6 2.1 %smooth.1 = f32[8,1536]{1,0:T(8,128)} custom-call(f32[4,6,1536]{2,1,0:T(8,128)} %pad_maximum_fusion.padded_ref, s32[8,128]{1,0:T(8,128)} %pad.4.dip_ref), custom_call_target="tpu_custom_call" | custom-call | tf_op jit(solution)/shard_map/smooth/pallas_call | solution.py:229
  94.7 1.4 %reshape.45 = f32[2,4,1536]{2,1,0:T(4,128)} reshape(f32[8,1536]{1,0:T(8,128)} %smooth.1) | data formatting | bytes 98304 | tf_op jit(solution)/shard_map/reshape | solution.py:259
  (4 shorter events, 0.1 us)
Async XLA Ops:
  8.5 10.4 %copy-start.2 = (s32[1536]{0:T(1024)S(1)}, s32[1536]{0:T(1024)}, u32[]{:S(2)}) copy-start(s32[1536]{0:T(1024)} %param.12) | copy-start | bytes 18436
  8.6 37.7 %all-to-all-start = ((bf16[128,64,128]{2,1,0:T(8,128)(2,1)}), bf16[128,64,128]{2,1,0:T(8,128)(2,1)S(1)}, u32[]{:S(2)}, u32[]{:S(2)}) async-start(bf16[128,64,128]{2,1,0:T(8,128)(2,1)} %bitcast.12), calls=%async_computation | async-start | bytes 4194304 | tf_op jit(solution)/shard_map/all_to_all | solution.py:254
  19.5 7.6 %copy-start.1 = (f32[2,4,1536]{2,1,0:T(4,128)S(1)}, f32[2,4,1536]{2,1,0:T(4,128)}, u32[]{:S(2)}) copy-start(f32[2,4,1536]{2,1,0:T(4,128)} %param.11) | copy-start | bytes 147460
  46.3 1.3 %copy-start = (bf16[128,64,128]{2,1,0:T(8,128)(2,1)}, bf16[128,64,128]{2,1,0:T(8,128)(2,1)S(1)}, u32[]{:S(2)}) copy-start(bf16[128,64,128]{2,1,0:T(8,128)(2,1)S(1)} %all-to-all-done) | copy-start | bytes 6291460
  47.6 40.0 %copy-start.3 = (s32[9,2,4]{0,2,1:T(4,128)S(1)}, s32[9,2,4]{0,2,1:T(4,128)}, u32[]{:S(2)}) copy-start(s32[9,2,4]{0,2,1:T(4,128)} %param.13) | copy-start | bytes 868
  71.0 6.7 %collective-permute-start = (f32[1,4,1536]{2,1,0:T(4,128)S(1)}, f32[1,4,1536]{2,1,0:T(4,128)S(1)}, u32[]{:S(2)}, u32[]{:S(2)}) collective-permute-start(f32[1,4,1536]{2,1,0:T(4,128)S(1)} %get-tuple-element.8), channel_id=1, source_target_pairs={{0,8},{8,16},{16,24},{24,32},{32,40},{40,48},{48,56},{56,64},{64,7... | collective-permute-start | bytes 73736 | tf_op jit(solution)/shard_map/ppermute | solution.py:243
  75.3 7.8 %collective-permute-start.1 = (f32[1,4,1536]{2,1,0:T(4,128)S(1)}, f32[1,4,1536]{2,1,0:T(4,128)S(1)}, u32[]{:S(2)}, u32[]{:S(2)}) collective-permute-start(f32[1,4,1536]{2,1,0:T(4,128)S(1)} %get-tuple-element.7), channel_id=1, source_target_pairs={{8,0},{16,8},{24,16},{32,24},{40,32},{48,40},{56,48},{64,56},{72,6... | collective-permute-start | bytes 73736 | tf_op jit(solution)/shard_map/ppermute | solution.py:244
  83.2 5.0 %collective-permute-start.3 = (f32[4,1,1536]{2,1,0:T(1,128)S(1)}, f32[4,1,1536]{2,1,0:T(1,128)S(1)}, u32[]{:S(2)}, u32[]{:S(2)}) collective-permute-start(f32[4,1,1536]{2,1,0:T(1,128)S(1)} %get-tuple-element.6), channel_id=1, source_target_pairs={{1,0},{2,1},{3,2},{4,3},{5,4},{6,5},{7,6},{9,8},{10,9},{11,10},{12... | collective-permute-start | bytes 73736 | tf_op jit(solution)/shard_map/ppermute | solution.py:244
  85.7 6.2 %collective-permute-start.2 = (f32[4,1,1536]{2,1,0:T(1,128)S(1)}, f32[4,1,1536]{2,1,0:T(1,128)S(1)}, u32[]{:S(2)}, u32[]{:S(2)}) collective-permute-start(f32[4,1,1536]{2,1,0:T(1,128)S(1)} %get-tuple-element.5), channel_id=1, source_target_pairs={{0,1},{1,2},{2,3},{3,4},{4,5},{5,6},{6,7},{8,9},{9,10},{10,11},{11... | collective-permute-start | bytes 73736 | tf_op jit(solution)/shard_map/ppermute | solution.py:243

commit v2 on v1

v2 whole, which is shorter than its diff:
```python
import functools

import jax
import jax.numpy as jnp
from jax import lax
from jax.experimental import pallas as pl
from jax.experimental.pallas import tpu as pltpu
from jax.sharding import PartitionSpec as P

BAND = 8
DIP = 4
REACH = BAND - 1
LANES = 128
CAP = 5
ROWS = 64
PITCH = 65
STEP = 32
HALVES = (0.5, 1.5, 2.5, 3.5)
VMEM = pl.BlockSpec(memory_space=pltpu.VMEM)

CENTER_WEIGHT = 0.5
SIDE_WEIGHT = 0.0625

AXES = ("xline", "iline")
F32 = jnp.float32
BF16 = jnp.bfloat16


def iota(shape, dim):
    return lax.broadcasted_iota(jnp.int32, shape, dim)


def dispatch_kernel(owners, traces_hbm, owner_ref, cell_ref, offset_ref, out_ref, traces_ref, stage, arrived):
    copy = pltpu.make_async_copy(traces_hbm, traces_ref, arrived)
    copy.start()
    rows, samples = traces_ref.shape
    blocks = samples // LANES
    owner = owner_ref[...]
    hot = (iota((owners, rows), 0) == owner).astype(F32)
    earlier = (iota((rows, rows), 0) < iota((rows, rows), 1)).astype(F32).astype(BF16)
    counts = jnp.dot(hot.astype(BF16), earlier, preferred_element_type=F32)
    rank = jnp.sum(hot * counts, axis=0, keepdims=True)
    picks = [jnp.where(rank == float(k), hot, 0.0).astype(BF16) for k in range(CAP)]
    pick = jnp.concatenate(picks, axis=0)
    meta = jnp.zeros((owners, LANES), F32)
    line = iota((LANES, rows), 0)
    offset = offset_ref[...]
    cell = (cell_ref[...] + 1).astype(F32)
    for k in range(CAP):
        source = jnp.where(line == 8 * k, offset, jnp.where(line == 8 * k + 1, cell, 0.0))
        meta = meta + lax.dot_general(
            picks[k], source.astype(BF16), (((1,), (1,)), ((), ())), preferred_element_type=F32
        )
    stage[pl.ds(CAP * blocks, owners, stride=PITCH), :] = meta
    for row in range(CAP * blocks + 1, ROWS):
        stage[pl.ds(row, owners, stride=PITCH), :] = jnp.zeros((owners, LANES), F32)
    copy.wait()
    wrapped = iota((CAP * owners, LANES), 1) < REACH

    def put(block, value):
        for k in range(CAP):
            stage[pl.ds(k * blocks + block, owners, stride=PITCH), :] = value[k * owners : (k + 1) * owners, :]

    first = previous = None
    for tile in range(0, samples, 2 * LANES):
        placed = jnp.dot(pick, traces_ref[:, tile : tile + 2 * LANES], preferred_element_type=F32)
        for half in range(2):
            turned = pltpu.roll(placed[:, half * LANES : (half + 1) * LANES], REACH, 1)
            if first is None:
                first = turned
            else:
                put(tile // LANES + half, jnp.where(wrapped, previous, turned))
            previous = turned
    put(0, jnp.where(wrapped, previous, first))
    for owner_row in range(owners):
        out_ref[owner_row * ROWS : (owner_row + 1) * ROWS, :] = stage[
            owner_row * PITCH : owner_row * PITCH + ROWS, :
        ].astype(BF16)


def dispatch(traces, owner, cell, offset, owners):
    rows, samples = traces.shape
    return pl.pallas_call(
        functools.partial(dispatch_kernel, owners),
        in_specs=[pl.BlockSpec(memory_space=pl.ANY), VMEM, VMEM, VMEM],
        out_specs=VMEM,
        out_shape=jax.ShapeDtypeStruct((owners * ROWS, LANES), BF16),
        scratch_shapes=[
            pltpu.VMEM((rows, samples), BF16),
            pltpu.VMEM((owners * PITCH, LANES), F32),
            pltpu.SemaphoreType.DMA,
        ],
        compiler_params=pltpu.CompilerParams(vmem_limit_bytes=24 << 20),
        name="dispatch",
    )(traces, owner.reshape(1, rows), cell.reshape(1, rows), offset.astype(F32).reshape(1, rows))


def bands_kernel(start_ref, out_ref):
    for block in range(out_ref.shape[0]):
        first = start_ref[:, block * LANES : (block + 1) * LANES] + (REACH - block * LANES)
        place = iota((2 * LANES, LANES), 0) - first
        for lag in range(BAND):
            out_ref[block, :, lag * LANES : (lag + 1) * LANES] = (place == lag).astype(F32).astype(BF16)


def bands(band_start):
    samples = band_start.shape[0]
    blocks = samples // LANES
    return pl.pallas_call(
        bands_kernel,
        in_specs=[VMEM],
        out_specs=VMEM,
        out_shape=jax.ShapeDtypeStruct((blocks, 2 * LANES, BAND * LANES), BF16),
        compiler_params=pltpu.CompilerParams(vmem_limit_bytes=24 << 20),
        name="bands",
    )(band_start.reshape(1, samples))


def split3(value):
    high = value.astype(BF16)
    rest = value - high.astype(F32)
    middle = rest.astype(BF16)
    low = (rest - middle.astype(F32)).astype(BF16)
    return high, middle, low


def correct(lag, band):
    square = lag * lag
    num = den = None
    for i, half in enumerate(HALVES):
        even, odd = square + (1.0 + half * half), lag * (2.0 * half)
        low, high = 1.0 / (even - odd), 1.0 / (even + odd)
        below, above = int(3.5 - half), int(3.5 + half)
        part = band(below) * low + band(above) * high
        both = low + high
        num, den = (part, both) if num is None else (num + part, den + both)
    return num / den


def stack_kernel(got_ref, bands_ref, start_ref, slow_ref, out_ref, first_ref, last_ref, stage, window, scaled, member, fold, pairs0, pairs1, added0, added1, moved0, moved1):
    blocks = bands_ref.shape[0]
    bins = slow_ref.shape[0]
    sources = got_ref.shape[0] // ROWS
    items = CAP * sources
    for src in range(sources):
        stage[src * PITCH : src * PITCH + ROWS, :] = got_ref[src * ROWS : (src + 1) * ROWS, :].astype(F32)
    meta = stage[pl.ds(CAP * blocks, sources, stride=PITCH), :]
    across = meta.T
    lane = iota((sources, LANES), 1)
    total = jnp.zeros((bins, 1), F32)
    for k in range(CAP):
        here = slice(k * sources, (k + 1) * sources)
        for b in range(blocks):
            rows = stage[pl.ds(k * blocks + b, sources, stride=PITCH), :].astype(BF16)
            window[b, here, :] = rows
            if b == 0:
                window[blocks, here, :] = rows
        offset = meta[:, 8 * k : 8 * k + 1]
        cell = meta[:, 8 * k + 1 : 8 * k + 2] - 1.0
        square = offset * offset
        high = square.astype(BF16).astype(F32)
        part = jnp.where(lane < 3 * bins, high, square - high)
        keep = ((lane % bins).astype(F32) == cell) & (lane < 6 * bins)
        scaled[here, :] = jnp.where(keep, part, 0.0).astype(BF16)
        ones = (across[8 * k + 1 : 8 * k + 2, :] == (iota((bins, sources), 0) + 1).astype(F32)).astype(F32)
        total = total + jnp.sum(ones, axis=1, keepdims=True)
        member[:, here] = ones.astype(BF16)
    fold[...] = jnp.broadcast_to(jnp.maximum(total, 1.0), fold.shape)

    def lanes(block):
        return pl.ds(pl.multiple_of(block * LANES, LANES), LANES)

    def multiply(block, pairs, added):
        wide = jnp.concatenate([window[block], window[block + 1]], axis=1)
        for half in range(0, BAND, 2):
            cols = slice(half * LANES, (half + 2) * LANES)
            pairs[:, cols] = jnp.dot(wide, bands_ref[block, :, cols], preferred_element_type=F32)
        parts = list(split3(slow_ref[:, lanes(block)]))
        parts = [p.astype(F32) for p in parts + parts] + [jnp.zeros((LANES - 6 * bins, LANES), F32)]
        table = jnp.concatenate(parts, axis=0).astype(BF16)
        added[...] = jnp.dot(scaled[...], table, preferred_element_type=F32)

    def weigh(block, pairs, added, moved):
        ticks = iota((1, LANES), 1) + block * LANES
        time = ticks.astype(F32)
        squared = jnp.where(ticks == 0, 1e-30, time * time)
        start = start_ref[:, lanes(block)].astype(F32) + 3.5
        for row in range(0, items, STEP):
            here = slice(row, row + STEP)
            total = squared + added[here, :]
            lag = start - total * lax.rsqrt(total)
            value = correct(lag, lambda i: pairs[here, i * LANES : (i + 1) * LANES])
            high = value.astype(BF16)
            moved[here, :] = high
            moved[items + row : items + row + STEP, :] = (value - high.astype(F32)).astype(BF16)

    def total_up(block, moved):
        sums = jnp.dot(member[...], moved[:items, :], preferred_element_type=F32) + jnp.dot(
            member[...], moved[items:, :], preferred_element_type=F32
        )
        out_ref[:, lanes(block)] = sums / fold[...]

    multiply(0, pairs0, added0)

    def two_blocks(i, carry):
        block = 2 * i
        multiply(block + 1, pairs1, added1)
        weigh(block, pairs0, added0, moved0)
        total_up(jnp.maximum(block - 1, 0), moved1)
        multiply(jnp.minimum(block + 2, blocks - 1), pairs0, added0)
        weigh(block + 1, pairs1, added1, moved1)
        total_up(block, moved0)
        return carry

    lax.fori_loop(0, blocks // 2, two_blocks, 0)
    total_up(blocks - 1, moved1)
    width = first_ref.shape[0]
    height = bins // width
    for x in range(width):
        first_ref[x : x + 1, :] = out_ref[x * height : x * height + 1, :]
        last_ref[x : x + 1, :] = out_ref[(x + 1) * height - 1 : (x + 1) * height, :]


def stack(got, picks, band_start, slowness, rows_x):
    bins, samples = slowness.shape
    blocks = samples // LANES
    sources = got.shape[0] // ROWS
    items = CAP * sources
    edge = jax.ShapeDtypeStruct((rows_x, samples), F32)
    return pl.pallas_call(
        stack_kernel,
        in_specs=[VMEM] * 4,
        out_specs=[VMEM] * 3,
        out_shape=[jax.ShapeDtypeStruct((bins, samples), F32), edge, edge],
        scratch_shapes=[
            pltpu.VMEM((sources * PITCH, LANES), F32),
            pltpu.VMEM((blocks + 1, items, LANES), BF16),
            pltpu.VMEM((items, LANES), BF16),
            pltpu.VMEM((bins, items), BF16),
            pltpu.VMEM((bins, LANES), F32),
            pltpu.VMEM((items, BAND * LANES), F32),
            pltpu.VMEM((items, BAND * LANES), F32),
            pltpu.VMEM((items, LANES), F32),
            pltpu.VMEM((items, LANES), F32),
            pltpu.VMEM((2 * items, LANES), BF16),
            pltpu.VMEM((2 * items, LANES), BF16),
        ],
        compiler_params=pltpu.CompilerParams(vmem_limit_bytes=40 << 20),
        name="stack",
    )(got, picks, band_start.reshape(1, samples), slowness)


def edges_kernel(stack_ref, before_ref, after_ref, first_ref, last_ref):
    width = before_ref.shape[0]
    height = stack_ref.shape[0] // width
    for x, ref in ((0, first_ref), (width - 1, last_ref)):
        ref[0:1, :] = before_ref[x : x + 1, :]
        ref[1 : height + 1, :] = stack_ref[x * height : (x + 1) * height, :]
        ref[height + 1 : height + 2, :] = after_ref[x : x + 1, :]


def edges(stacked, before, after):
    rows_x, samples = before.shape
    edge = jax.ShapeDtypeStruct((stacked.shape[0] // rows_x + 2, samples), F32)
    return pl.pallas_call(
        edges_kernel,
        in_specs=[VMEM] * 3,
        out_specs=[VMEM] * 2,
        out_shape=[edge, edge],
        compiler_params=pltpu.CompilerParams(vmem_limit_bytes=8 << 20),
        name="edges",
    )(stacked, before, after)


def smooth_kernel(stack_ref, before_ref, after_ref, low_ref, high_ref, dip_ref, out_ref, padded):
    width = before_ref.shape[0]
    bins, samples = stack_ref.shape
    height = bins // width
    pitch = height + 2
    padded[0:pitch, :] = low_ref[...]
    for x in range(width):
        row = (x + 1) * pitch
        padded[row : row + 1, :] = before_ref[x : x + 1, :]
        padded[row + 1 : row + 1 + height, :] = stack_ref[x * height : (x + 1) * height, :]
        padded[row + 1 + height : row + pitch, :] = after_ref[x : x + 1, :]
    padded[(width + 1) * pitch : (width + 2) * pitch, :] = high_ref[...]
    near = []
    for n in range(9):
        dx, dy = n // 3, n % 3
        rows = [(dx + x) * pitch + dy for x in range(width)]
        near.append(jnp.concatenate([padded[r : r + height, :] for r in rows], axis=0))
    time = iota((bins, samples), 1)
    result = jnp.zeros((bins, samples), F32)
    for lag in range(-DIP, DIP + 1):
        part = jnp.zeros((bins, samples), F32)
        for n in range(9):
            factor = CENTER_WEIGHT if n == 4 else SIDE_WEIGHT
            weight = jnp.where(dip_ref[:, n : n + 1] == lag, factor, 0.0)
            part = part + weight * near[n]
        if lag:
            part = pltpu.roll(part, (-lag) % samples, 1)
            part = jnp.where((time + lag >= 0) & (time + lag < samples), part, 0.0)
        result = result + part
    for x in range(width):
        out_ref[x] = result[x * height : (x + 1) * height, :]


def smooth(stacked, before, after, low, high, dip):
    rows_x, samples = before.shape
    bins = stacked.shape[0]
    rows_y = bins // rows_x
    return pl.pallas_call(
        smooth_kernel,
        in_specs=[VMEM] * 6,
        out_specs=VMEM,
        out_shape=jax.ShapeDtypeStruct((rows_x, rows_y, samples), F32),
        scratch_shapes=[pltpu.VMEM(((rows_x + 2) * (rows_y + 2), samples), F32)],
        compiler_params=pltpu.CompilerParams(vmem_limit_bytes=8 << 20),
        name="smooth",
    )(stacked, before, after, low, high, dip)


def exchange(first, last, axis):
    size = lax.axis_size(axis)
    before = lax.ppermute(last, axis, [(i, i + 1) for i in range(size - 1)])
    after = lax.ppermute(first, axis, [(i + 1, i) for i in range(size - 1)])
    return before, after


def body(traces, trace_offset, trace_owner, trace_cell, slowness, band_start, dip_shift):
    owners = lax.axis_size(AXES)
    rows_x, rows_y, samples = slowness.shape
    bins = rows_x * rows_y
    send = dispatch(traces, trace_owner, trace_cell, trace_offset, owners)
    got = lax.all_to_all(send.reshape(owners, ROWS, LANES), AXES, split_axis=0, concat_axis=0, tiled=True)
    picks = bands(band_start)
    stacked, first, last = stack(
        got.reshape(owners * ROWS, LANES), picks, band_start, slowness.reshape(bins, samples), rows_x
    )
    before, after = exchange(first, last, "iline")
    low, high = exchange(*edges(stacked, before, after), "xline")
    return smooth(stacked, before, after, low, high, dip_shift.reshape(9, bins).T)


def solution(mesh):
    return jax.shard_map(
        body,
        mesh=mesh,
        in_specs=(
            P(AXES, None),
            P(AXES),
            P(AXES),
            P(AXES),
            P("xline", "iline", None),
            P(),
            P(None, "xline", "iline"),
        ),
        out_specs=P("xline", "iline", None),
        check_vma=False,
    )
```

time: 96.8 us -> 82 us (0.85)
  the two profiles are of different devices: /device:TPU:14 before, /device:TPU:15 now
where the time goes in v2:
time: 82 us; the launch traced here: 81.6 us
  waiting for transfers between devices  31.3 us (38%)
  starting transfers between devices  21.1 us (26%)
  Pallas kernels  20.1 us (25%)
  local copies, waits for them, and re-layouts  8.24 us (10%)
    all_to_all x1, waiting for transfers between devices, body(): lax.all_to_all(send.reshape(owners, ROWS, LANES), AXES, split_axis=0, con...  22.8 us
    pallas_call x1, Pallas kernels, stack(): pl.pallas_call(stack_kernel, in_specs=[VMEM] * 4, out_specs=[VMEM] * 3, o...  13.2 us
    all_to_all x1, starting transfers between devices, body(): lax.all_to_all(send.reshape(owners, ROWS, LANES), AXES, split_axis=0, con...  10.7 us
    ppermute x2, waiting for transfers between devices, exchange(): after = lax.ppermute(first, axis, [(i + 1, i) for i in range(size - 1)])  8.48 us
    unnamed x16, local copies, waits for them, and re-layouts  8.22 us
    ppermute x2, starting transfers between devices, exchange(): before = lax.ppermute(last, axis, [(i, i + 1) for i in range(size - 1)])  6.63 us
    pallas_call x1, Pallas kernels, dispatch(): pl.pallas_call(functools.partial(dispatch_kernel, owners), in_specs=[pl.B...  3.86 us
    ppermute x2, starting transfers between devices, exchange(): after = lax.ppermute(first, axis, [(i + 1, i) for i in range(size - 1)])  3.84 us
  transfers between devices with their start and end apart: 5, of which 3 were waited for; matrix products, arithmetic and copies ran while one was open for 0% of the time, Pallas kernels for 2%

profile of v2, /device:TPU:15, one launch (start us, length us, event | category | flops | bytes accessed | tf_op | source)
XLA Modules:
  0.0 81.6 jit_solution(13645028075481925678)
XLA Ops:
  0.0 0.7 reshape.36
  0.7 0.0 copy-start.2
  0.7 1.4 %copy-done.2 = bf16[512,1536]{1,0:T(8,128)(2,1)S(1)} copy-done((bf16[512,1536]{1,0:T(8,128)(2,1)S(1)}, bf16[512,1536]{1,0:T(8,128)(2,1)}, u32[]{:S(2)}) %copy-start.2) | copy-done | bytes 1572888
  2.1 0.0 copy-start.4
  2.1 0.7 copy-done.4
  2.8 0.0 copy-start.5
  2.8 0.7 copy-done.5
  3.5 3.9 %dispatch.1 = bf16[8192,128]{1,0:T(8,128)(2,1)} custom-call(bf16[512,1536]{1,0:T(8,128)(2,1)S(1)} %copy-done.2, s32[1,512]{1,0:T(1,128)S(1)} %bitcast.11, s32[1,512]{1,0:T(1,128)S(1)} %bitcast.12, f32[1,512]{1,0:T(1,128)S(1)} %bitcast.9), custom_call_target="tpu_custom_call" | custom-call | tf_op jit(solution)/shard_map/dispatch/pallas_call | solution.py:83
  7.3 0.0 copy-start.7
  7.3 0.0 copy-start.6
  7.3 10.7 %all-to-all-start = ((bf16[128,64,128]{2,1,0:T(8,128)(2,1)}), bf16[128,64,128]{2,1,0:T(8,128)(2,1)S(1)}, u32[]{:S(2)}, u32[]{:S(2)}) async-start(bf16[128,64,128]{2,1,0:T(8,128)(2,1)} %bitcast.3), calls=%async_computation | async-start | bytes 4194304 | tf_op jit(solution)/shard_map/all_to_all | solution.py:335
  18.0 0.0 copy-done.7
  18.0 0.0 copy-done.6
  18.1 1.9 %bands.1.bands_ref = bf16[12,256,1024]{2,1,0:T(8,128)(2,1)S(1)} custom-call(s32[1,1536]{1,0:T(1,128)S(1)} %reshape.33.start_ref), custom_call_target="tpu_custom_call" | custom-call | tf_op jit(solution)/shard_map/bands/pallas_call | solution.py:109
  19.9 0.0 copy-start
  20.0 2.6 %copy-done = bf16[12,256,1024]{2,1,0:T(8,128)(2,1)} copy-done((bf16[12,256,1024]{2,1,0:T(8,128)(2,1)}, bf16[12,256,1024]{2,1,0:T(8,128)(2,1)S(1)}, u32[]{:S(2)}) %copy-start) | copy-done | bytes 6291480
  22.6 22.8 %all-to-all-done = bf16[128,64,128]{2,1,0:T(8,128)(2,1)S(1)} async-done(((bf16[128,64,128]{2,1,0:T(8,128)(2,1)}), bf16[128,64,128]{2,1,0:T(8,128)(2,1)S(1)}, u32[]{:S(2)}, u32[]{:S(2)}) %all-to-all-start) | async-done | bytes 2097184 | tf_op jit(solution)/shard_map/all_to_all | solution.py:335
  45.4 0.0 copy-start.1
  45.4 2.8 %copy-done.1 = bf16[12,256,1024]{2,1,0:T(8,128)(2,1)S(1)} copy-done((bf16[12,256,1024]{2,1,0:T(8,128)(2,1)S(1)}, bf16[12,256,1024]{2,1,0:T(8,128)(2,1)}, u32[]{:S(2)}) %copy-start.1) | copy-done | bytes 6291480
  48.2 0.0 copy-start.3
  48.2 13.2 %stack.1 = (f32[8,1536]{1,0:T(8,128)S(1)}, f32[2,1536]{1,0:T(2,128)S(1)}, f32[2,1536]{1,0:T(2,128)S(1)}) custom-call(bf16[8192,128]{1,0:T(8,128)(2,1)S(1)} %bitcast.8, bf16[12,256,1024]{2,1,0:T(8,128)(2,1)S(1)} %copy-done.1, s32[1,1536]{1,0:T(1,128)S(1)} %reshape.33.start_ref, f32[8,1536]{1,0:T(8,128)S(1)} %reshape.34.slow_ref), custom_call_target="tpu_custom_call" | custom-call | tf_op jit(solution)/shard_map/stack/pallas_call | solution.py:230
  61.4 3.2 %collective-permute-start = (f32[2,1536]{1,0:T(2,128)S(1)}, f32[2,1536]{1,0:T(2,128)S(1)}, u32[]{:S(2)}, u32[]{:S(2)}) collective-permute-start(f32[2,1536]{1,0:T(2,128)S(1)} %get-tuple-element.11), channel_id=1, source_target_pairs={{0,1},{1,2},{2,3},{3,4},{4,5},{5,6},{6,7},{8,9},{9,10},{10,11},{11... | collective-permute-start | bytes 36872 | tf_op jit(solution)/shard_map/ppermute | solution.py:325
  64.6 1.9 %collective-permute-start.1 = (f32[2,1536]{1,0:T(2,128)S(1)}, f32[2,1536]{1,0:T(2,128)S(1)}, u32[]{:S(2)}, u32[]{:S(2)}) collective-permute-start(f32[2,1536]{1,0:T(2,128)S(1)} %get-tuple-element.12), channel_id=1, source_target_pairs={{1,0},{2,1},{3,2},{4,3},{5,4},{6,5},{7,6},{9,8},{10,9},{11,10},{12... | collective-permute-start | bytes 36872 | tf_op jit(solution)/shard_map/ppermute | solution.py:326
  66.5 0.0 collective-permute-done.before_ref
  66.5 3.1 %collective-permute-done.1.after_ref = f32[2,1536]{1,0:T(2,128)S(1)} collective-permute-done((f32[2,1536]{1,0:T(2,128)S(1)}, f32[2,1536]{1,0:T(2,128)S(1)}, u32[]{:S(2)}, u32[]{:S(2)}) %collective-permute-start.1) | collective-permute-done | bytes 12320 | tf_op jit(solution)/shard_map/ppermute | solution.py:326
  69.6 3.5 %collective-permute-start.2 = (f32[6,1536]{1,0:T(8,128)S(1)}, f32[6,1536]{1,0:T(8,128)S(1)}, u32[]{:S(2)}, u32[]{:S(2)}) collective-permute-start(f32[6,1536]{1,0:T(8,128)S(1)} %get-tuple-element.13), channel_id=1, source_target_pairs={{0,8},{8,16},{16,24},{24,32},{32,40},{40,48},{48,56},{56,64},{64,7... | collective-permute-start | bytes 110600 | tf_op jit(solution)/shard_map/ppermute | solution.py:325
  73.1 1.9 %collective-permute-start.3 = (f32[6,1536]{1,0:T(8,128)S(1)}, f32[6,1536]{1,0:T(8,128)S(1)}, u32[]{:S(2)}, u32[]{:S(2)}) collective-permute-start(f32[6,1536]{1,0:T(8,128)S(1)} %get-tuple-element.14), channel_id=1, source_target_pairs={{8,0},{16,8},{24,16},{32,24},{40,32},{48,40},{56,48},{64,56},{72,6... | collective-permute-start | bytes 110600 | tf_op jit(solution)/shard_map/ppermute | solution.py:326
  75.0 0.0 collective-permute-done.2.low_ref
  75.0 5.4 %collective-permute-done.3.high_ref = f32[6,1536]{1,0:T(8,128)S(1)} collective-permute-done((f32[6,1536]{1,0:T(8,128)S(1)}, f32[6,1536]{1,0:T(8,128)S(1)}, u32[]{:S(2)}, u32[]{:S(2)}) %collective-permute-start.3) | collective-permute-done | bytes 36896 | tf_op jit(solution)/shard_map/ppermute | solution.py:326
  80.4 0.0 copy-done.3
  80.4 1.2 %smooth.1 = f32[2,4,1536]{2,1,0:T(4,128)} custom-call(f32[8,1536]{1,0:T(8,128)S(1)} %get-tuple-element.10.stack_ref, f32[2,1536]{1,0:T(2,128)S(1)} %collective-permute-done.before_ref, f32[2,1536]{1,0:T(2,128)S(1)} %collective-permute-done.1.after_ref, f32[6,1536]{1,0:T(8,128)S(1)} %collective-permute-done.2.low_ref, ...), custom_call_target="tpu_custom_call" | custom-call | tf_op jit(solution)/shard_map/smooth/pallas_call | solution.py:312
  (3 shorter events, 0.0 us)
Async XLA Ops:
  0.7 1.4 %copy-start.2 = (bf16[512,1536]{1,0:T(8,128)(2,1)S(1)}, bf16[512,1536]{1,0:T(8,128)(2,1)}, u32[]{:S(2)}) copy-start(bf16[512,1536]{1,0:T(8,128)(2,1)} %traces_hbm.1) | copy-start | bytes 4718596
  2.1 0.7 copy-start.4
  2.8 0.7 copy-start.5
  7.3 10.7 %copy-start.7 = (s32[1536]{0:T(1024)S(1)}, s32[1536]{0:T(1024)}, u32[]{:S(2)}) copy-start(s32[1536]{0:T(1024)} %param.12) | copy-start | bytes 18436
  7.3 10.7 %copy-start.6 = (f32[2,4,1536]{2,1,0:T(4,128)S(1)}, f32[2,4,1536]{2,1,0:T(4,128)}, u32[]{:S(2)}) copy-start(f32[2,4,1536]{2,1,0:T(4,128)} %param.11) | copy-start | bytes 147460
  7.3 38.1 %all-to-all-start = ((bf16[128,64,128]{2,1,0:T(8,128)(2,1)}), bf16[128,64,128]{2,1,0:T(8,128)(2,1)S(1)}, u32[]{:S(2)}, u32[]{:S(2)}) async-start(bf16[128,64,128]{2,1,0:T(8,128)(2,1)} %bitcast.3), calls=%async_computation | async-start | bytes 4194304 | tf_op jit(solution)/shard_map/all_to_all | solution.py:335
  19.9 2.7 %copy-start = (bf16[12,256,1024]{2,1,0:T(8,128)(2,1)}, bf16[12,256,1024]{2,1,0:T(8,128)(2,1)S(1)}, u32[]{:S(2)}) copy-start(bf16[12,256,1024]{2,1,0:T(8,128)(2,1)S(1)} %bands.1.bands_ref) | copy-start | bytes 18874372
  45.4 2.8 %copy-start.1 = (bf16[12,256,1024]{2,1,0:T(8,128)(2,1)S(1)}, bf16[12,256,1024]{2,1,0:T(8,128)(2,1)}, u32[]{:S(2)}) copy-start(bf16[12,256,1024]{2,1,0:T(8,128)(2,1)} %copy-done) | copy-start | bytes 18874372
  48.2 32.3 %copy-start.3 = (s32[9,2,4]{0,2,1:T(4,128)S(1)}, s32[9,2,4]{0,2,1:T(4,128)}, u32[]{:S(2)}) copy-start(s32[9,2,4]{0,2,1:T(4,128)} %param.13) | copy-start | bytes 868
  61.4 5.1 %collective-permute-start = (f32[2,1536]{1,0:T(2,128)S(1)}, f32[2,1536]{1,0:T(2,128)S(1)}, u32[]{:S(2)}, u32[]{:S(2)}) collective-permute-start(f32[2,1536]{1,0:T(2,128)S(1)} %get-tuple-element.11), channel_id=1, source_target_pairs={{0,1},{1,2},{2,3},{3,4},{4,5},{5,6},{6,7},{8,9},{9,10},{10,11},{11... | collective-permute-start | bytes 36872 | tf_op jit(solution)/shard_map/ppermute | solution.py:325
  64.6 5.0 %collective-permute-start.1 = (f32[2,1536]{1,0:T(2,128)S(1)}, f32[2,1536]{1,0:T(2,128)S(1)}, u32[]{:S(2)}, u32[]{:S(2)}) collective-permute-start(f32[2,1536]{1,0:T(2,128)S(1)} %get-tuple-element.12), channel_id=1, source_target_pairs={{1,0},{2,1},{3,2},{4,3},{5,4},{6,5},{7,6},{9,8},{10,9},{11,10},{12... | collective-permute-start | bytes 36872 | tf_op jit(solution)/shard_map/ppermute | solution.py:326
  69.6 5.4 %collective-permute-start.2 = (f32[6,1536]{1,0:T(8,128)S(1)}, f32[6,1536]{1,0:T(8,128)S(1)}, u32[]{:S(2)}, u32[]{:S(2)}) collective-permute-start(f32[6,1536]{1,0:T(8,128)S(1)} %get-tuple-element.13), channel_id=1, source_target_pairs={{0,8},{8,16},{16,24},{24,32},{32,40},{40,48},{48,56},{56,64},{64,7... | collective-permute-start | bytes 110600 | tf_op jit(solution)/shard_map/ppermute | solution.py:325
  73.1 7.3 %collective-permute-start.3 = (f32[6,1536]{1,0:T(8,128)S(1)}, f32[6,1536]{1,0:T(8,128)S(1)}, u32[]{:S(2)}, u32[]{:S(2)}) collective-permute-start(f32[6,1536]{1,0:T(8,128)S(1)} %get-tuple-element.14), channel_id=1, source_target_pairs={{8,0},{16,8},{24,16},{32,24},{40,32},{48,40},{56,48},{64,56},{72,6... | collective-permute-start | bytes 110600 | tf_op jit(solution)/shard_map/ppermute | solution.py:326

commit v3 on v2

v3 whole, which is shorter than its diff:
```python
import functools

import jax
import jax.numpy as jnp
from jax import lax
from jax.experimental import pallas as pl
from jax.experimental.pallas import tpu as pltpu
from jax.sharding import PartitionSpec as P

BAND = 8
DIP = 4
REACH = BAND - 1
LANES = 128
CAP = 5
ROWS = 64
PITCH = 65
STEP = 32
HALVES = (0.5, 1.5, 2.5, 3.5)
VMEM = pl.BlockSpec(memory_space=pltpu.VMEM)
HBM = pl.BlockSpec(memory_space=pltpu.HBM)

CENTER_WEIGHT = 0.5
SIDE_WEIGHT = 0.0625

AXES = ("xline", "iline")
F32 = jnp.float32
BF16 = jnp.bfloat16


def iota(shape, dim):
    return lax.broadcasted_iota(jnp.int32, shape, dim)


def in_line(value):
    return jnp.concatenate([value[i : i + 1, :] for i in range(value.shape[0])], axis=1)


def dispatch_kernel(owners, traces_hbm, owner_hbm, cell_hbm, offset_hbm, out_ref, traces_ref, owner_ref, cell_ref, offset_ref, stage, arrived):
    pairs = ((owner_hbm, owner_ref), (cell_hbm, cell_ref), (offset_hbm, offset_ref), (traces_hbm, traces_ref))
    copies = [pltpu.make_async_copy(there, here, arrived.at[i]) for i, (there, here) in enumerate(pairs)]
    for copy in copies:
        copy.start()
    rows, samples = traces_ref.shape
    blocks = samples // LANES
    for copy in copies[:3]:
        copy.wait()
    owner = in_line(owner_ref[...])
    hot = (iota((owners, rows), 0) == owner).astype(F32)
    earlier = (iota((rows, rows), 0) < iota((rows, rows), 1)).astype(F32).astype(BF16)
    counts = jnp.dot(hot.astype(BF16), earlier, preferred_element_type=F32)
    rank = jnp.sum(hot * counts, axis=0, keepdims=True)
    picks = [jnp.where(rank == float(k), hot, 0.0).astype(BF16) for k in range(CAP)]
    pick = jnp.concatenate(picks, axis=0)
    meta = jnp.zeros((owners, LANES), F32)
    line = iota((LANES, rows), 0)
    offset = in_line(offset_ref[...].astype(F32))
    cell = in_line(cell_ref[...] + 1).astype(F32)
    for k in range(CAP):
        source = jnp.where(line == 8 * k, offset, jnp.where(line == 8 * k + 1, cell, 0.0))
        meta = meta + lax.dot_general(
            picks[k], source.astype(BF16), (((1,), (1,)), ((), ())), preferred_element_type=F32
        )
    stage[pl.ds(CAP * blocks, owners, stride=PITCH), :] = meta
    for row in range(CAP * blocks + 1, ROWS):
        stage[pl.ds(row, owners, stride=PITCH), :] = jnp.zeros((owners, LANES), F32)
    copies[3].wait()
    wrapped = iota((CAP * owners, LANES), 1) < REACH

    def put(block, value):
        for k in range(CAP):
            stage[pl.ds(k * blocks + block, owners, stride=PITCH), :] = value[k * owners : (k + 1) * owners, :]

    first = previous = None
    for tile in range(0, samples, 2 * LANES):
        placed = jnp.dot(pick, traces_ref[:, tile : tile + 2 * LANES], preferred_element_type=F32)
        for half in range(2):
            turned = pltpu.roll(placed[:, half * LANES : (half + 1) * LANES], REACH, 1)
            if first is None:
                first = turned
            else:
                put(tile // LANES + half, jnp.where(wrapped, previous, turned))
            previous = turned
    put(0, jnp.where(wrapped, previous, first))
    for owner_row in range(owners):
        out_ref[owner_row * ROWS : (owner_row + 1) * ROWS, :] = stage[
            owner_row * PITCH : owner_row * PITCH + ROWS, :
        ].astype(BF16)


def dispatch(traces, owner, cell, offset, owners):
    rows, samples = traces.shape
    return pl.pallas_call(
        functools.partial(dispatch_kernel, owners),
        in_specs=[HBM] * 4,
        out_specs=VMEM,
        out_shape=jax.ShapeDtypeStruct((owners * ROWS, LANES), BF16),
        scratch_shapes=[
            pltpu.VMEM((rows, samples), BF16),
            pltpu.VMEM((rows // LANES, LANES), jnp.int32),
            pltpu.VMEM((rows // LANES, LANES), jnp.int32),
            pltpu.VMEM((rows // LANES, LANES), BF16),
            pltpu.VMEM((owners * PITCH, LANES), F32),
            pltpu.SemaphoreType.DMA((4,)),
        ],
        name="dispatch",
    )(traces, *(v.reshape(rows // LANES, LANES) for v in (owner, cell, offset)))


def bands_kernel(start_ref, out_ref):
    first = start_ref[...] + (REACH - pl.program_id(0) * LANES)
    place = iota((2 * LANES, LANES), 0) - first
    for i, half in enumerate(HALVES):
        low = (place == int(3.5 - half)).astype(F32)
        high = (place == int(3.5 + half)).astype(F32)
        out_ref[0, :, i * LANES : (i + 1) * LANES] = (0.5 * (low + high)).astype(BF16)
        out_ref[0, :, (4 + i) * LANES : (5 + i) * LANES] = (half * (low - high)).astype(BF16)


def bands(band_start):
    samples = band_start.shape[0]
    blocks = samples // LANES
    return pl.pallas_call(
        bands_kernel,
        grid=(blocks,),
        in_specs=[pl.BlockSpec((1, LANES), lambda b: (0, b))],
        out_specs=pl.BlockSpec((1, 2 * LANES, BAND * LANES), lambda b: (b, 0, 0)),
        out_shape=jax.ShapeDtypeStruct((blocks, 2 * LANES, BAND * LANES), BF16),
        name="bands",
    )(band_start.reshape(1, samples))


def split3(value):
    high = value.astype(BF16)
    rest = value - high.astype(F32)
    middle = rest.astype(BF16)
    low = (rest - middle.astype(F32)).astype(BF16)
    return high, middle, low


def correct(lag, band):
    square = lag * lag
    num = odd = den = None
    for i, half in enumerate(HALVES):
        near = square + (1.0 + half * half)
        if half == 0.5:
            prod = near * near - square
        else:
            prod = (square + (2.0 - 2.0 * half * half)) * square + (1.0 + half * half) ** 2
        both = 1.0 / prod
        share = near * both
        part, tilt = band(i) * share, band(4 + i) * both
        num, odd, den = (part, tilt, share) if num is None else (num + part, odd + tilt, den + share)
    return (num + lag * odd) / den


def stack_kernel(got_ref, bands_hbm, start_ref, slow_ref, out_ref, first_ref, last_ref, stage, bands_ref, window, scaled, member, fold, pairs0, pairs1, added0, added1, moved0, moved1, arrived):
    blocks = bands_hbm.shape[0]

    def fetch(block):
        return pltpu.make_async_copy(bands_hbm.at[block], bands_ref.at[block], arrived.at[block])

    for block in range(blocks):
        fetch(block).start()
    bins = slow_ref.shape[0]
    sources = got_ref.shape[0] // ROWS
    items = CAP * sources
    for src in range(sources):
        stage[src * PITCH : src * PITCH + ROWS, :] = got_ref[src * ROWS : (src + 1) * ROWS, :].astype(F32)
    meta = stage[pl.ds(CAP * blocks, sources, stride=PITCH), :]
    across = meta.T
    lane = iota((sources, LANES), 1)
    total = jnp.zeros((bins, 1), F32)
    for k in range(CAP):
        here = slice(k * sources, (k + 1) * sources)
        for b in range(blocks):
            rows = stage[pl.ds(k * blocks + b, sources, stride=PITCH), :].astype(BF16)
            window[b, here, :] = rows
            if b == 0:
                window[blocks, here, :] = rows
        offset = meta[:, 8 * k : 8 * k + 1]
        cell = meta[:, 8 * k + 1 : 8 * k + 2] - 1.0
        square = offset * offset
        high = square.astype(BF16).astype(F32)
        part = jnp.where(lane < 3 * bins, high, square - high)
        keep = ((lane % bins).astype(F32) == cell) & (lane < 6 * bins)
        scaled[here, :] = jnp.where(keep, part, 0.0).astype(BF16)
        ones = (across[8 * k + 1 : 8 * k + 2, :] == (iota((bins, sources), 0) + 1).astype(F32)).astype(F32)
        total = total + jnp.sum(ones, axis=1, keepdims=True)
        member[:, here] = ones.astype(BF16)
    fold[...] = jnp.broadcast_to(jnp.maximum(total, 1.0), fold.shape)

    def lanes(block):
        return slice(block * LANES, (block + 1) * LANES)

    def multiply(block, pairs, added):
        wide = jnp.concatenate([window[block], window[block + 1]], axis=1)

        def shift():
            parts = list(split3(slow_ref[:, lanes(block)]))
            parts = [p.astype(F32) for p in parts + parts] + [jnp.zeros((LANES - 6 * bins, LANES), F32)]
            table = jnp.concatenate(parts, axis=0).astype(BF16)
            added[...] = jnp.dot(scaled[...], table, preferred_element_type=F32)

        def pick(half):
            cols = slice(half * LANES, (half + 2) * LANES)
            pairs[:, cols] = jnp.dot(wide, bands_ref[block, :, cols], preferred_element_type=F32)

        return [shift] + [functools.partial(pick, half) for half in range(0, BAND, 2)]

    def weigh(block, pairs, added, moved):
        ticks = iota((1, LANES), 1) + block * LANES
        time = ticks.astype(F32)
        squared = jnp.where(ticks == 0, 1e-30, time * time)
        start = start_ref[:, lanes(block)].astype(F32) + 3.5

        def chunk(row):
            here = slice(row, row + STEP)
            total = squared + added[here, :]
            lag = start - total * lax.rsqrt(total)
            value = correct(lag, lambda i: pairs[here, i * LANES : (i + 1) * LANES])
            high = value.astype(BF16)
            moved[here, :] = high
            moved[items + row : items + row + STEP, :] = (value - high.astype(F32)).astype(BF16)

        return [functools.partial(chunk, row) for row in range(0, items, STEP)]

    def total_up(block, moved):
        sums = jnp.dot(member[...], moved[:items, :], preferred_element_type=F32) + jnp.dot(
            member[...], moved[items:, :], preferred_element_type=F32
        )
        out_ref[:, lanes(block)] = sums / fold[...]

    def interleave(few, many):
        for i, work in enumerate(many):
            for j, other in enumerate(few):
                if j * len(many) // len(few) == i:
                    other()
            work()

    for block in range(blocks):
        fetch(block).wait()
    for work in multiply(0, pairs0, added0):
        work()

    pairs, added, moved = (pairs0, pairs1), (added0, added1), (moved0, moved1)
    for block in range(blocks):
        now, later = block % 2, (block + 1) % 2
        ahead = []
        if block + 1 < blocks:
            ahead = multiply(block + 1, pairs[later], added[later])
        if block:
            total_up(block - 1, moved[later])
        interleave(ahead, weigh(block, pairs[now], added[now], moved[now]))
    total_up(blocks - 1, moved[(blocks - 1) % 2])
    first_ref[...] = out_ref[: first_ref.shape[0], :]
    last_ref[...] = out_ref[bins - last_ref.shape[0] :, :]


def stack(got, picks, band_start, slowness, rows_y):
    bins, samples = slowness.shape
    blocks = samples // LANES
    sources = got.shape[0] // ROWS
    items = CAP * sources
    edge = jax.ShapeDtypeStruct((rows_y, samples), F32)
    return pl.pallas_call(
        stack_kernel,
        in_specs=[VMEM, HBM, VMEM, VMEM],
        out_specs=[VMEM] * 3,
        out_shape=[jax.ShapeDtypeStruct((bins, samples), F32), edge, edge],
        scratch_shapes=[
            pltpu.VMEM((sources * PITCH, LANES), F32),
            pltpu.VMEM((blocks, 2 * LANES, BAND * LANES), BF16),
            pltpu.VMEM((blocks + 1, items, LANES), BF16),
            pltpu.VMEM((items, LANES), BF16),
            pltpu.VMEM((bins, items), BF16),
            pltpu.VMEM((bins, LANES), F32),
            pltpu.VMEM((items, BAND * LANES), F32),
            pltpu.VMEM((items, BAND * LANES), F32),
            pltpu.VMEM((items, LANES), F32),
            pltpu.VMEM((items, LANES), F32),
            pltpu.VMEM((2 * items, LANES), BF16),
            pltpu.VMEM((2 * items, LANES), BF16),
            pltpu.SemaphoreType.DMA((blocks,)),
        ],
        compiler_params=pltpu.CompilerParams(vmem_limit_bytes=40 << 20),
        name="stack",
    )(got, picks, band_start.reshape(1, samples), slowness)


def edges_kernel(stack_ref, low_ref, high_ref, first_ref, last_ref):
    height = low_ref.shape[0]
    width = stack_ref.shape[0] // height
    for y, ref in ((0, first_ref), (height - 1, last_ref)):
        ref[0:1, :] = low_ref[y : y + 1, :]
        for x in range(width):
            ref[x + 1 : x + 2, :] = stack_ref[x * height + y : x * height + y + 1, :]
        ref[width + 1 : width + 2, :] = high_ref[y : y + 1, :]


def edges(stacked, low, high):
    rows_y, samples = low.shape
    edge = jax.ShapeDtypeStruct((stacked.shape[0] // rows_y + 2, samples), F32)
    return pl.pallas_call(
        edges_kernel,
        in_specs=[VMEM] * 3,
        out_specs=[VMEM] * 2,
        out_shape=[edge, edge],
        compiler_params=pltpu.CompilerParams(vmem_limit_bytes=8 << 20),
        name="edges",
    )(stacked, low, high)


def smooth_kernel(stack_ref, low_ref, high_ref, before_ref, after_ref, dip_ref, out_ref, padded):
    height = low_ref.shape[0]
    bins, samples = stack_ref.shape
    width = bins // height
    pitch = height + 2
    for x in range(width + 2):
        row = x * pitch
        padded[row : row + 1, :] = before_ref[x : x + 1, :]
        if x == 0:
            inner = low_ref[...]
        elif x == width + 1:
            inner = high_ref[...]
        else:
            inner = stack_ref[(x - 1) * height : x * height, :]
        padded[row + 1 : row + 1 + height, :] = inner
        padded[row + 1 + height : row + pitch, :] = after_ref[x : x + 1, :]
    across, down = iota(dip_ref.shape, 1), iota(dip_ref.shape, 0)
    bin_x = lax.axis_index("xline") * width + down // height + across // 3 - 1
    bin_y = lax.axis_index("iline") * height + down % height + across % 3 - 1
    limit_x, limit_y = lax.axis_size("xline") * width, lax.axis_size("iline") * height
    inside = (bin_x >= 0) & (bin_x < limit_x) & (bin_y >= 0) & (bin_y < limit_y)
    dip = jnp.where(inside, dip_ref[...], 2 * DIP + 1)
    near = []
    for n in range(9):
        dx, dy = n // 3, n % 3
        rows = [(dx + x) * pitch + dy for x in range(width)]
        near.append(jnp.concatenate([padded[r : r + height, :] for r in rows], axis=0))
    time = iota((bins, samples), 1)
    result = jnp.zeros((bins, samples), F32)
    for lag in range(-DIP, DIP + 1):
        part = jnp.zeros((bins, samples), F32)
        for n in range(9):
            factor = CENTER_WEIGHT if n == 4 else SIDE_WEIGHT
            weight = jnp.where(dip[:, n : n + 1] == lag, factor, 0.0)
            part = part + weight * near[n]
        if lag:
            part = pltpu.roll(part, (-lag) % samples, 1)
            part = jnp.where((time + lag >= 0) & (time + lag < samples), part, 0.0)
        result = result + part
    for x in range(width):
        out_ref[x] = result[x * height : (x + 1) * height, :]


def smooth(stacked, low, high, before, after, dip):
    rows_y, samples = low.shape
    bins = stacked.shape[0]
    rows_x = bins // rows_y
    return pl.pallas_call(
        smooth_kernel,
        in_specs=[VMEM] * 6,
        out_specs=VMEM,
        out_shape=jax.ShapeDtypeStruct((rows_x, rows_y, samples), F32),
        scratch_shapes=[pltpu.VMEM(((rows_x + 2) * (rows_y + 2), samples), F32)],
        compiler_params=pltpu.CompilerParams(vmem_limit_bytes=8 << 20),
        name="smooth",
    )(stacked, low, high, before, after, dip)


def exchange(first, last, axis):
    size = lax.axis_size(axis)
    before = lax.ppermute(last, axis, [(i, (i + 1) % size) for i in range(size)])
    after = lax.ppermute(first, axis, [((i + 1) % size, i) for i in range(size)])
    return before, after


def body(traces, trace_offset, trace_owner, trace_cell, slowness, band_start, dip_shift):
    owners = lax.axis_size(AXES)
    rows_x, rows_y, samples = slowness.shape
    bins = rows_x * rows_y
    send = dispatch(traces, trace_owner, trace_cell, trace_offset, owners)
    got = lax.all_to_all(send.reshape(owners, ROWS, LANES), AXES, split_axis=0, concat_axis=0, tiled=True)
    picks = pltpu.with_memory_space_constraint(bands(band_start), pltpu.HBM)
    stacked, first, last = stack(
        got.reshape(owners * ROWS, LANES), picks, band_start, slowness.reshape(bins, samples), rows_y
    )
    low, high = exchange(first, last, "xline")
    before, after = exchange(*edges(stacked, low, high), "iline")
    return smooth(stacked, low, high, before, after, dip_shift.reshape(9, bins).T)


def solution(mesh):
    return jax.shard_map(
        body,
        mesh=mesh,
        in_specs=(
            P(AXES, None),
            P(AXES),
            P(AXES),
            P(AXES),
            P("xline", "iline", None),
            P(),
            P(None, "xline", "iline"),
        ),
        out_specs=P("xline", "iline", None),
        check_vma=False,
    )
```

time: 82 us -> 70.9 us (0.86)
  the two profiles are of different devices: /device:TPU:15 before, /device:TPU:25 now
where the time goes in v3:
time: 70.9 us; the launch traced here: 70.6 us
  waiting for transfers between devices  24.8 us (35%)
  Pallas kernels  24.6 us (35%)
  starting transfers between devices  20.4 us (29%)
    all_to_all x1, waiting for transfers between devices, body(): lax.all_to_all(send.reshape(owners, ROWS, LANES), AXES, split_axis=0, con...  19.1 us
    pallas_call x1, Pallas kernels, stack(): pl.pallas_call(stack_kernel, in_specs=[VMEM, HBM, VMEM, VMEM], out_specs=...  11.2 us
    all_to_all x1, starting transfers between devices, body(): lax.all_to_all(send.reshape(owners, ROWS, LANES), AXES, split_axis=0, con...  10.6 us
    pallas_call x1, Pallas kernels, bands(): pl.pallas_call(bands_kernel, grid=(blocks,), in_specs=[pl.BlockSpec((1, L...  7.72 us
    ppermute x2, starting transfers between devices, exchange(): lax.ppermute(last, axis, [(i, (i + 1) % size) for i in range(size)])  5.7 us
    pallas_call x1, Pallas kernels, dispatch(): pl.pallas_call(functools.partial(dispatch_kernel, owners), in_specs=[HBM]...  4.53 us
    ppermute x2, starting transfers between devices, exchange(): lax.ppermute(first, axis, [((i + 1) % size, i) for i in range(size)])  4.18 us
    ppermute x2, waiting for transfers between devices, exchange(): lax.ppermute(first, axis, [((i + 1) % size, i) for i in range(size)])  3.52 us
  transfers between devices with their start and end apart: 5, of which 4 were waited for; matrix products, arithmetic and copies ran while one was open for 1% of the time, Pallas kernels for 11%

profile of v3, /device:TPU:25, one launch (start us, length us, event | category | flops | bytes accessed | tf_op | source)
XLA Modules:
  0.0 70.6 jit_solution(2518644175862679477)
XLA Ops:
  0.0 4.5 %dispatch.1 = bf16[8192,128]{1,0:T(8,128)(2,1)} custom-call(bf16[512,1536]{1,0:T(8,128)(2,1)} %traces_hbm.1, s32[4,128]{1,0:T(4,128)} %bitcast.11, s32[4,128]{1,0:T(4,128)} %bitcast.12, bf16[4,128]{1,0:T(4,128)(2,1)} %bitcast.13), custom_call_target="tpu_custom_call" | custom-call | tf_op jit(solution)/shard_map/dispatch/pallas_call | solution.py:92
  4.5 0.0 copy-start.3
  4.6 0.0 copy-start.2
  4.6 10.6 %all-to-all-start = ((bf16[128,64,128]{2,1,0:T(8,128)(2,1)}), bf16[128,64,128]{2,1,0:T(8,128)(2,1)S(1)}, u32[]{:S(2)}, u32[]{:S(2)}) async-start(bf16[128,64,128]{2,1,0:T(8,128)(2,1)} %bitcast.10), calls=%async_computation | async-start | bytes 4194304 | tf_op jit(solution)/shard_map/all_to_all | solution.py:383
  15.1 0.0 copy-done.3
  15.2 0.6 reshape.30.start_ref
  15.8 0.0 copy-done.2
  15.8 0.0 copy-start
  15.8 7.7 %bands.1.bands_hbm = bf16[12,256,1024]{2,1,0:T(8,128)(2,1)} custom-call(s32[1,1536]{1,0:T(1,128)} %reshape.30.start_ref), custom_call_target="tpu_custom_call" | custom-call | tf_op jit(solution)/shard_map/bands/pallas_call | solution.py:122
  23.5 19.1 %all-to-all-done = bf16[128,64,128]{2,1,0:T(8,128)(2,1)S(1)} async-done(((bf16[128,64,128]{2,1,0:T(8,128)(2,1)}), bf16[128,64,128]{2,1,0:T(8,128)(2,1)S(1)}, u32[]{:S(2)}, u32[]{:S(2)}) %all-to-all-start) | async-done | bytes 2097184 | tf_op jit(solution)/shard_map/all_to_all | solution.py:383
  42.6 0.0 copy-done
  42.6 0.0 copy-start.1
  42.6 11.2 %stack.1 = (f32[8,1536]{1,0:T(8,128)S(1)}, f32[4,1536]{1,0:T(4,128)S(1)}, f32[4,1536]{1,0:T(4,128)S(1)}) custom-call(bf16[8192,128]{1,0:T(8,128)(2,1)S(1)} %bitcast.8, bf16[12,256,1024]{2,1,0:T(8,128)(2,1)} %bands.1.bands_hbm, s32[1,1536]{1,0:T(1,128)S(1)} %copy-done, f32[8,1536]{1,0:T(8,128)S(1)} %reshape.31.slow_ref), custom_call_target="tpu_custom_call" | custom-call | tf_op jit(solution)/shard_map/stack/pallas_call | solution.py:265
  53.9 0.7 collective-permute-start
  54.6 4.2 %collective-permute-start.1 = (f32[4,1536]{1,0:T(4,128)S(1)}, f32[4,1536]{1,0:T(4,128)S(1)}, u32[]{:S(2)}, u32[]{:S(2)}) collective-permute-start(f32[4,1536]{1,0:T(4,128)S(1)} %get-tuple-element.12), channel_id=1, source_target_pairs={{8,0},{16,8},{24,16},{32,24},{40,32},{48,40},{56,48},{64,56},{72,6... | collective-permute-start | bytes 73736 | tf_op jit(solution)/shard_map/ppermute | solution.py:374
  58.7 1.2 %collective-permute-done.low_ref = f32[4,1536]{1,0:T(4,128)S(1)} collective-permute-done((f32[4,1536]{1,0:T(4,128)S(1)}, f32[4,1536]{1,0:T(4,128)S(1)}, u32[]{:S(2)}, u32[]{:S(2)}) %collective-permute-start) | collective-permute-done | bytes 24608 | tf_op jit(solution)/shard_map/ppermute | solution.py:373
  59.9 0.0 collective-permute-done.1.high_ref
  60.0 5.0 %collective-permute-start.2 = (f32[4,1536]{1,0:T(4,128)S(1)}, f32[4,1536]{1,0:T(4,128)S(1)}, u32[]{:S(2)}, u32[]{:S(2)}) collective-permute-start(f32[4,1536]{1,0:T(4,128)S(1)} %get-tuple-element.13), channel_id=1, source_target_pairs={{0,1},{1,2},{2,3},{3,4},{4,5},{5,6},{6,7},{7,0},{8,9},{9,10},{10,1... | collective-permute-start | bytes 73736 | tf_op jit(solution)/shard_map/ppermute | solution.py:373
  65.0 0.0 collective-permute-start.3
  65.0 0.9 %collective-permute-done.2.before_ref = f32[4,1536]{1,0:T(4,128)S(1)} collective-permute-done((f32[4,1536]{1,0:T(4,128)S(1)}, f32[4,1536]{1,0:T(4,128)S(1)}, u32[]{:S(2)}, u32[]{:S(2)}) %collective-permute-start.2) | collective-permute-done | bytes 24608 | tf_op jit(solution)/shard_map/ppermute | solution.py:373
  65.9 3.5 %collective-permute-done.3.after_ref = f32[4,1536]{1,0:T(4,128)S(1)} collective-permute-done((f32[4,1536]{1,0:T(4,128)S(1)}, f32[4,1536]{1,0:T(4,128)S(1)}, u32[]{:S(2)}, u32[]{:S(2)}) %collective-permute-start.3) | collective-permute-done | bytes 24608 | tf_op jit(solution)/shard_map/ppermute | solution.py:374
  69.4 0.0 copy-done.1
  69.4 1.1 %smooth.1 = f32[2,4,1536]{2,1,0:T(4,128)} custom-call(f32[8,1536]{1,0:T(8,128)S(1)} %get-tuple-element.10.stack_ref, f32[4,1536]{1,0:T(4,128)S(1)} %collective-permute-done.low_ref, f32[4,1536]{1,0:T(4,128)S(1)} %collective-permute-done.1.high_ref, f32[4,1536]{1,0:T(4,128)S(1)} %collective-permute-done.2.before_ref, ...), custom_call_target="tpu_custom_call" | custom-call | tf_op jit(solution)/shard_map/smooth/pallas_call | solution.py:360
  (2 shorter events, 0.0 us)
Async XLA Ops:
  4.5 10.6 %copy-start.3 = (s32[1536]{0:T(1024)S(1)}, s32[1536]{0:T(1024)}, u32[]{:S(2)}) copy-start(s32[1536]{0:T(1024)} %param.12) | copy-start | bytes 18436
  4.6 11.2 %copy-start.2 = (f32[2,4,1536]{2,1,0:T(4,128)S(1)}, f32[2,4,1536]{2,1,0:T(4,128)}, u32[]{:S(2)}) copy-start(f32[2,4,1536]{2,1,0:T(4,128)} %param.11) | copy-start | bytes 147460
  4.6 38.1 %all-to-all-start = ((bf16[128,64,128]{2,1,0:T(8,128)(2,1)}), bf16[128,64,128]{2,1,0:T(8,128)(2,1)S(1)}, u32[]{:S(2)}, u32[]{:S(2)}) async-start(bf16[128,64,128]{2,1,0:T(8,128)(2,1)} %bitcast.10), calls=%async_computation | async-start | bytes 4194304 | tf_op jit(solution)/shard_map/all_to_all | solution.py:383
  15.8 26.8 %copy-start = (s32[1,1536]{1,0:T(1,128)S(1)}, s32[1,1536]{1,0:T(1,128)}, u32[]{:S(2)}) copy-start(s32[1,1536]{1,0:T(1,128)} %reshape.30.start_ref) | copy-start | bytes 18436
  42.6 26.8 %copy-start.1 = (s32[9,2,4]{0,2,1:T(4,128)S(1)}, s32[9,2,4]{0,2,1:T(4,128)}, u32[]{:S(2)}) copy-start(s32[9,2,4]{0,2,1:T(4,128)} %param.13) | copy-start | bytes 868
  53.9 6.1 %collective-permute-start = (f32[4,1536]{1,0:T(4,128)S(1)}, f32[4,1536]{1,0:T(4,128)S(1)}, u32[]{:S(2)}, u32[]{:S(2)}) collective-permute-start(f32[4,1536]{1,0:T(4,128)S(1)} %get-tuple-element.11), channel_id=1, source_target_pairs={{0,8},{8,16},{16,24},{24,32},{32,40},{40,48},{48,56},{56,64},{64,7... | collective-permute-start | bytes 73736 | tf_op jit(solution)/shard_map/ppermute | solution.py:373
  54.6 5.4 %collective-permute-start.1 = (f32[4,1536]{1,0:T(4,128)S(1)}, f32[4,1536]{1,0:T(4,128)S(1)}, u32[]{:S(2)}, u32[]{:S(2)}) collective-permute-start(f32[4,1536]{1,0:T(4,128)S(1)} %get-tuple-element.12), channel_id=1, source_target_pairs={{8,0},{16,8},{24,16},{32,24},{40,32},{48,40},{56,48},{64,56},{72,6... | collective-permute-start | bytes 73736 | tf_op jit(solution)/shard_map/ppermute | solution.py:374
  60.0 6.0 %collective-permute-start.2 = (f32[4,1536]{1,0:T(4,128)S(1)}, f32[4,1536]{1,0:T(4,128)S(1)}, u32[]{:S(2)}, u32[]{:S(2)}) collective-permute-start(f32[4,1536]{1,0:T(4,128)S(1)} %get-tuple-element.13), channel_id=1, source_target_pairs={{0,1},{1,2},{2,3},{3,4},{4,5},{5,6},{6,7},{7,0},{8,9},{9,10},{10,1... | collective-permute-start | bytes 73736 | tf_op jit(solution)/shard_map/ppermute | solution.py:373
  65.0 4.5 %collective-permute-start.3 = (f32[4,1536]{1,0:T(4,128)S(1)}, f32[4,1536]{1,0:T(4,128)S(1)}, u32[]{:S(2)}, u32[]{:S(2)}) collective-permute-start(f32[4,1536]{1,0:T(4,128)S(1)} %get-tuple-element.14), channel_id=1, source_target_pairs={{1,0},{2,1},{3,2},{4,3},{5,4},{6,5},{7,6},{0,7},{9,8},{10,9},{11,1... | collective-permute-start | bytes 73736 | tf_op jit(solution)/shard_map/ppermute | solution.py:374

commit v4 on v3

--- a/solution.py
+++ b/solution.py
@@ -12,8 +12,9 @@
 REACH = BAND - 1
 LANES = 128
 CAP = 5
-ROWS = 64
-PITCH = 65
+ROWS = 62
+PARTS = 4
+REACHED = 144
 STEP = 32
 HALVES = (0.5, 1.5, 2.5, 3.5)
 VMEM = pl.BlockSpec(memory_space=pltpu.VMEM)
@@ -35,7 +36,7 @@
     return jnp.concatenate([value[i : i + 1, :] for i in range(value.shape[0])], axis=1)
 
 
-def dispatch_kernel(owners, traces_hbm, owner_hbm, cell_hbm, offset_hbm, out_ref, traces_ref, owner_ref, cell_ref, offset_ref, stage, arrived):
+def dispatch_kernel(owners, traces_hbm, owner_hbm, cell_hbm, offset_hbm, out_ref, traces_ref, owner_ref, cell_ref, offset_ref, stage, packed, arrived, sent):
     pairs = ((owner_hbm, owner_ref), (cell_hbm, cell_ref), (offset_hbm, offset_ref), (traces_hbm, traces_ref))
     copies = [pltpu.make_async_copy(there, here, arrived.at[i]) for i, (there, here) in enumerate(pairs)]
     for copy in copies:
@@ -60,15 +61,15 @@
         meta = meta + lax.dot_general(
             picks[k], source.astype(BF16), (((1,), (1,)), ((), ())), preferred_element_type=F32
         )
-    stage[pl.ds(CAP * blocks, owners, stride=PITCH), :] = meta
+    stage[pl.ds(CAP * blocks, owners, stride=ROWS), :] = meta
     for row in range(CAP * blocks + 1, ROWS):
-        stage[pl.ds(row, owners, stride=PITCH), :] = jnp.zeros((owners, LANES), F32)
+        stage[pl.ds(row, owners, stride=ROWS), :] = jnp.zeros((owners, LANES), F32)
     copies[3].wait()
     wrapped = iota((CAP * owners, LANES), 1) < REACH
 
     def put(block, value):
         for k in range(CAP):
-            stage[pl.ds(k * blocks + block, owners, stride=PITCH), :] = value[k * owners : (k + 1) * owners, :]
+            stage[pl.ds(k * blocks + block, owners, stride=ROWS), :] = value[k * owners : (k + 1) * owners, :]
 
     first = previous = None
     for tile in range(0, samples, 2 * LANES):
@@ -81,10 +82,15 @@
                 put(tile // LANES + half, jnp.where(wrapped, previous, turned))
             previous = turned
     put(0, jnp.where(wrapped, previous, first))
-    for owner_row in range(owners):
-        out_ref[owner_row * ROWS : (owner_row + 1) * ROWS, :] = stage[
-            owner_row * PITCH : owner_row * PITCH + ROWS, :
-        ].astype(BF16)
+    size = owners * ROWS // PARTS
+    sends = []
+    for part in range(PARTS):
+        here = pl.ds(part * size, size)
+        packed[here, :] = stage[here, :].astype(BF16)
+        sends.append(pltpu.make_async_copy(packed.at[here, :], out_ref.at[here, :], sent.at[part]))
+        sends[-1].start()
+    for copy in sends:
+        copy.wait()
 
 
 def dispatch(traces, owner, cell, offset, owners):
@@ -92,15 +98,17 @@
     return pl.pallas_call(
         functools.partial(dispatch_kernel, owners),
         in_specs=[HBM] * 4,
-        out_specs=VMEM,
+        out_specs=HBM,
         out_shape=jax.ShapeDtypeStruct((owners * ROWS, LANES), BF16),
         scratch_shapes=[
             pltpu.VMEM((rows, samples), BF16),
             pltpu.VMEM((rows // LANES, LANES), jnp.int32),
             pltpu.VMEM((rows // LANES, LANES), jnp.int32),
             pltpu.VMEM((rows // LANES, LANES), BF16),
-            pltpu.VMEM((owners * PITCH, LANES), F32),
+            pltpu.VMEM((owners * ROWS, LANES), F32),
+            pltpu.VMEM((owners * ROWS, LANES), BF16),
             pltpu.SemaphoreType.DMA((4,)),
+            pltpu.SemaphoreType.DMA((PARTS,)),
         ],
         name="dispatch",
     )(traces, *(v.reshape(rows // LANES, LANES) for v in (owner, cell, offset)))
@@ -108,7 +116,7 @@
 
 def bands_kernel(start_ref, out_ref):
     first = start_ref[...] + (REACH - pl.program_id(0) * LANES)
-    place = iota((2 * LANES, LANES), 0) - first
+    place = iota((REACHED, LANES), 0) - first
     for i, half in enumerate(HALVES):
         low = (place == int(3.5 - half)).astype(F32)
         high = (place == int(3.5 + half)).astype(F32)
@@ -123,8 +131,8 @@
         bands_kernel,
         grid=(blocks,),
         in_specs=[pl.BlockSpec((1, LANES), lambda b: (0, b))],
-        out_specs=pl.BlockSpec((1, 2 * LANES, BAND * LANES), lambda b: (b, 0, 0)),
-        out_shape=jax.ShapeDtypeStruct((blocks, 2 * LANES, BAND * LANES), BF16),
+        out_specs=pl.BlockSpec((1, REACHED, BAND * LANES), lambda b: (b, 0, 0)),
+        out_shape=jax.ShapeDtypeStruct((blocks, REACHED, BAND * LANES), BF16),
         name="bands",
     )(band_start.reshape(1, samples))
 
@@ -164,19 +172,13 @@
     bins = slow_ref.shape[0]
     sources = got_ref.shape[0] // ROWS
     items = CAP * sources
-    for src in range(sources):
-        stage[src * PITCH : src * PITCH + ROWS, :] = got_ref[src * ROWS : (src + 1) * ROWS, :].astype(F32)
-    meta = stage[pl.ds(CAP * blocks, sources, stride=PITCH), :]
+    stage[...] = got_ref[...].astype(F32)
+    meta = stage[pl.ds(CAP * blocks, sources, stride=ROWS), :]
     across = meta.T
     lane = iota((sources, LANES), 1)
     total = jnp.zeros((bins, 1), F32)
     for k in range(CAP):
         here = slice(k * sources, (k + 1) * sources)
-        for b in range(blocks):
-            rows = stage[pl.ds(k * blocks + b, sources, stride=PITCH), :].astype(BF16)
-            window[b, here, :] = rows
-            if b == 0:
-                window[blocks, here, :] = rows
         offset = meta[:, 8 * k : 8 * k + 1]
         cell = meta[:, 8 * k + 1 : 8 * k + 2] - 1.0
         square = offset * offset
@@ -189,6 +191,11 @@
         member[:, here] = ones.astype(BF16)
     fold[...] = jnp.broadcast_to(jnp.maximum(total, 1.0), fold.shape)
 
+    def gather(block):
+        for k in range(CAP):
+            rows = stage[pl.ds(k * blocks + block % blocks, sources, stride=ROWS), :]
+            window[block, k * sources : (k + 1) * sources, :] = rows.astype(BF16)
+
     def lanes(block):
         return slice(block * LANES, (block + 1) * LANES)
 
@@ -203,7 +210,8 @@
 
         def pick(half):
             cols = slice(half * LANES, (half + 2) * LANES)
-            pairs[:, cols] = jnp.dot(wide, bands_ref[block, :, cols], preferred_element_type=F32)
+            rows = jnp.concatenate([bands_ref[block, :, cols], jnp.zeros((2 * LANES - REACHED, 2 * LANES), BF16)], axis=0)
+            pairs[:, cols] = jnp.dot(wide, rows, preferred_element_type=F32)
 
         return [shift] + [functools.partial(pick, half) for half in range(0, BAND, 2)]
 
@@ -239,6 +247,8 @@
 
     for block in range(blocks):
         fetch(block).wait()
+    gather(0)
+    gather(1)
     for work in multiply(0, pairs0, added0):
         work()
 
@@ -247,6 +257,7 @@
         now, later = block % 2, (block + 1) % 2
         ahead = []
         if block + 1 < blocks:
+            gather(block + 2)
             ahead = multiply(block + 1, pairs[later], added[later])
         if block:
             total_up(block - 1, moved[later])
@@ -268,8 +279,8 @@
         out_specs=[VMEM] * 3,
         out_shape=[jax.ShapeDtypeStruct((bins, samples), F32), edge, edge],
         scratch_shapes=[
-            pltpu.VMEM((sources * PITCH, LANES), F32),
-            pltpu.VMEM((blocks, 2 * LANES, BAND * LANES), BF16),
+            pltpu.VMEM((sources * ROWS, LANES), F32),
+            pltpu.VMEM((blocks, REACHED, BAND * LANES), BF16),
             pltpu.VMEM((blocks + 1, items, LANES), BF16),
             pltpu.VMEM((items, LANES), BF16),
             pltpu.VMEM((bins, items), BF16),
@@ -380,7 +391,8 @@
     rows_x, rows_y, samples = slowness.shape
     bins = rows_x * rows_y
     send = dispatch(traces, trace_owner, trace_cell, trace_offset, owners)
-    got = lax.all_to_all(send.reshape(owners, ROWS, LANES), AXES, split_axis=0, concat_axis=0, tiled=True)
+    send = send.reshape(owners, ROWS // 2, 2, LANES)
+    got = lax.all_to_all(send, AXES, split_axis=0, concat_axis=0, tiled=True)
     picks = pltpu.with_memory_space_constraint(bands(band_start), pltpu.HBM)
     stacked, first, last = stack(
         got.reshape(owners * ROWS, LANES), picks, band_start, slowness.reshape(bins, samples), rows_y

time: 70.9 us -> 69.5 us (0.980)
  Pallas kernels: 24.6 us -> 23 us
    pallas_call x1, Pallas kernels: 7.72 us -> 6.87 us  [bands(): pl.pallas_call(bands_kernel, grid=(blocks,), in_specs=[pl.BlockSpec((1, L...]
  transfers between devices with their start and end apart: 5 -> 5, of which waited for: 4 -> 4; matrix products, arithmetic and copies ran while one was open for 1% -> 1% of each run, Pallas kernels for 11% -> 10%
where the time goes in v4:
time: 69.5 us; the launch traced here: 69.1 us
  waiting for transfers between devices  25 us (36%)
  Pallas kernels  23 us (33%)
  starting transfers between devices  20.4 us (29%)
    all_to_all x1, waiting for transfers between devices, body(): got = lax.all_to_all(send, AXES, split_axis=0, concat_axis=0, tiled=True)  19.3 us
    pallas_call x1, Pallas kernels, stack(): pl.pallas_call(stack_kernel, in_specs=[VMEM, HBM, VMEM, VMEM], out_specs=...  10.7 us
    all_to_all x1, starting transfers between devices, body(): got = lax.all_to_all(send, AXES, split_axis=0, concat_axis=0, tiled=True)  10.6 us
    pallas_call x1, Pallas kernels, bands(): pl.pallas_call(bands_kernel, grid=(blocks,), in_specs=[pl.BlockSpec((1, L...  6.87 us
    ppermute x2, starting transfers between devices, exchange(): lax.ppermute(last, axis, [(i, (i + 1) % size) for i in range(size)])  5.63 us
    pallas_call x1, Pallas kernels, dispatch(): pl.pallas_call(functools.partial(dispatch_kernel, owners), in_specs=[HBM]...  4.4 us
    ppermute x2, starting transfers between devices, exchange(): lax.ppermute(first, axis, [((i + 1) % size, i) for i in range(size)])  4.21 us
    ppermute x2, waiting for transfers between devices, exchange(): lax.ppermute(first, axis, [((i + 1) % size, i) for i in range(size)])  3.52 us
  transfers between devices with their start and end apart: 5, of which 4 were waited for; matrix products, arithmetic and copies ran while one was open for 1% of the time, Pallas kernels for 10%

profile of v4, /device:TPU:25, one launch (start us, length us, event | category | flops | bytes accessed | tf_op | source)
XLA Modules:
  0.0 69.1 jit_solution(15551776097314412318)
XLA Ops:
  0.0 4.4 %dispatch.1 = bf16[7936,128]{1,0:T(8,128)(2,1)} custom-call(bf16[512,1536]{1,0:T(8,128)(2,1)} %traces_hbm.1, s32[4,128]{1,0:T(4,128)} %bitcast.11, s32[4,128]{1,0:T(4,128)} %bitcast.12, bf16[4,128]{1,0:T(4,128)(2,1)} %bitcast.13), custom_call_target="tpu_custom_call" | custom-call | tf_op jit(solution)/shard_map/dispatch/pallas_call | solution.py:98
  4.4 0.0 copy-start.3
  4.4 0.0 copy-start.2
  4.4 10.6 %all-to-all-start = ((bf16[128,31,2,128]{3,2,1,0:T(2,128)(2,1)}), bf16[128,31,2,128]{3,2,1,0:T(2,128)(2,1)S(1)}, u32[]{:S(2)}, u32[]{:S(2)}) async-start(bf16[128,31,2,128]{3,2,1,0:T(2,128)(2,1)} %bitcast.10), calls=%async_computation | async-start | bytes 4063232 | tf_op jit(solution)/shard_map/all_to_all | solution.py:395
  15.0 0.0 copy-done.3
  15.0 0.6 reshape.30.start_ref
  15.6 0.0 copy-done.2
  15.6 0.0 copy-start
  15.6 6.9 %bands.1.bands_hbm = bf16[12,144,1024]{2,1,0:T(8,128)(2,1)} custom-call(s32[1,1536]{1,0:T(1,128)} %reshape.30.start_ref), custom_call_target="tpu_custom_call" | custom-call | tf_op jit(solution)/shard_map/bands/pallas_call | solution.py:130
  22.5 19.3 %all-to-all-done = bf16[128,31,2,128]{3,2,1,0:T(2,128)(2,1)S(1)} async-done(((bf16[128,31,2,128]{3,2,1,0:T(2,128)(2,1)}), bf16[128,31,2,128]{3,2,1,0:T(2,128)(2,1)S(1)}, u32[]{:S(2)}, u32[]{:S(2)}) %all-to-all-start) | async-done | bytes 2031648 | tf_op jit(solution)/shard_map/all_to_all | solution.py:395
  41.8 0.0 copy-done
  41.8 0.0 copy-start.1
  41.8 10.7 %stack.1 = (f32[8,1536]{1,0:T(8,128)S(1)}, f32[4,1536]{1,0:T(4,128)S(1)}, f32[4,1536]{1,0:T(4,128)S(1)}) custom-call(bf16[7936,128]{1,0:T(8,128)(2,1)S(1)} %bitcast.8, bf16[12,144,1024]{2,1,0:T(8,128)(2,1)} %bands.1.bands_hbm, s32[1,1536]{1,0:T(1,128)S(1)} %copy-done, f32[8,1536]{1,0:T(8,128)S(1)} %reshape.31.slow_ref), custom_call_target="tpu_custom_call" | custom-call | tf_op jit(solution)/shard_map/stack/pallas_call | solution.py:276
  52.5 0.6 collective-permute-start
  53.1 4.2 %collective-permute-start.1 = (f32[4,1536]{1,0:T(4,128)S(1)}, f32[4,1536]{1,0:T(4,128)S(1)}, u32[]{:S(2)}, u32[]{:S(2)}) collective-permute-start(f32[4,1536]{1,0:T(4,128)S(1)} %get-tuple-element.12), channel_id=1, source_target_pairs={{8,0},{16,8},{24,16},{32,24},{40,32},{48,40},{56,48},{64,56},{72,6... | collective-permute-start | bytes 73736 | tf_op jit(solution)/shard_map/ppermute | solution.py:385
  57.3 1.2 %collective-permute-done.low_ref = f32[4,1536]{1,0:T(4,128)S(1)} collective-permute-done((f32[4,1536]{1,0:T(4,128)S(1)}, f32[4,1536]{1,0:T(4,128)S(1)}, u32[]{:S(2)}, u32[]{:S(2)}) %collective-permute-start) | collective-permute-done | bytes 24608 | tf_op jit(solution)/shard_map/ppermute | solution.py:384
  58.6 0.0 collective-permute-done.1.high_ref
  58.6 5.0 %collective-permute-start.2 = (f32[4,1536]{1,0:T(4,128)S(1)}, f32[4,1536]{1,0:T(4,128)S(1)}, u32[]{:S(2)}, u32[]{:S(2)}) collective-permute-start(f32[4,1536]{1,0:T(4,128)S(1)} %get-tuple-element.13), channel_id=1, source_target_pairs={{0,1},{1,2},{2,3},{3,4},{4,5},{5,6},{6,7},{7,0},{8,9},{9,10},{10,1... | collective-permute-start | bytes 73736 | tf_op jit(solution)/shard_map/ppermute | solution.py:384
  63.6 0.0 collective-permute-start.3
  63.6 0.9 %collective-permute-done.2.before_ref = f32[4,1536]{1,0:T(4,128)S(1)} collective-permute-done((f32[4,1536]{1,0:T(4,128)S(1)}, f32[4,1536]{1,0:T(4,128)S(1)}, u32[]{:S(2)}, u32[]{:S(2)}) %collective-permute-start.2) | collective-permute-done | bytes 24608 | tf_op jit(solution)/shard_map/ppermute | solution.py:384
  64.5 3.5 %collective-permute-done.3.after_ref = f32[4,1536]{1,0:T(4,128)S(1)} collective-permute-done((f32[4,1536]{1,0:T(4,128)S(1)}, f32[4,1536]{1,0:T(4,128)S(1)}, u32[]{:S(2)}, u32[]{:S(2)}) %collective-permute-start.3) | collective-permute-done | bytes 24608 | tf_op jit(solution)/shard_map/ppermute | solution.py:385
  68.0 0.0 copy-done.1
  68.0 1.1 %smooth.1 = f32[2,4,1536]{2,1,0:T(4,128)} custom-call(f32[8,1536]{1,0:T(8,128)S(1)} %get-tuple-element.10.stack_ref, f32[4,1536]{1,0:T(4,128)S(1)} %collective-permute-done.low_ref, f32[4,1536]{1,0:T(4,128)S(1)} %collective-permute-done.1.high_ref, f32[4,1536]{1,0:T(4,128)S(1)} %collective-permute-done.2.before_ref, ...), custom_call_target="tpu_custom_call" | custom-call | tf_op jit(solution)/shard_map/smooth/pallas_call | solution.py:371
  (2 shorter events, 0.0 us)
Async XLA Ops:
  4.4 10.6 %copy-start.3 = (s32[1536]{0:T(1024)S(1)}, s32[1536]{0:T(1024)}, u32[]{:S(2)}) copy-start(s32[1536]{0:T(1024)} %param.12) | copy-start | bytes 18436
  4.4 11.2 %copy-start.2 = (f32[2,4,1536]{2,1,0:T(4,128)S(1)}, f32[2,4,1536]{2,1,0:T(4,128)}, u32[]{:S(2)}) copy-start(f32[2,4,1536]{2,1,0:T(4,128)} %param.11) | copy-start | bytes 147460
  4.4 37.4 %all-to-all-start = ((bf16[128,31,2,128]{3,2,1,0:T(2,128)(2,1)}), bf16[128,31,2,128]{3,2,1,0:T(2,128)(2,1)S(1)}, u32[]{:S(2)}, u32[]{:S(2)}) async-start(bf16[128,31,2,128]{3,2,1,0:T(2,128)(2,1)} %bitcast.10), calls=%async_computation | async-start | bytes 4063232 | tf_op jit(solution)/shard_map/all_to_all | solution.py:395
  15.6 26.2 %copy-start = (s32[1,1536]{1,0:T(1,128)S(1)}, s32[1,1536]{1,0:T(1,128)}, u32[]{:S(2)}) copy-start(s32[1,1536]{1,0:T(1,128)} %reshape.30.start_ref) | copy-start | bytes 18436
  41.8 26.2 %copy-start.1 = (s32[9,2,4]{0,2,1:T(4,128)S(1)}, s32[9,2,4]{0,2,1:T(4,128)}, u32[]{:S(2)}) copy-start(s32[9,2,4]{0,2,1:T(4,128)} %param.13) | copy-start | bytes 868
  52.5 6.1 %collective-permute-start = (f32[4,1536]{1,0:T(4,128)S(1)}, f32[4,1536]{1,0:T(4,128)S(1)}, u32[]{:S(2)}, u32[]{:S(2)}) collective-permute-start(f32[4,1536]{1,0:T(4,128)S(1)} %get-tuple-element.11), channel_id=1, source_target_pairs={{0,8},{8,16},{16,24},{24,32},{32,40},{40,48},{48,56},{56,64},{64,7... | collective-permute-start | bytes 73736 | tf_op jit(solution)/shard_map/ppermute | solution.py:384
  53.1 5.4 %collective-permute-start.1 = (f32[4,1536]{1,0:T(4,128)S(1)}, f32[4,1536]{1,0:T(4,128)S(1)}, u32[]{:S(2)}, u32[]{:S(2)}) collective-permute-start(f32[4,1536]{1,0:T(4,128)S(1)} %get-tuple-element.12), channel_id=1, source_target_pairs={{8,0},{16,8},{24,16},{32,24},{40,32},{48,40},{56,48},{64,56},{72,6... | collective-permute-start | bytes 73736 | tf_op jit(solution)/shard_map/ppermute | solution.py:385
  58.6 5.9 %collective-permute-start.2 = (f32[4,1536]{1,0:T(4,128)S(1)}, f32[4,1536]{1,0:T(4,128)S(1)}, u32[]{:S(2)}, u32[]{:S(2)}) collective-permute-start(f32[4,1536]{1,0:T(4,128)S(1)} %get-tuple-element.13), channel_id=1, source_target_pairs={{0,1},{1,2},{2,3},{3,4},{4,5},{5,6},{6,7},{7,0},{8,9},{9,10},{10,1... | collective-permute-start | bytes 73736 | tf_op jit(solution)/shard_map/ppermute | solution.py:384
  63.6 4.5 %collective-permute-start.3 = (f32[4,1536]{1,0:T(4,128)S(1)}, f32[4,1536]{1,0:T(4,128)S(1)}, u32[]{:S(2)}, u32[]{:S(2)}) collective-permute-start(f32[4,1536]{1,0:T(4,128)S(1)} %get-tuple-element.14), channel_id=1, source_target_pairs={{1,0},{2,1},{3,2},{4,3},{5,4},{6,5},{7,6},{0,7},{9,8},{10,9},{11,1... | collective-permute-start | bytes 73736 | tf_op jit(solution)/shard_map/ppermute | solution.py:385

commit v5 on v4

--- a/solution.py
+++ b/solution.py
@@ -65,23 +65,22 @@
     for row in range(CAP * blocks + 1, ROWS):
         stage[pl.ds(row, owners, stride=ROWS), :] = jnp.zeros((owners, LANES), F32)
     copies[3].wait()
-    wrapped = iota((CAP * owners, LANES), 1) < REACH
-
-    def put(block, value):
+    wrapped = iota((rows, LANES), 1) < REACH
+
+    def turned(block):
+        return pltpu.roll(traces_ref[:, block * LANES : (block + 1) * LANES], REACH, 1)
+
+    previous = turned(blocks - 1)
+    for tile in range(0, blocks, 2):
+        one, two = turned(tile), turned(tile + 1)
+        moved = jnp.concatenate([jnp.where(wrapped, previous, one), jnp.where(wrapped, one, two)], axis=1)
+        previous = two
+        placed = jnp.dot(pick, moved, preferred_element_type=F32)
         for k in range(CAP):
-            stage[pl.ds(k * blocks + block, owners, stride=ROWS), :] = value[k * owners : (k + 1) * owners, :]
-
-    first = previous = None
-    for tile in range(0, samples, 2 * LANES):
-        placed = jnp.dot(pick, traces_ref[:, tile : tile + 2 * LANES], preferred_element_type=F32)
-        for half in range(2):
-            turned = pltpu.roll(placed[:, half * LANES : (half + 1) * LANES], REACH, 1)
-            if first is None:
-                first = turned
-            else:
-                put(tile // LANES + half, jnp.where(wrapped, previous, turned))
-            previous = turned
-    put(0, jnp.where(wrapped, previous, first))
+            for half in range(2):
+                stage[pl.ds(k * blocks + tile + half, owners, stride=ROWS), :] = placed[
+                    k * owners : (k + 1) * owners, half * LANES : (half + 1) * LANES
+                ]
     size = owners * ROWS // PARTS
     sends = []
     for part in range(PARTS):
@@ -161,7 +160,7 @@
     return (num + lag * odd) / den
 
 
-def stack_kernel(got_ref, bands_hbm, start_ref, slow_ref, out_ref, first_ref, last_ref, stage, bands_ref, window, scaled, member, fold, pairs0, pairs1, added0, added1, moved0, moved1, arrived):
+def stack_kernel(got_ref, bands_hbm, start_ref, slow_ref, out_ref, first_ref, last_ref, stage, bands_ref, window, scaled, member, fold, lags, pairs0, pairs1, moved0, moved1, arrived):
     blocks = bands_hbm.shape[0]
 
     def fetch(block):
@@ -199,32 +198,30 @@
     def lanes(block):
         return slice(block * LANES, (block + 1) * LANES)
 
-    def multiply(block, pairs, added):
+    def shift(block):
+        parts = list(split3(slow_ref[:, lanes(block)]))
+        parts = [p.astype(F32) for p in parts + parts] + [jnp.zeros((LANES - 6 * bins, LANES), F32)]
+        table = jnp.concatenate(parts, axis=0).astype(BF16)
+        added = jnp.dot(scaled[...], table, preferred_element_type=F32)
+        ticks = iota((1, LANES), 1) + block * LANES
+        time = ticks.astype(F32)
+        total = jnp.where(ticks == 0, 1e-30, time * time) + added
+        lags[block] = (start_ref[:, lanes(block)].astype(F32) + 3.5) - total * lax.rsqrt(total)
+
+    def multiply(block, pairs):
         wide = jnp.concatenate([window[block], window[block + 1]], axis=1)
-
-        def shift():
-            parts = list(split3(slow_ref[:, lanes(block)]))
-            parts = [p.astype(F32) for p in parts + parts] + [jnp.zeros((LANES - 6 * bins, LANES), F32)]
-            table = jnp.concatenate(parts, axis=0).astype(BF16)
-            added[...] = jnp.dot(scaled[...], table, preferred_element_type=F32)
 
         def pick(half):
             cols = slice(half * LANES, (half + 2) * LANES)
             rows = jnp.concatenate([bands_ref[block, :, cols], jnp.zeros((2 * LANES - REACHED, 2 * LANES), BF16)], axis=0)
             pairs[:, cols] = jnp.dot(wide, rows, preferred_element_type=F32)
 
-        return [shift] + [functools.partial(pick, half) for half in range(0, BAND, 2)]
-
-    def weigh(block, pairs, added, moved):
-        ticks = iota((1, LANES), 1) + block * LANES
-        time = ticks.astype(F32)
-        squared = jnp.where(ticks == 0, 1e-30, time * time)
-        start = start_ref[:, lanes(block)].astype(F32) + 3.5
-
+        return [functools.partial(pick, half) for half in range(0, BAND, 2)]
+
+    def weigh(block, pairs, moved):
         def chunk(row):
             here = slice(row, row + STEP)
-            total = squared + added[here, :]
-            lag = start - total * lax.rsqrt(total)
+            lag = lags[block, here, :]
             value = correct(lag, lambda i: pairs[here, i * LANES : (i + 1) * LANES])
             high = value.astype(BF16)
             moved[here, :] = high
@@ -245,23 +242,24 @@
                     other()
             work()
 
+    gather(0)
+    gather(1)
+    for block in range(blocks):
+        shift(block)
     for block in range(blocks):
         fetch(block).wait()
-    gather(0)
-    gather(1)
-    for work in multiply(0, pairs0, added0):
+    pairs, moved = (pairs0, pairs1), (moved0, moved1)
+    for work in multiply(0, pairs0):
         work()
-
-    pairs, added, moved = (pairs0, pairs1), (added0, added1), (moved0, moved1)
     for block in range(blocks):
         now, later = block % 2, (block + 1) % 2
         ahead = []
         if block + 1 < blocks:
             gather(block + 2)
-            ahead = multiply(block + 1, pairs[later], added[later])
+            ahead = multiply(block + 1, pairs[later])
         if block:
             total_up(block - 1, moved[later])
-        interleave(ahead, weigh(block, pairs[now], added[now], moved[now]))
+        interleave(ahead, weigh(block, pairs[now], moved[now]))
     total_up(blocks - 1, moved[(blocks - 1) % 2])
     first_ref[...] = out_ref[: first_ref.shape[0], :]
     last_ref[...] = out_ref[bins - last_ref.shape[0] :, :]
@@ -285,10 +283,9 @@
             pltpu.VMEM((items, LANES), BF16),
             pltpu.VMEM((bins, items), BF16),
             pltpu.VMEM((bins, LANES), F32),
+            pltpu.VMEM((blocks, items, LANES), F32),
             pltpu.VMEM((items, BAND * LANES), F32),
             pltpu.VMEM((items, BAND * LANES), F32),
-            pltpu.VMEM((items, LANES), F32),
-            pltpu.VMEM((items, LANES), F32),
             pltpu.VMEM((2 * items, LANES), BF16),
             pltpu.VMEM((2 * items, LANES), BF16),
             pltpu.SemaphoreType.DMA((blocks,)),
@@ -321,14 +318,45 @@
     )(stacked, low, high)
 
 
-def smooth_kernel(stack_ref, low_ref, high_ref, before_ref, after_ref, dip_ref, out_ref, padded):
+def inner_dip(dip, width, height):
+    neighbour, bin_of = iota(dip.shape, 1), iota(dip.shape, 0)
+    bin_x = lax.axis_index("xline") * width + bin_of // height + neighbour // 3 - 1
+    bin_y = lax.axis_index("iline") * height + bin_of % height + neighbour % 3 - 1
+    limit_x, limit_y = lax.axis_size("xline") * width, lax.axis_size("iline") * height
+    inside = (bin_x >= 0) & (bin_x < limit_x) & (bin_y >= 0) & (bin_y < limit_y)
+    return jnp.where(inside, dip, 2 * DIP + 1)
+
+
+def steer(terms):
+    shape = terms[0][0].shape
+    samples = shape[1]
+    time = iota(shape, 1)
+    result = None
+    for lag in range(-DIP, DIP + 1):
+        part = None
+        for rows, dip, factor in terms:
+            value = jnp.where(dip == lag, factor, 0.0) * rows
+            part = value if part is None else part + value
+        if lag:
+            part = pltpu.roll(part, (-lag) % samples, 1)
+            part = jnp.where((time + lag >= 0) & (time + lag < samples), part, 0.0)
+        result = part if result is None else result + part
+    return result
+
+
+def factor_of(n):
+    return CENTER_WEIGHT if n == 4 else SIDE_WEIGHT
+
+
+def smooth_kernel(stack_ref, low_ref, high_ref, dip_ref, out_ref, padded):
     height = low_ref.shape[0]
     bins, samples = stack_ref.shape
     width = bins // height
     pitch = height + 2
+    zero = jnp.zeros((1, samples), F32)
     for x in range(width + 2):
         row = x * pitch
-        padded[row : row + 1, :] = before_ref[x : x + 1, :]
+        padded[row : row + 1, :] = zero
         if x == 0:
             inner = low_ref[...]
         elif x == width + 1:
@@ -336,47 +364,62 @@
         else:
             inner = stack_ref[(x - 1) * height : x * height, :]
         padded[row + 1 : row + 1 + height, :] = inner
-        padded[row + 1 + height : row + pitch, :] = after_ref[x : x + 1, :]
-    across, down = iota(dip_ref.shape, 1), iota(dip_ref.shape, 0)
-    bin_x = lax.axis_index("xline") * width + down // height + across // 3 - 1
-    bin_y = lax.axis_index("iline") * height + down % height + across % 3 - 1
-    limit_x, limit_y = lax.axis_size("xline") * width, lax.axis_size("iline") * height
-    inside = (bin_x >= 0) & (bin_x < limit_x) & (bin_y >= 0) & (bin_y < limit_y)
-    dip = jnp.where(inside, dip_ref[...], 2 * DIP + 1)
-    near = []
+        padded[row + 1 + height : row + pitch, :] = zero
+    dip = inner_dip(dip_ref[...], width, height)
+    terms = []
     for n in range(9):
         dx, dy = n // 3, n % 3
         rows = [(dx + x) * pitch + dy for x in range(width)]
-        near.append(jnp.concatenate([padded[r : r + height, :] for r in rows], axis=0))
-    time = iota((bins, samples), 1)
-    result = jnp.zeros((bins, samples), F32)
-    for lag in range(-DIP, DIP + 1):
-        part = jnp.zeros((bins, samples), F32)
-        for n in range(9):
-            factor = CENTER_WEIGHT if n == 4 else SIDE_WEIGHT
-            weight = jnp.where(dip[:, n : n + 1] == lag, factor, 0.0)
-            part = part + weight * near[n]
-        if lag:
-            part = pltpu.roll(part, (-lag) % samples, 1)
-            part = jnp.where((time + lag >= 0) & (time + lag < samples), part, 0.0)
-        result = result + part
+        near = jnp.concatenate([padded[r : r + height, :] for r in rows], axis=0)
+        terms.append((near, dip[:, n : n + 1], factor_of(n)))
+    out_ref[...] = steer(terms)
+
+
+def border_kernel(part_ref, before_ref, after_ref, dip_ref, out_ref):
+    width = before_ref.shape[0] - 2
+    bins, samples = part_ref.shape
+    height = bins // width
+    dip = inner_dip(dip_ref[...], width, height)
+    terms = []
+    for dx in range(3):
+        near = jnp.concatenate([before_ref[dx : dx + width, :], after_ref[dx : dx + width, :]], axis=0)
+        shifts = [dip[x * height : x * height + 1, 3 * dx : 3 * dx + 1] for x in range(width)]
+        shifts += [dip[(x + 1) * height - 1 : (x + 1) * height, 3 * dx + 2 : 3 * dx + 3] for x in range(width)]
+        terms.append((near, jnp.concatenate(shifts, axis=0), SIDE_WEIGHT))
+    border = steer(terms)
     for x in range(width):
-        out_ref[x] = result[x * height : (x + 1) * height, :]
-
-
-def smooth(stacked, low, high, before, after, dip):
+        out_ref[x] = part_ref[x * height : (x + 1) * height, :]
+        out_ref[x, 0:1, :] = part_ref[x * height : x * height + 1, :] + border[x : x + 1, :]
+        last = (x + 1) * height - 1
+        out_ref[x, height - 1 : height, :] = part_ref[last : last + 1, :] + border[width + x : width + x + 1, :]
+
+
+def smooth(stacked, low, high, dip):
     rows_y, samples = low.shape
     bins = stacked.shape[0]
     rows_x = bins // rows_y
     return pl.pallas_call(
         smooth_kernel,
-        in_specs=[VMEM] * 6,
+        in_specs=[VMEM] * 4,
         out_specs=VMEM,
-        out_shape=jax.ShapeDtypeStruct((rows_x, rows_y, samples), F32),
+        out_shape=jax.ShapeDtypeStruct((bins, samples), F32),
         scratch_shapes=[pltpu.VMEM(((rows_x + 2) * (rows_y + 2), samples), F32)],
         compiler_params=pltpu.CompilerParams(vmem_limit_bytes=8 << 20),
         name="smooth",
-    )(stacked, low, high, before, after, dip)
+    )(stacked, low, high, dip)
+
+
+def border(part, before, after, dip):
+    bins, samples = part.shape
+    rows_x = before.shape[0] - 2
+    return pl.pallas_call(
+        border_kernel,
+        in_specs=[VMEM] * 4,
+        out_specs=VMEM,
+        out_shape=jax.ShapeDtypeStruct((rows_x, bins // rows_x, samples), F32),
+        compiler_params=pltpu.CompilerParams(vmem_limit_bytes=8 << 20),
+        name="border",
+    )(part, before, after, dip)
 
 
 def exchange(first, last, axis):
@@ -399,7 +442,8 @@
     )
     low, high = exchange(first, last, "xline")
     before, after = exchange(*edges(stacked, low, high), "iline")
-    return smooth(stacked, low, high, before, after, dip_shift.reshape(9, bins).T)
+    dip = dip_shift.reshape(9, bins).T
+    return border(smooth(stacked, low, high, dip), before, after, dip)
 
 
 def solution(mesh):

time: 69.5 us -> 69.4 us (level)
    pallas_call x1 -> x2, Pallas kernels: 1.11 us -> 1.44 us  [the longest x1 0.96 us: border(): pl.pallas_call(border_kernel, in_specs=[VMEM] * 4, out_specs=VMEM, out_sh...]
  transfers between devices with their start and end apart: 5 -> 5, of which waited for: 4 -> 4; matrix products, arithmetic and copies ran while one was open for 1% -> 1% of each run, Pallas kernels for 10% -> 11%
where the time goes in v5:
time: 69.4 us; the launch traced here: 69 us
  waiting for transfers between devices  24.5 us (35%)
  Pallas kernels  23.4 us (34%)
  starting transfers between devices  20.4 us (29%)
    all_to_all x1, waiting for transfers between devices, body(): got = lax.all_to_all(send, AXES, split_axis=0, concat_axis=0, tiled=True)  19.3 us
    pallas_call x1, Pallas kernels, stack(): pl.pallas_call(stack_kernel, in_specs=[VMEM, HBM, VMEM, VMEM], out_specs=...  10.8 us
    all_to_all x1, starting transfers between devices, body(): got = lax.all_to_all(send, AXES, split_axis=0, concat_axis=0, tiled=True)  10.6 us
    pallas_call x1, Pallas kernels, bands(): pl.pallas_call(bands_kernel, grid=(blocks,), in_specs=[pl.BlockSpec((1, L...  6.87 us
    ppermute x2, starting transfers between devices, exchange(): lax.ppermute(last, axis, [(i, (i + 1) % size) for i in range(size)])  5.56 us
    pallas_call x1, Pallas kernels, dispatch(): pl.pallas_call(functools.partial(dispatch_kernel, owners), in_specs=[HBM]...  4.34 us
    ppermute x2, starting transfers between devices, exchange(): lax.ppermute(first, axis, [((i + 1) % size, i) for i in range(size)])  4.24 us
    ppermute x2, waiting for transfers between devices, exchange(): lax.ppermute(first, axis, [((i + 1) % size, i) for i in range(size)])  3.52 us
  transfers between devices with their start and end apart: 5, of which 4 were waited for; matrix products, arithmetic and copies ran while one was open for 1% of the time, Pallas kernels for 11%

profile of v5, /device:TPU:25, one launch (start us, length us, event | category | flops | bytes accessed | tf_op | source)
XLA Modules:
  0.0 69.0 jit_solution(5077706415458241500)
XLA Ops:
  0.0 4.3 %dispatch.1 = bf16[7936,128]{1,0:T(8,128)(2,1)} custom-call(bf16[512,1536]{1,0:T(8,128)(2,1)} %traces_hbm.1, s32[4,128]{1,0:T(4,128)} %bitcast.12, s32[4,128]{1,0:T(4,128)} %bitcast.13, bf16[4,128]{1,0:T(4,128)(2,1)} %bitcast.14), custom_call_target="tpu_custom_call" | custom-call | tf_op jit(solution)/shard_map/dispatch/pallas_call | solution.py:97
  4.3 0.0 copy-start.3
  4.4 0.0 copy-start.2
  4.4 10.6 %all-to-all-start = ((bf16[128,31,2,128]{3,2,1,0:T(2,128)(2,1)}), bf16[128,31,2,128]{3,2,1,0:T(2,128)(2,1)S(1)}, u32[]{:S(2)}, u32[]{:S(2)}) async-start(bf16[128,31,2,128]{3,2,1,0:T(2,128)(2,1)} %bitcast.11), calls=%async_computation | async-start | bytes 4063232 | tf_op jit(solution)/shard_map/all_to_all | solution.py:438
  14.9 0.0 copy-done.3
  15.0 0.6 reshape.30.start_ref
  15.6 0.0 copy-done.2
  15.6 0.0 copy-start
  15.6 6.9 %bands.1.bands_hbm = bf16[12,144,1024]{2,1,0:T(8,128)(2,1)} custom-call(s32[1,1536]{1,0:T(1,128)} %reshape.30.start_ref), custom_call_target="tpu_custom_call" | custom-call | tf_op jit(solution)/shard_map/bands/pallas_call | solution.py:129
  22.4 19.3 %all-to-all-done = bf16[128,31,2,128]{3,2,1,0:T(2,128)(2,1)S(1)} async-done(((bf16[128,31,2,128]{3,2,1,0:T(2,128)(2,1)}), bf16[128,31,2,128]{3,2,1,0:T(2,128)(2,1)S(1)}, u32[]{:S(2)}, u32[]{:S(2)}) %all-to-all-start) | async-done | bytes 2031648 | tf_op jit(solution)/shard_map/all_to_all | solution.py:438
  41.8 0.0 copy-done
  41.8 0.0 copy-start.1
  41.8 10.8 %stack.1 = (f32[8,1536]{1,0:T(8,128)S(1)}, f32[4,1536]{1,0:T(4,128)S(1)}, f32[4,1536]{1,0:T(4,128)S(1)}) custom-call(bf16[7936,128]{1,0:T(8,128)(2,1)S(1)} %bitcast.8, bf16[12,144,1024]{2,1,0:T(8,128)(2,1)} %bands.1.bands_hbm, s32[1,1536]{1,0:T(1,128)S(1)} %copy-done, f32[8,1536]{1,0:T(8,128)S(1)} %reshape.31.slow_ref), custom_call_target="tpu_custom_call" | custom-call | tf_op jit(solution)/shard_map/stack/pallas_call | solution.py:274
  52.5 0.6 collective-permute-start
  53.2 4.2 %collective-permute-start.1 = (f32[4,1536]{1,0:T(4,128)S(1)}, f32[4,1536]{1,0:T(4,128)S(1)}, u32[]{:S(2)}, u32[]{:S(2)}) collective-permute-start(f32[4,1536]{1,0:T(4,128)S(1)} %get-tuple-element.12), channel_id=1, source_target_pairs={{8,0},{16,8},{24,16},{32,24},{40,32},{48,40},{56,48},{64,56},{72,6... | collective-permute-start | bytes 73736 | tf_op jit(solution)/shard_map/ppermute | solution.py:428
  57.4 1.2 %collective-permute-done.low_ref = f32[4,1536]{1,0:T(4,128)S(1)} collective-permute-done((f32[4,1536]{1,0:T(4,128)S(1)}, f32[4,1536]{1,0:T(4,128)S(1)}, u32[]{:S(2)}, u32[]{:S(2)}) %collective-permute-start) | collective-permute-done | bytes 24608 | tf_op jit(solution)/shard_map/ppermute | solution.py:427
  58.6 0.0 collective-permute-done.1.high_ref
  58.6 4.9 %collective-permute-start.2 = (f32[4,1536]{1,0:T(4,128)S(1)}, f32[4,1536]{1,0:T(4,128)S(1)}, u32[]{:S(2)}, u32[]{:S(2)}) collective-permute-start(f32[4,1536]{1,0:T(4,128)S(1)} %get-tuple-element.13), channel_id=1, source_target_pairs={{0,1},{1,2},{2,3},{3,4},{4,5},{5,6},{6,7},{7,0},{8,9},{9,10},{10,1... | collective-permute-start | bytes 73736 | tf_op jit(solution)/shard_map/ppermute | solution.py:427
  63.6 0.0 collective-permute-start.3
  63.6 0.0 copy-done.1
  63.6 0.5 smooth.1.part_ref
  64.1 0.5 collective-permute-done.2.before_ref
  64.5 3.5 %collective-permute-done.3.after_ref = f32[4,1536]{1,0:T(4,128)S(1)} collective-permute-done((f32[4,1536]{1,0:T(4,128)S(1)}, f32[4,1536]{1,0:T(4,128)S(1)}, u32[]{:S(2)}, u32[]{:S(2)}) %collective-permute-start.3) | collective-permute-done | bytes 24608 | tf_op jit(solution)/shard_map/ppermute | solution.py:428
  68.0 1.0 %border.1 = f32[2,4,1536]{2,1,0:T(4,128)} custom-call(f32[8,1536]{1,0:T(8,128)S(1)} %smooth.1.part_ref, f32[4,1536]{1,0:T(4,128)S(1)} %collective-permute-done.2.before_ref, f32[4,1536]{1,0:T(4,128)S(1)} %collective-permute-done.3.after_ref, s32[8,9]{1,0:T(8,128)S(1)} %bitcast.10), custom_call_target="tpu_custom_call" | custom-call | tf_op jit(solution)/shard_map/border/pallas_call | solution.py:415
  (2 shorter events, 0.0 us)
Async XLA Ops:
  4.3 10.6 %copy-start.3 = (s32[1536]{0:T(1024)S(1)}, s32[1536]{0:T(1024)}, u32[]{:S(2)}) copy-start(s32[1536]{0:T(1024)} %param.12) | copy-start | bytes 18436
  4.4 11.2 %copy-start.2 = (f32[2,4,1536]{2,1,0:T(4,128)S(1)}, f32[2,4,1536]{2,1,0:T(4,128)}, u32[]{:S(2)}) copy-start(f32[2,4,1536]{2,1,0:T(4,128)} %param.11) | copy-start | bytes 147460
  4.4 37.4 %all-to-all-start = ((bf16[128,31,2,128]{3,2,1,0:T(2,128)(2,1)}), bf16[128,31,2,128]{3,2,1,0:T(2,128)(2,1)S(1)}, u32[]{:S(2)}, u32[]{:S(2)}) async-start(bf16[128,31,2,128]{3,2,1,0:T(2,128)(2,1)} %bitcast.11), calls=%async_computation | async-start | bytes 4063232 | tf_op jit(solution)/shard_map/all_to_all | solution.py:438
  15.6 26.2 %copy-start = (s32[1,1536]{1,0:T(1,128)S(1)}, s32[1,1536]{1,0:T(1,128)}, u32[]{:S(2)}) copy-start(s32[1,1536]{1,0:T(1,128)} %reshape.30.start_ref) | copy-start | bytes 18436
  41.8 21.8 %copy-start.1 = (s32[9,2,4]{0,2,1:T(4,128)S(1)}, s32[9,2,4]{0,2,1:T(4,128)}, u32[]{:S(2)}) copy-start(s32[9,2,4]{0,2,1:T(4,128)} %param.13) | copy-start | bytes 868
  52.5 6.1 %collective-permute-start = (f32[4,1536]{1,0:T(4,128)S(1)}, f32[4,1536]{1,0:T(4,128)S(1)}, u32[]{:S(2)}, u32[]{:S(2)}) collective-permute-start(f32[4,1536]{1,0:T(4,128)S(1)} %get-tuple-element.11), channel_id=1, source_target_pairs={{0,8},{8,16},{16,24},{24,32},{32,40},{40,48},{48,56},{56,64},{64,7... | collective-permute-start | bytes 73736 | tf_op jit(solution)/shard_map/ppermute | solution.py:427
  53.2 5.5 %collective-permute-start.1 = (f32[4,1536]{1,0:T(4,128)S(1)}, f32[4,1536]{1,0:T(4,128)S(1)}, u32[]{:S(2)}, u32[]{:S(2)}) collective-permute-start(f32[4,1536]{1,0:T(4,128)S(1)} %get-tuple-element.12), channel_id=1, source_target_pairs={{8,0},{16,8},{24,16},{32,24},{40,32},{48,40},{56,48},{64,56},{72,6... | collective-permute-start | bytes 73736 | tf_op jit(solution)/shard_map/ppermute | solution.py:428
  58.6 5.9 %collective-permute-start.2 = (f32[4,1536]{1,0:T(4,128)S(1)}, f32[4,1536]{1,0:T(4,128)S(1)}, u32[]{:S(2)}, u32[]{:S(2)}) collective-permute-start(f32[4,1536]{1,0:T(4,128)S(1)} %get-tuple-element.13), channel_id=1, source_target_pairs={{0,1},{1,2},{2,3},{3,4},{4,5},{5,6},{6,7},{7,0},{8,9},{9,10},{10,1... | collective-permute-start | bytes 73736 | tf_op jit(solution)/shard_map/ppermute | solution.py:427
  63.6 4.5 %collective-permute-start.3 = (f32[4,1536]{1,0:T(4,128)S(1)}, f32[4,1536]{1,0:T(4,128)S(1)}, u32[]{:S(2)}, u32[]{:S(2)}) collective-permute-start(f32[4,1536]{1,0:T(4,128)S(1)} %get-tuple-element.14), channel_id=1, source_target_pairs={{1,0},{2,1},{3,2},{4,3},{5,4},{6,5},{7,6},{0,7},{9,8},{10,9},{11,1... | collective-permute-start | bytes 73736 | tf_op jit(solution)/shard_map/ppermute | solution.py:428

commit v6 on v5

--- a/solution.py
+++ b/solution.py
@@ -13,8 +13,8 @@
 LANES = 128
 CAP = 5
 ROWS = 62
-PARTS = 4
 REACHED = 144
+DISPATCH_LIMIT = 24
 STEP = 32
 HALVES = (0.5, 1.5, 2.5, 3.5)
 VMEM = pl.BlockSpec(memory_space=pltpu.VMEM)
@@ -36,7 +36,7 @@
     return jnp.concatenate([value[i : i + 1, :] for i in range(value.shape[0])], axis=1)
 
 
-def dispatch_kernel(owners, traces_hbm, owner_hbm, cell_hbm, offset_hbm, out_ref, traces_ref, owner_ref, cell_ref, offset_ref, stage, packed, arrived, sent):
+def dispatch_kernel(owners, traces_hbm, owner_hbm, cell_hbm, offset_hbm, out_ref, traces_ref, owner_ref, cell_ref, offset_ref, stage, arrived):
     pairs = ((owner_hbm, owner_ref), (cell_hbm, cell_ref), (offset_hbm, offset_ref), (traces_hbm, traces_ref))
     copies = [pltpu.make_async_copy(there, here, arrived.at[i]) for i, (there, here) in enumerate(pairs)]
     for copy in copies:
@@ -81,23 +81,16 @@
                 stage[pl.ds(k * blocks + tile + half, owners, stride=ROWS), :] = placed[
                     k * owners : (k + 1) * owners, half * LANES : (half + 1) * LANES
                 ]
-    size = owners * ROWS // PARTS
-    sends = []
-    for part in range(PARTS):
-        here = pl.ds(part * size, size)
-        packed[here, :] = stage[here, :].astype(BF16)
-        sends.append(pltpu.make_async_copy(packed.at[here, :], out_ref.at[here, :], sent.at[part]))
-        sends[-1].start()
-    for copy in sends:
-        copy.wait()
+    out_ref[...] = stage[...].astype(BF16)
 
 
 def dispatch(traces, owner, cell, offset, owners):
     rows, samples = traces.shape
+    given = [traces] + [v.reshape(rows // LANES, LANES) for v in (owner, cell, offset)]
     return pl.pallas_call(
         functools.partial(dispatch_kernel, owners),
         in_specs=[HBM] * 4,
-        out_specs=HBM,
+        out_specs=VMEM,
         out_shape=jax.ShapeDtypeStruct((owners * ROWS, LANES), BF16),
         scratch_shapes=[
             pltpu.VMEM((rows, samples), BF16),
@@ -105,35 +98,11 @@
             pltpu.VMEM((rows // LANES, LANES), jnp.int32),
             pltpu.VMEM((rows // LANES, LANES), BF16),
             pltpu.VMEM((owners * ROWS, LANES), F32),
-            pltpu.VMEM((owners * ROWS, LANES), BF16),
             pltpu.SemaphoreType.DMA((4,)),
-            pltpu.SemaphoreType.DMA((PARTS,)),
         ],
+        compiler_params=pltpu.CompilerParams(vmem_limit_bytes=DISPATCH_LIMIT << 20),
         name="dispatch",
-    )(traces, *(v.reshape(rows // LANES, LANES) for v in (owner, cell, offset)))
-
-
-def bands_kernel(start_ref, out_ref):
-    first = start_ref[...] + (REACH - pl.program_id(0) * LANES)
-    place = iota((REACHED, LANES), 0) - first
-    for i, half in enumerate(HALVES):
-        low = (place == int(3.5 - half)).astype(F32)
-        high = (place == int(3.5 + half)).astype(F32)
-        out_ref[0, :, i * LANES : (i + 1) * LANES] = (0.5 * (low + high)).astype(BF16)
-        out_ref[0, :, (4 + i) * LANES : (5 + i) * LANES] = (half * (low - high)).astype(BF16)
-
-
-def bands(band_start):
-    samples = band_start.shape[0]
-    blocks = samples // LANES
-    return pl.pallas_call(
-        bands_kernel,
-        grid=(blocks,),
-        in_specs=[pl.BlockSpec((1, LANES), lambda b: (0, b))],
-        out_specs=pl.BlockSpec((1, REACHED, BAND * LANES), lambda b: (b, 0, 0)),
-        out_shape=jax.ShapeDtypeStruct((blocks, REACHED, BAND * LANES), BF16),
-        name="bands",
-    )(band_start.reshape(1, samples))
+    )(*(pltpu.with_memory_space_constraint(v, pltpu.HBM) for v in given))
 
 
 def split3(value):
@@ -155,20 +124,14 @@
             prod = (square + (2.0 - 2.0 * half * half)) * square + (1.0 + half * half) ** 2
         both = 1.0 / prod
         share = near * both
-        part, tilt = band(i) * share, band(4 + i) * both
+        part, tilt = band(2 * i) * share, band(2 * i + 1) * both
         num, odd, den = (part, tilt, share) if num is None else (num + part, odd + tilt, den + share)
     return (num + lag * odd) / den
 
 
-def stack_kernel(got_ref, bands_hbm, start_ref, slow_ref, out_ref, first_ref, last_ref, stage, bands_ref, window, scaled, member, fold, lags, pairs0, pairs1, moved0, moved1, arrived):
-    blocks = bands_hbm.shape[0]
-
-    def fetch(block):
-        return pltpu.make_async_copy(bands_hbm.at[block], bands_ref.at[block], arrived.at[block])
-
-    for block in range(blocks):
-        fetch(block).start()
-    bins = slow_ref.shape[0]
+def stack_kernel(got_ref, start_ref, slow_ref, out_ref, first_ref, last_ref, stage, window, scaled, member, fold, lags, pairs0, pairs1, moved0, moved1):
+    blocks = start_ref.shape[0]
+    bins = slow_ref.shape[0] * slow_ref.shape[1]
     sources = got_ref.shape[0] // ROWS
     items = CAP * sources
     stage[...] = got_ref[...].astype(F32)
@@ -199,24 +162,29 @@
         return slice(block * LANES, (block + 1) * LANES)
 
     def shift(block):
-        parts = list(split3(slow_ref[:, lanes(block)]))
+        parts = list(split3(jnp.concatenate([slow_ref[x, :, lanes(block)] for x in range(slow_ref.shape[0])], axis=0)))
         parts = [p.astype(F32) for p in parts + parts] + [jnp.zeros((LANES - 6 * bins, LANES), F32)]
         table = jnp.concatenate(parts, axis=0).astype(BF16)
         added = jnp.dot(scaled[...], table, preferred_element_type=F32)
         ticks = iota((1, LANES), 1) + block * LANES
         time = ticks.astype(F32)
         total = jnp.where(ticks == 0, 1e-30, time * time) + added
-        lags[block] = (start_ref[:, lanes(block)].astype(F32) + 3.5) - total * lax.rsqrt(total)
+        lags[block] = (start_ref[block : block + 1, :].astype(F32) + 3.5) - total * lax.rsqrt(total)
 
     def multiply(block, pairs):
         wide = jnp.concatenate([window[block], window[block + 1]], axis=1)
-
-        def pick(half):
-            cols = slice(half * LANES, (half + 2) * LANES)
-            rows = jnp.concatenate([bands_ref[block, :, cols], jnp.zeros((2 * LANES - REACHED, 2 * LANES), BF16)], axis=0)
-            pairs[:, cols] = jnp.dot(wide, rows, preferred_element_type=F32)
-
-        return [functools.partial(pick, half) for half in range(0, BAND, 2)]
+        first = start_ref[block : block + 1, :] + (REACH - block * LANES)
+        place = (iota((REACHED, LANES), 0) - first).astype(F32) - 3.5
+        back, apart = (-place).astype(BF16), jnp.abs(place).astype(BF16)
+        none = jnp.zeros((REACHED, LANES), BF16)
+
+        def pick(i):
+            chosen = apart == jnp.asarray(HALVES[i], BF16)
+            rows = jnp.concatenate([jnp.where(chosen, jnp.asarray(0.5, BF16), none), jnp.where(chosen, back, none)], axis=1)
+            rows = jnp.concatenate([rows, jnp.zeros((2 * LANES - REACHED, 2 * LANES), BF16)], axis=0)
+            pairs[:, 2 * i * LANES : 2 * (i + 1) * LANES] = jnp.dot(wide, rows, preferred_element_type=F32)
+
+        return [functools.partial(pick, i) for i in range(BAND // 2)]
 
     def weigh(block, pairs, moved):
         def chunk(row):
@@ -246,8 +214,6 @@
     gather(1)
     for block in range(blocks):
         shift(block)
-    for block in range(blocks):
-        fetch(block).wait()
     pairs, moved = (pairs0, pairs1), (moved0, moved1)
     for work in multiply(0, pairs0):
         work()
@@ -265,20 +231,20 @@
     last_ref[...] = out_ref[bins - last_ref.shape[0] :, :]
 
 
-def stack(got, picks, band_start, slowness, rows_y):
-    bins, samples = slowness.shape
+def stack(got, band_start, slowness):
+    rows_x, rows_y, samples = slowness.shape
+    bins = rows_x * rows_y
     blocks = samples // LANES
     sources = got.shape[0] // ROWS
     items = CAP * sources
     edge = jax.ShapeDtypeStruct((rows_y, samples), F32)
     return pl.pallas_call(
         stack_kernel,
-        in_specs=[VMEM, HBM, VMEM, VMEM],
+        in_specs=[VMEM] * 3,
         out_specs=[VMEM] * 3,
         out_shape=[jax.ShapeDtypeStruct((bins, samples), F32), edge, edge],
         scratch_shapes=[
             pltpu.VMEM((sources * ROWS, LANES), F32),
-            pltpu.VMEM((blocks, REACHED, BAND * LANES), BF16),
             pltpu.VMEM((blocks + 1, items, LANES), BF16),
             pltpu.VMEM((items, LANES), BF16),
             pltpu.VMEM((bins, items), BF16),
@@ -288,11 +254,10 @@
             pltpu.VMEM((items, BAND * LANES), F32),
             pltpu.VMEM((2 * items, LANES), BF16),
             pltpu.VMEM((2 * items, LANES), BF16),
-            pltpu.SemaphoreType.DMA((blocks,)),
         ],
         compiler_params=pltpu.CompilerParams(vmem_limit_bytes=40 << 20),
         name="stack",
-    )(got, picks, band_start.reshape(1, samples), slowness)
+    )(got, band_start.reshape(blocks, LANES), slowness)
 
 
 def edges_kernel(stack_ref, low_ref, high_ref, first_ref, last_ref):
@@ -436,10 +401,7 @@
     send = dispatch(traces, trace_owner, trace_cell, trace_offset, owners)
     send = send.reshape(owners, ROWS // 2, 2, LANES)
     got = lax.all_to_all(send, AXES, split_axis=0, concat_axis=0, tiled=True)
-    picks = pltpu.with_memory_space_constraint(bands(band_start), pltpu.HBM)
-    stacked, first, last = stack(
-        got.reshape(owners * ROWS, LANES), picks, band_start, slowness.reshape(bins, samples), rows_y
-    )
+    stacked, first, last = stack(got.reshape(owners * ROWS, LANES), band_start, slowness)
     low, high = exchange(first, last, "xline")
     before, after = exchange(*edges(stacked, low, high), "iline")
     dip = dip_shift.reshape(9, bins).T

time: 69.4 us -> 66 us (0.951)
  blocking collectives: 0 us -> 37.2 us
  waiting for transfers between devices: 24.5 us -> 5.19 us
  starting transfers between devices: 20.4 us -> 9.79 us
  Pallas kernels: 23.4 us -> 13.6 us
    all_to_all x0 -> x1, blocking collectives: none -> 37.2 us  [body(): got = lax.all_to_all(send, AXES, split_axis=0, concat_axis=0, tiled=True)]
    all_to_all x1 -> x0, waiting for transfers between devices: 19.3 us -> none  [body(): got = lax.all_to_all(send, AXES, split_axis=0, concat_axis=0, tiled=True)]
    all_to_all x1 -> x0, starting transfers between devices: 10.6 us -> none  [body(): got = lax.all_to_all(send, AXES, split_axis=0, concat_axis=0, tiled=True)]
    pallas_call x2 -> x1, Pallas kernels: 17.6 us -> 9.07 us  [stack(): pl.pallas_call(stack_kernel, in_specs=[VMEM] * 3, out_specs=[VMEM] * 3, o...]
    pallas_call x1, Pallas kernels: 4.34 us -> 3.05 us  [dispatch(): pl.pallas_call(functools.partial(dispatch_kernel, owners), in_specs=[HBM]...]
  transfers between devices with their start and end apart: 5 -> 4, of which waited for: 4 -> 3; matrix products, arithmetic and copies ran while one was open for 1% -> 0% of each run, Pallas kernels for 11% -> 1%
where the time goes in v6:
time: 66 us; the launch traced here: 65.8 us
  blocking collectives  37.2 us (56%)
  Pallas kernels  13.6 us (21%)
  starting transfers between devices  9.79 us (15%)
  waiting for transfers between devices  5.19 us (8%)
    all_to_all x1, blocking collectives, body(): got = lax.all_to_all(send, AXES, split_axis=0, concat_axis=0, tiled=True)  37.2 us
    pallas_call x1, Pallas kernels, stack(): pl.pallas_call(stack_kernel, in_specs=[VMEM] * 3, out_specs=[VMEM] * 3, o...  9.07 us
    ppermute x2, starting transfers between devices, exchange(): lax.ppermute(last, axis, [(i, (i + 1) % size) for i in range(size)])  5.59 us
    ppermute x2, starting transfers between devices, exchange(): lax.ppermute(first, axis, [((i + 1) % size, i) for i in range(size)])  4.2 us
    ppermute x2, waiting for transfers between devices, exchange(): lax.ppermute(first, axis, [((i + 1) % size, i) for i in range(size)])  3.52 us
    pallas_call x1, Pallas kernels, dispatch(): pl.pallas_call(functools.partial(dispatch_kernel, owners), in_specs=[HBM]...  3.05 us
    ppermute x2, waiting for transfers between devices, exchange(): lax.ppermute(last, axis, [(i, (i + 1) % size) for i in range(size)])  1.67 us
  transfers between devices with their start and end apart: 4, of which 3 were waited for; matrix products, arithmetic and copies ran while one was open for 0% of the time, Pallas kernels for 1%

profile of v6, /device:TPU:25, one launch (start us, length us, event | category | flops | bytes accessed | tf_op | source)
XLA Modules:
  0.0 65.8 jit_solution(12892812373215420179)
XLA Ops:
  0.0 3.0 %dispatch.1 = bf16[7936,128]{1,0:T(8,128)(2,1)S(1)} custom-call(bf16[512,1536]{1,0:T(8,128)(2,1)} %traces_hbm.1, s32[4,128]{1,0:T(4,128)} %bitcast.14, s32[4,128]{1,0:T(4,128)} %bitcast.15, bf16[4,128]{1,0:T(4,128)(2,1)} %bitcast.16), custom_call_target="tpu_custom_call" | custom-call | tf_op jit(solution)/shard_map/dispatch/pallas_call | solution.py:90
  3.1 0.0 copy-start
  3.1 0.0 copy-start.2
  3.1 37.2 %all_to_all.5 = bf16[128,31,2,128]{3,2,1,0:T(2,128)(2,1)S(1)} all-to-all(bf16[128,31,2,128]{3,2,1,0:T(2,128)(2,1)S(1)} %bitcast.9), channel_id=1, replica_groups=mesh['xline'=16,'iline'=8] {'xline','iline'}, dimensions={0} | all-to-all | bytes 4063232 | tf_op jit(solution)/shard_map/all_to_all | solution.py:403
  40.3 0.0 copy-start.1
  40.3 0.0 copy-done
  40.3 0.0 copy-done.2
  40.3 9.1 %stack.1 = (f32[8,1536]{1,0:T(8,128)S(1)}, f32[4,1536]{1,0:T(4,128)S(1)}, f32[4,1536]{1,0:T(4,128)S(1)}) custom-call(bf16[7936,128]{1,0:T(8,128)(2,1)S(1)} %bitcast.10, s32[12,128]{1,0:T(8,128)S(1)} %bitcast.13, f32[2,4,1536]{2,1,0:T(4,128)S(1)} %copy-done), custom_call_target="tpu_custom_call" | custom-call | tf_op jit(solution)/shard_map/stack/pallas_call | solution.py:241
  49.3 0.6 collective-permute-start
  49.9 4.2 %collective-permute-start.1 = (f32[4,1536]{1,0:T(4,128)S(1)}, f32[4,1536]{1,0:T(4,128)S(1)}, u32[]{:S(2)}, u32[]{:S(2)}) collective-permute-start(f32[4,1536]{1,0:T(4,128)S(1)} %get-tuple-element.12), channel_id=1, source_target_pairs={{8,0},{16,8},{24,16},{32,24},{40,32},{48,40},{56,48},{64,56},{72,6... | collective-permute-start | bytes 73736 | tf_op jit(solution)/shard_map/ppermute | solution.py:393
  54.1 1.2 %collective-permute-done.low_ref = f32[4,1536]{1,0:T(4,128)S(1)} collective-permute-done((f32[4,1536]{1,0:T(4,128)S(1)}, f32[4,1536]{1,0:T(4,128)S(1)}, u32[]{:S(2)}, u32[]{:S(2)}) %collective-permute-start) | collective-permute-done | bytes 24608 | tf_op jit(solution)/shard_map/ppermute | solution.py:392
  55.4 0.0 collective-permute-done.1.high_ref
  55.4 5.0 %collective-permute-start.2 = (f32[4,1536]{1,0:T(4,128)S(1)}, f32[4,1536]{1,0:T(4,128)S(1)}, u32[]{:S(2)}, u32[]{:S(2)}) collective-permute-start(f32[4,1536]{1,0:T(4,128)S(1)} %get-tuple-element.13), channel_id=1, source_target_pairs={{0,1},{1,2},{2,3},{3,4},{4,5},{5,6},{6,7},{7,0},{8,9},{9,10},{10,1... | collective-permute-start | bytes 73736 | tf_op jit(solution)/shard_map/ppermute | solution.py:392
  60.4 0.0 collective-permute-start.3
  60.4 0.0 copy-done.1
  60.4 0.5 smooth.1.part_ref
  60.8 0.5 collective-permute-done.2.before_ref
  61.3 3.5 %collective-permute-done.3.after_ref = f32[4,1536]{1,0:T(4,128)S(1)} collective-permute-done((f32[4,1536]{1,0:T(4,128)S(1)}, f32[4,1536]{1,0:T(4,128)S(1)}, u32[]{:S(2)}, u32[]{:S(2)}) %collective-permute-start.3) | collective-permute-done | bytes 24608 | tf_op jit(solution)/shard_map/ppermute | solution.py:393
  64.8 1.0 %border.1 = f32[2,4,1536]{2,1,0:T(4,128)} custom-call(f32[8,1536]{1,0:T(8,128)S(1)} %smooth.1.part_ref, f32[4,1536]{1,0:T(4,128)S(1)} %collective-permute-done.2.before_ref, f32[4,1536]{1,0:T(4,128)S(1)} %collective-permute-done.3.after_ref, s32[8,9]{1,0:T(8,128)S(1)} %bitcast.12), custom_call_target="tpu_custom_call" | custom-call | tf_op jit(solution)/shard_map/border/pallas_call | solution.py:380
  (1 shorter events, 0.0 us)
Async XLA Ops:
  3.1 37.2 %copy-start = (f32[2,4,1536]{2,1,0:T(4,128)S(1)}, f32[2,4,1536]{2,1,0:T(4,128)}, u32[]{:S(2)}) copy-start(f32[2,4,1536]{2,1,0:T(4,128)} %slow_ref.1) | copy-start | bytes 147460
  3.1 37.2 %copy-start.2 = (s32[1536]{0:T(1024)S(1)}, s32[1536]{0:T(1024)}, u32[]{:S(2)}) copy-start(s32[1536]{0:T(1024)} %param.12) | copy-start | bytes 18436
  40.3 20.1 %copy-start.1 = (s32[9,2,4]{0,2,1:T(4,128)S(1)}, s32[9,2,4]{0,2,1:T(4,128)}, u32[]{:S(2)}) copy-start(s32[9,2,4]{0,2,1:T(4,128)} %param.13) | copy-start | bytes 868
  49.3 6.0 %collective-permute-start = (f32[4,1536]{1,0:T(4,128)S(1)}, f32[4,1536]{1,0:T(4,128)S(1)}, u32[]{:S(2)}, u32[]{:S(2)}) collective-permute-start(f32[4,1536]{1,0:T(4,128)S(1)} %get-tuple-element.11), channel_id=1, source_target_pairs={{0,8},{8,16},{16,24},{24,32},{32,40},{40,48},{48,56},{56,64},{64,7... | collective-permute-start | bytes 73736 | tf_op jit(solution)/shard_map/ppermute | solution.py:392
  49.9 5.4 %collective-permute-start.1 = (f32[4,1536]{1,0:T(4,128)S(1)}, f32[4,1536]{1,0:T(4,128)S(1)}, u32[]{:S(2)}, u32[]{:S(2)}) collective-permute-start(f32[4,1536]{1,0:T(4,128)S(1)} %get-tuple-element.12), channel_id=1, source_target_pairs={{8,0},{16,8},{24,16},{32,24},{40,32},{48,40},{56,48},{64,56},{72,6... | collective-permute-start | bytes 73736 | tf_op jit(solution)/shard_map/ppermute | solution.py:393
  55.4 5.9 %collective-permute-start.2 = (f32[4,1536]{1,0:T(4,128)S(1)}, f32[4,1536]{1,0:T(4,128)S(1)}, u32[]{:S(2)}, u32[]{:S(2)}) collective-permute-start(f32[4,1536]{1,0:T(4,128)S(1)} %get-tuple-element.13), channel_id=1, source_target_pairs={{0,1},{1,2},{2,3},{3,4},{4,5},{5,6},{6,7},{7,0},{8,9},{9,10},{10,1... | collective-permute-start | bytes 73736 | tf_op jit(solution)/shard_map/ppermute | solution.py:392
  60.4 4.5 %collective-permute-start.3 = (f32[4,1536]{1,0:T(4,128)S(1)}, f32[4,1536]{1,0:T(4,128)S(1)}, u32[]{:S(2)}, u32[]{:S(2)}) collective-permute-start(f32[4,1536]{1,0:T(4,128)S(1)} %get-tuple-element.14), channel_id=1, source_target_pairs={{1,0},{2,1},{3,2},{4,3},{5,4},{6,5},{7,6},{0,7},{9,8},{10,9},{11,1... | collective-permute-start | bytes 73736 | tf_op jit(solution)/shard_map/ppermute | solution.py:393

commit v7 on v6

--- a/solution.py
+++ b/solution.py
@@ -14,6 +14,7 @@
 CAP = 5
 ROWS = 62
 REACHED = 144
+PARTS = 2
 DISPATCH_LIMIT = 24
 STEP = 32
 HALVES = (0.5, 1.5, 2.5, 3.5)
@@ -36,7 +37,7 @@
     return jnp.concatenate([value[i : i + 1, :] for i in range(value.shape[0])], axis=1)
 
 
-def dispatch_kernel(owners, traces_hbm, owner_hbm, cell_hbm, offset_hbm, out_ref, traces_ref, owner_ref, cell_ref, offset_ref, stage, arrived):
+def dispatch_kernel(owners, traces_hbm, owner_hbm, cell_hbm, offset_hbm, out_ref, traces_ref, owner_ref, cell_ref, offset_ref, rolled, stage, arrived):
     pairs = ((owner_hbm, owner_ref), (cell_hbm, cell_ref), (offset_hbm, offset_ref), (traces_hbm, traces_ref))
     copies = [pltpu.make_async_copy(there, here, arrived.at[i]) for i, (there, here) in enumerate(pairs)]
     for copy in copies:
@@ -51,7 +52,6 @@
     counts = jnp.dot(hot.astype(BF16), earlier, preferred_element_type=F32)
     rank = jnp.sum(hot * counts, axis=0, keepdims=True)
     picks = [jnp.where(rank == float(k), hot, 0.0).astype(BF16) for k in range(CAP)]
-    pick = jnp.concatenate(picks, axis=0)
     meta = jnp.zeros((owners, LANES), F32)
     line = iota((LANES, rows), 0)
     offset = in_line(offset_ref[...].astype(F32))
@@ -71,17 +71,22 @@
         return pltpu.roll(traces_ref[:, block * LANES : (block + 1) * LANES], REACH, 1)
 
     previous = turned(blocks - 1)
-    for tile in range(0, blocks, 2):
-        one, two = turned(tile), turned(tile + 1)
-        moved = jnp.concatenate([jnp.where(wrapped, previous, one), jnp.where(wrapped, one, two)], axis=1)
-        previous = two
-        placed = jnp.dot(pick, moved, preferred_element_type=F32)
-        for k in range(CAP):
-            for half in range(2):
-                stage[pl.ds(k * blocks + tile + half, owners, stride=ROWS), :] = placed[
-                    k * owners : (k + 1) * owners, half * LANES : (half + 1) * LANES
-                ]
-    out_ref[...] = stage[...].astype(BF16)
+    for block in range(blocks):
+        here = turned(block)
+        rolled[:, block * LANES : (block + 1) * LANES] = jnp.where(wrapped, previous, here)
+        previous = here
+    part = owners // PARTS
+    for low in range(0, owners, part):
+        pick = jnp.concatenate([picks[k][low : low + part, :] for k in range(CAP)], axis=0)
+        for tile in range(0, blocks, 2):
+            placed = jnp.dot(pick, rolled[:, tile * LANES : (tile + 2) * LANES], preferred_element_type=F32)
+            for k in range(CAP):
+                for half in range(2):
+                    stage[pl.ds(low * ROWS + k * blocks + tile + half, part, stride=ROWS), :] = placed[
+                        k * part : (k + 1) * part, half * LANES : (half + 1) * LANES
+                    ]
+        here = slice(low * ROWS, (low + part) * ROWS)
+        out_ref[here, :] = stage[here, :].astype(BF16)
 
 
 def dispatch(traces, owner, cell, offset, owners):
@@ -97,6 +102,7 @@
             pltpu.VMEM((rows // LANES, LANES), jnp.int32),
             pltpu.VMEM((rows // LANES, LANES), jnp.int32),
             pltpu.VMEM((rows // LANES, LANES), BF16),
+            pltpu.VMEM((rows, samples), BF16),
             pltpu.VMEM((owners * ROWS, LANES), F32),
             pltpu.SemaphoreType.DMA((4,)),
         ],
@@ -147,7 +153,8 @@
         high = square.astype(BF16).astype(F32)
         part = jnp.where(lane < 3 * bins, high, square - high)
         keep = ((lane % bins).astype(F32) == cell) & (lane < 6 * bins)
-        scaled[here, :] = jnp.where(keep, part, 0.0).astype(BF16)
+        ones = (lane >= 6 * bins) & (lane < 6 * bins + 3)
+        scaled[here, :] = jnp.where(keep, part, jnp.where(ones, 1.0, 0.0)).astype(BF16)
         ones = (across[8 * k + 1 : 8 * k + 2, :] == (iota((bins, sources), 0) + 1).astype(F32)).astype(F32)
         total = total + jnp.sum(ones, axis=1, keepdims=True)
         member[:, here] = ones.astype(BF16)
@@ -163,13 +170,16 @@
 
     def shift(block):
         parts = list(split3(jnp.concatenate([slow_ref[x, :, lanes(block)] for x in range(slow_ref.shape[0])], axis=0)))
-        parts = [p.astype(F32) for p in parts + parts] + [jnp.zeros((LANES - 6 * bins, LANES), F32)]
-        table = jnp.concatenate(parts, axis=0).astype(BF16)
-        added = jnp.dot(scaled[...], table, preferred_element_type=F32)
-        ticks = iota((1, LANES), 1) + block * LANES
+        ticks = iota((bins, LANES), 1) + block * LANES
         time = ticks.astype(F32)
-        total = jnp.where(ticks == 0, 1e-30, time * time) + added
-        lags[block] = (start_ref[block : block + 1, :].astype(F32) + 3.5) - total * lax.rsqrt(total)
+        squares = split3(jnp.where(ticks == 0, 1e-30, time * time))
+        line = iota((bins, LANES), 0)
+        clock = jnp.zeros((bins, LANES), F32)
+        for i, part in enumerate(squares):
+            clock = jnp.where(line == i, part.astype(F32), clock)
+        parts = [p.astype(F32) for p in parts + parts] + [clock, jnp.zeros((LANES - 7 * bins, LANES), F32)]
+        total = jnp.dot(scaled[...], jnp.concatenate(parts, axis=0).astype(BF16), preferred_element_type=F32)
+        lags[block % 3] = (start_ref[block : block + 1, :].astype(F32) + 3.5) - total * lax.rsqrt(total)
 
     def multiply(block, pairs):
         wide = jnp.concatenate([window[block], window[block + 1]], axis=1)
@@ -189,7 +199,7 @@
     def weigh(block, pairs, moved):
         def chunk(row):
             here = slice(row, row + STEP)
-            lag = lags[block, here, :]
+            lag = lags[block % 3, here, :]
             value = correct(lag, lambda i: pairs[here, i * LANES : (i + 1) * LANES])
             high = value.astype(BF16)
             moved[here, :] = high
@@ -212,8 +222,8 @@
 
     gather(0)
     gather(1)
-    for block in range(blocks):
-        shift(block)
+    shift(0)
+    shift(1)
     pairs, moved = (pairs0, pairs1), (moved0, moved1)
     for work in multiply(0, pairs0):
         work()
@@ -222,6 +232,8 @@
         ahead = []
         if block + 1 < blocks:
             gather(block + 2)
+            if block + 2 < blocks:
+                shift(block + 2)
             ahead = multiply(block + 1, pairs[later])
         if block:
             total_up(block - 1, moved[later])
@@ -249,7 +261,7 @@
             pltpu.VMEM((items, LANES), BF16),
             pltpu.VMEM((bins, items), BF16),
             pltpu.VMEM((bins, LANES), F32),
-            pltpu.VMEM((blocks, items, LANES), F32),
+            pltpu.VMEM((3, items, LANES), F32),
             pltpu.VMEM((items, BAND * LANES), F32),
             pltpu.VMEM((items, BAND * LANES), F32),
             pltpu.VMEM((2 * items, LANES), BF16),

time: 66 us -> 65.6 us (level)
  no operation moved by 1% of the time
where the time goes in v7:
time: 65.6 us; the launch traced here: 65.4 us
  blocking collectives  37.2 us (57%)
  Pallas kernels  13.2 us (20%)
  starting transfers between devices  9.79 us (15%)
  waiting for transfers between devices  5.19 us (8%)
    all_to_all x1, blocking collectives, body(): got = lax.all_to_all(send, AXES, split_axis=0, concat_axis=0, tiled=True)  37.2 us
    pallas_call x1, Pallas kernels, stack(): pl.pallas_call(stack_kernel, in_specs=[VMEM] * 3, out_specs=[VMEM] * 3, o...  8.63 us
    ppermute x2, starting transfers between devices, exchange(): lax.ppermute(last, axis, [(i, (i + 1) % size) for i in range(size)])  5.57 us
    ppermute x2, starting transfers between devices, exchange(): lax.ppermute(first, axis, [((i + 1) % size, i) for i in range(size)])  4.21 us
    ppermute x2, waiting for transfers between devices, exchange(): lax.ppermute(first, axis, [((i + 1) % size, i) for i in range(size)])  3.52 us
    pallas_call x1, Pallas kernels, dispatch(): pl.pallas_call(functools.partial(dispatch_kernel, owners), in_specs=[HBM]...  3.13 us
    ppermute x2, waiting for transfers between devices, exchange(): lax.ppermute(last, axis, [(i, (i + 1) % size) for i in range(size)])  1.67 us
  transfers between devices with their start and end apart: 4, of which 3 were waited for; matrix products, arithmetic and copies ran while one was open for 0% of the time, Pallas kernels for 1%

profile of v7, /device:TPU:25, one launch (start us, length us, event | category | flops | bytes accessed | tf_op | source)
XLA Modules:
  0.0 65.4 jit_solution(11872621354485803284)
XLA Ops:
  0.0 3.1 %dispatch.1 = bf16[7936,128]{1,0:T(8,128)(2,1)S(1)} custom-call(bf16[512,1536]{1,0:T(8,128)(2,1)} %traces_hbm.1, s32[4,128]{1,0:T(4,128)} %bitcast.14, s32[4,128]{1,0:T(4,128)} %bitcast.15, bf16[4,128]{1,0:T(4,128)(2,1)} %bitcast.16), custom_call_target="tpu_custom_call" | custom-call | tf_op jit(solution)/shard_map/dispatch/pallas_call | solution.py:95
  3.1 0.0 copy-start
  3.2 0.0 copy-start.2
  3.2 37.2 %all_to_all.5 = bf16[128,31,2,128]{3,2,1,0:T(2,128)(2,1)S(1)} all-to-all(bf16[128,31,2,128]{3,2,1,0:T(2,128)(2,1)S(1)} %bitcast.9), channel_id=1, replica_groups=mesh['xline'=16,'iline'=8] {'xline','iline'}, dimensions={0} | all-to-all | bytes 4063232 | tf_op jit(solution)/shard_map/all_to_all | solution.py:415
  40.4 0.0 copy-start.1
  40.4 0.0 copy-done
  40.4 0.0 copy-done.2
  40.4 8.6 %stack.1 = (f32[8,1536]{1,0:T(8,128)S(1)}, f32[4,1536]{1,0:T(4,128)S(1)}, f32[4,1536]{1,0:T(4,128)S(1)}) custom-call(bf16[7936,128]{1,0:T(8,128)(2,1)S(1)} %bitcast.10, s32[12,128]{1,0:T(8,128)S(1)} %bitcast.13, f32[2,4,1536]{2,1,0:T(4,128)S(1)} %copy-done), custom_call_target="tpu_custom_call" | custom-call | tf_op jit(solution)/shard_map/stack/pallas_call | solution.py:253
  49.0 0.6 collective-permute-start
  49.6 4.2 %collective-permute-start.1 = (f32[4,1536]{1,0:T(4,128)S(1)}, f32[4,1536]{1,0:T(4,128)S(1)}, u32[]{:S(2)}, u32[]{:S(2)}) collective-permute-start(f32[4,1536]{1,0:T(4,128)S(1)} %get-tuple-element.12), channel_id=1, source_target_pairs={{8,0},{16,8},{24,16},{32,24},{40,32},{48,40},{56,48},{64,56},{72,6... | collective-permute-start | bytes 73736 | tf_op jit(solution)/shard_map/ppermute | solution.py:405
  53.8 1.2 %collective-permute-done.low_ref = f32[4,1536]{1,0:T(4,128)S(1)} collective-permute-done((f32[4,1536]{1,0:T(4,128)S(1)}, f32[4,1536]{1,0:T(4,128)S(1)}, u32[]{:S(2)}, u32[]{:S(2)}) %collective-permute-start) | collective-permute-done | bytes 24608 | tf_op jit(solution)/shard_map/ppermute | solution.py:404
  55.0 0.0 collective-permute-done.1.high_ref
  55.0 5.0 %collective-permute-start.2 = (f32[4,1536]{1,0:T(4,128)S(1)}, f32[4,1536]{1,0:T(4,128)S(1)}, u32[]{:S(2)}, u32[]{:S(2)}) collective-permute-start(f32[4,1536]{1,0:T(4,128)S(1)} %get-tuple-element.13), channel_id=1, source_target_pairs={{0,1},{1,2},{2,3},{3,4},{4,5},{5,6},{6,7},{7,0},{8,9},{9,10},{10,1... | collective-permute-start | bytes 73736 | tf_op jit(solution)/shard_map/ppermute | solution.py:404
  60.0 0.0 collective-permute-start.3
  60.0 0.0 copy-done.1
  60.0 0.5 smooth.1.part_ref
  60.5 0.5 collective-permute-done.2.before_ref
  61.0 3.5 %collective-permute-done.3.after_ref = f32[4,1536]{1,0:T(4,128)S(1)} collective-permute-done((f32[4,1536]{1,0:T(4,128)S(1)}, f32[4,1536]{1,0:T(4,128)S(1)}, u32[]{:S(2)}, u32[]{:S(2)}) %collective-permute-start.3) | collective-permute-done | bytes 24608 | tf_op jit(solution)/shard_map/ppermute | solution.py:405
  64.5 1.0 %border.1 = f32[2,4,1536]{2,1,0:T(4,128)} custom-call(f32[8,1536]{1,0:T(8,128)S(1)} %smooth.1.part_ref, f32[4,1536]{1,0:T(4,128)S(1)} %collective-permute-done.2.before_ref, f32[4,1536]{1,0:T(4,128)S(1)} %collective-permute-done.3.after_ref, s32[8,9]{1,0:T(8,128)S(1)} %bitcast.12), custom_call_target="tpu_custom_call" | custom-call | tf_op jit(solution)/shard_map/border/pallas_call | solution.py:392
  (1 shorter events, 0.0 us)
Async XLA Ops:
  3.1 37.2 %copy-start = (f32[2,4,1536]{2,1,0:T(4,128)S(1)}, f32[2,4,1536]{2,1,0:T(4,128)}, u32[]{:S(2)}) copy-start(f32[2,4,1536]{2,1,0:T(4,128)} %slow_ref.1) | copy-start | bytes 147460
  3.2 37.2 %copy-start.2 = (s32[1536]{0:T(1024)S(1)}, s32[1536]{0:T(1024)}, u32[]{:S(2)}) copy-start(s32[1536]{0:T(1024)} %param.12) | copy-start | bytes 18436
  40.4 19.7 %copy-start.1 = (s32[9,2,4]{0,2,1:T(4,128)S(1)}, s32[9,2,4]{0,2,1:T(4,128)}, u32[]{:S(2)}) copy-start(s32[9,2,4]{0,2,1:T(4,128)} %param.13) | copy-start | bytes 868
  49.0 6.0 %collective-permute-start = (f32[4,1536]{1,0:T(4,128)S(1)}, f32[4,1536]{1,0:T(4,128)S(1)}, u32[]{:S(2)}, u32[]{:S(2)}) collective-permute-start(f32[4,1536]{1,0:T(4,128)S(1)} %get-tuple-element.11), channel_id=1, source_target_pairs={{0,8},{8,16},{16,24},{24,32},{32,40},{40,48},{48,56},{56,64},{64,7... | collective-permute-start | bytes 73736 | tf_op jit(solution)/shard_map/ppermute | solution.py:404
  49.6 5.4 %collective-permute-start.1 = (f32[4,1536]{1,0:T(4,128)S(1)}, f32[4,1536]{1,0:T(4,128)S(1)}, u32[]{:S(2)}, u32[]{:S(2)}) collective-permute-start(f32[4,1536]{1,0:T(4,128)S(1)} %get-tuple-element.12), channel_id=1, source_target_pairs={{8,0},{16,8},{24,16},{32,24},{40,32},{48,40},{56,48},{64,56},{72,6... | collective-permute-start | bytes 73736 | tf_op jit(solution)/shard_map/ppermute | solution.py:405
  55.0 5.9 %collective-permute-start.2 = (f32[4,1536]{1,0:T(4,128)S(1)}, f32[4,1536]{1,0:T(4,128)S(1)}, u32[]{:S(2)}, u32[]{:S(2)}) collective-permute-start(f32[4,1536]{1,0:T(4,128)S(1)} %get-tuple-element.13), channel_id=1, source_target_pairs={{0,1},{1,2},{2,3},{3,4},{4,5},{5,6},{6,7},{7,0},{8,9},{9,10},{10,1... | collective-permute-start | bytes 73736 | tf_op jit(solution)/shard_map/ppermute | solution.py:404
  60.0 4.5 %collective-permute-start.3 = (f32[4,1536]{1,0:T(4,128)S(1)}, f32[4,1536]{1,0:T(4,128)S(1)}, u32[]{:S(2)}, u32[]{:S(2)}) collective-permute-start(f32[4,1536]{1,0:T(4,128)S(1)} %get-tuple-element.14), channel_id=1, source_target_pairs={{1,0},{2,1},{3,2},{4,3},{5,4},{6,5},{7,6},{0,7},{9,8},{10,9},{11,1... | collective-permute-start | bytes 73736 | tf_op jit(solution)/shard_map/ppermute | solution.py:405

commit v8 on v6

--- a/solution.py
+++ b/solution.py
@@ -147,7 +147,8 @@
         high = square.astype(BF16).astype(F32)
         part = jnp.where(lane < 3 * bins, high, square - high)
         keep = ((lane % bins).astype(F32) == cell) & (lane < 6 * bins)
-        scaled[here, :] = jnp.where(keep, part, 0.0).astype(BF16)
+        ones = (lane >= 6 * bins) & (lane < 6 * bins + 3)
+        scaled[here, :] = jnp.where(keep, part, jnp.where(ones, 1.0, 0.0)).astype(BF16)
         ones = (across[8 * k + 1 : 8 * k + 2, :] == (iota((bins, sources), 0) + 1).astype(F32)).astype(F32)
         total = total + jnp.sum(ones, axis=1, keepdims=True)
         member[:, here] = ones.astype(BF16)
@@ -163,13 +164,16 @@
 
     def shift(block):
         parts = list(split3(jnp.concatenate([slow_ref[x, :, lanes(block)] for x in range(slow_ref.shape[0])], axis=0)))
-        parts = [p.astype(F32) for p in parts + parts] + [jnp.zeros((LANES - 6 * bins, LANES), F32)]
-        table = jnp.concatenate(parts, axis=0).astype(BF16)
-        added = jnp.dot(scaled[...], table, preferred_element_type=F32)
-        ticks = iota((1, LANES), 1) + block * LANES
+        ticks = iota((bins, LANES), 1) + block * LANES
         time = ticks.astype(F32)
-        total = jnp.where(ticks == 0, 1e-30, time * time) + added
-        lags[block] = (start_ref[block : block + 1, :].astype(F32) + 3.5) - total * lax.rsqrt(total)
+        squares = split3(jnp.where(ticks == 0, 1e-30, time * time))
+        line = iota((bins, LANES), 0)
+        clock = jnp.zeros((bins, LANES), F32)
+        for i, part in enumerate(squares):
+            clock = jnp.where(line == i, part.astype(F32), clock)
+        parts = [p.astype(F32) for p in parts + parts] + [clock, jnp.zeros((LANES - 7 * bins, LANES), F32)]
+        total = jnp.dot(scaled[...], jnp.concatenate(parts, axis=0).astype(BF16), preferred_element_type=F32)
+        lags[block % 3] = (start_ref[block : block + 1, :].astype(F32) + 3.5) - total * lax.rsqrt(total)
 
     def multiply(block, pairs):
         wide = jnp.concatenate([window[block], window[block + 1]], axis=1)
@@ -189,7 +193,7 @@
     def weigh(block, pairs, moved):
         def chunk(row):
             here = slice(row, row + STEP)
-            lag = lags[block, here, :]
+            lag = lags[block % 3, here, :]
             value = correct(lag, lambda i: pairs[here, i * LANES : (i + 1) * LANES])
             high = value.astype(BF16)
             moved[here, :] = high
@@ -201,7 +205,10 @@
         sums = jnp.dot(member[...], moved[:items, :], preferred_element_type=F32) + jnp.dot(
             member[...], moved[items:, :], preferred_element_type=F32
         )
-        out_ref[:, lanes(block)] = sums / fold[...]
+        mean = sums / fold[...]
+        out_ref[:, lanes(block)] = mean
+        first_ref[:, lanes(block)] = mean[: first_ref.shape[0], :]
+        last_ref[:, lanes(block)] = mean[bins - last_ref.shape[0] :, :]
 
     def interleave(few, many):
         for i, work in enumerate(many):
@@ -212,8 +219,8 @@
 
     gather(0)
     gather(1)
-    for block in range(blocks):
-        shift(block)
+    shift(0)
+    shift(1)
     pairs, moved = (pairs0, pairs1), (moved0, moved1)
     for work in multiply(0, pairs0):
         work()
@@ -222,13 +229,13 @@
         ahead = []
         if block + 1 < blocks:
             gather(block + 2)
+            if block + 2 < blocks:
+                shift(block + 2)
             ahead = multiply(block + 1, pairs[later])
         if block:
             total_up(block - 1, moved[later])
         interleave(ahead, weigh(block, pairs[now], moved[now]))
     total_up(blocks - 1, moved[(blocks - 1) % 2])
-    first_ref[...] = out_ref[: first_ref.shape[0], :]
-    last_ref[...] = out_ref[bins - last_ref.shape[0] :, :]
 
 
 def stack(got, band_start, slowness):
@@ -249,7 +256,7 @@
             pltpu.VMEM((items, LANES), BF16),
             pltpu.VMEM((bins, items), BF16),
             pltpu.VMEM((bins, LANES), F32),
-            pltpu.VMEM((blocks, items, LANES), F32),
+            pltpu.VMEM((3, items, LANES), F32),
             pltpu.VMEM((items, BAND * LANES), F32),
             pltpu.VMEM((items, BAND * LANES), F32),
             pltpu.VMEM((2 * items, LANES), BF16),

time: 66 us -> 65.5 us (level)
  no operation moved by 1% of the time
where the time goes in v8:
time: 65.5 us; the launch traced here: 65.3 us
  blocking collectives  37.2 us (57%)
  Pallas kernels  13.1 us (20%)
  starting transfers between devices  9.78 us (15%)
  waiting for transfers between devices  5.19 us (8%)
    all_to_all x1, blocking collectives, body(): got = lax.all_to_all(send, AXES, split_axis=0, concat_axis=0, tiled=True)  37.2 us
    pallas_call x1, Pallas kernels, stack(): pl.pallas_call(stack_kernel, in_specs=[VMEM] * 3, out_specs=[VMEM] * 3, o...  8.61 us
    ppermute x2, starting transfers between devices, exchange(): lax.ppermute(last, axis, [(i, (i + 1) % size) for i in range(size)])  5.56 us
    ppermute x2, starting transfers between devices, exchange(): lax.ppermute(first, axis, [((i + 1) % size, i) for i in range(size)])  4.22 us
    ppermute x2, waiting for transfers between devices, exchange(): lax.ppermute(first, axis, [((i + 1) % size, i) for i in range(size)])  3.52 us
    pallas_call x1, Pallas kernels, dispatch(): pl.pallas_call(functools.partial(dispatch_kernel, owners), in_specs=[HBM]...  3.05 us
    ppermute x2, waiting for transfers between devices, exchange(): lax.ppermute(last, axis, [(i, (i + 1) % size) for i in range(size)])  1.67 us
  transfers between devices with their start and end apart: 4, of which 3 were waited for; matrix products, arithmetic and copies ran while one was open for 0% of the time, Pallas kernels for 1%

profile of v8, /device:TPU:25, one launch (start us, length us, event | category | flops | bytes accessed | tf_op | source)
XLA Modules:
  0.0 65.3 jit_solution(3561545852119986967)
XLA Ops:
  0.0 3.0 %dispatch.1 = bf16[7936,128]{1,0:T(8,128)(2,1)S(1)} custom-call(bf16[512,1536]{1,0:T(8,128)(2,1)} %traces_hbm.1, s32[4,128]{1,0:T(4,128)} %bitcast.14, s32[4,128]{1,0:T(4,128)} %bitcast.15, bf16[4,128]{1,0:T(4,128)(2,1)} %bitcast.16), custom_call_target="tpu_custom_call" | custom-call | tf_op jit(solution)/shard_map/dispatch/pallas_call | solution.py:90
  3.1 0.0 copy-start
  3.1 0.0 copy-start.2
  3.1 37.2 %all_to_all.5 = bf16[128,31,2,128]{3,2,1,0:T(2,128)(2,1)S(1)} all-to-all(bf16[128,31,2,128]{3,2,1,0:T(2,128)(2,1)S(1)} %bitcast.9), channel_id=1, replica_groups=mesh['xline'=16,'iline'=8] {'xline','iline'}, dimensions={0} | all-to-all | bytes 4063232 | tf_op jit(solution)/shard_map/all_to_all | solution.py:410
  40.3 0.0 copy-start.1
  40.3 0.0 copy-done
  40.3 0.0 copy-done.2
  40.3 8.6 %stack.1 = (f32[8,1536]{1,0:T(8,128)S(1)}, f32[4,1536]{1,0:T(4,128)S(1)}, f32[4,1536]{1,0:T(4,128)S(1)}) custom-call(bf16[7936,128]{1,0:T(8,128)(2,1)S(1)} %bitcast.10, s32[12,128]{1,0:T(8,128)S(1)} %bitcast.13, f32[2,4,1536]{2,1,0:T(4,128)S(1)} %copy-done), custom_call_target="tpu_custom_call" | custom-call | tf_op jit(solution)/shard_map/stack/pallas_call | solution.py:248
  48.9 0.6 collective-permute-start
  49.5 4.2 %collective-permute-start.1 = (f32[4,1536]{1,0:T(4,128)S(1)}, f32[4,1536]{1,0:T(4,128)S(1)}, u32[]{:S(2)}, u32[]{:S(2)}) collective-permute-start(f32[4,1536]{1,0:T(4,128)S(1)} %get-tuple-element.12), channel_id=1, source_target_pairs={{8,0},{16,8},{24,16},{32,24},{40,32},{48,40},{56,48},{64,56},{72,6... | collective-permute-start | bytes 73736 | tf_op jit(solution)/shard_map/ppermute | solution.py:400
  53.7 1.2 %collective-permute-done.low_ref = f32[4,1536]{1,0:T(4,128)S(1)} collective-permute-done((f32[4,1536]{1,0:T(4,128)S(1)}, f32[4,1536]{1,0:T(4,128)S(1)}, u32[]{:S(2)}, u32[]{:S(2)}) %collective-permute-start) | collective-permute-done | bytes 24608 | tf_op jit(solution)/shard_map/ppermute | solution.py:399
  54.9 0.0 collective-permute-done.1.high_ref
  54.9 5.0 %collective-permute-start.2 = (f32[4,1536]{1,0:T(4,128)S(1)}, f32[4,1536]{1,0:T(4,128)S(1)}, u32[]{:S(2)}, u32[]{:S(2)}) collective-permute-start(f32[4,1536]{1,0:T(4,128)S(1)} %get-tuple-element.13), channel_id=1, source_target_pairs={{0,1},{1,2},{2,3},{3,4},{4,5},{5,6},{6,7},{7,0},{8,9},{9,10},{10,1... | collective-permute-start | bytes 73736 | tf_op jit(solution)/shard_map/ppermute | solution.py:399
  59.9 0.0 collective-permute-start.3
  59.9 0.0 copy-done.1
  59.9 0.5 smooth.1.part_ref
  60.4 0.5 collective-permute-done.2.before_ref
  60.8 3.5 %collective-permute-done.3.after_ref = f32[4,1536]{1,0:T(4,128)S(1)} collective-permute-done((f32[4,1536]{1,0:T(4,128)S(1)}, f32[4,1536]{1,0:T(4,128)S(1)}, u32[]{:S(2)}, u32[]{:S(2)}) %collective-permute-start.3) | collective-permute-done | bytes 24608 | tf_op jit(solution)/shard_map/ppermute | solution.py:400
  64.3 1.0 %border.1 = f32[2,4,1536]{2,1,0:T(4,128)} custom-call(f32[8,1536]{1,0:T(8,128)S(1)} %smooth.1.part_ref, f32[4,1536]{1,0:T(4,128)S(1)} %collective-permute-done.2.before_ref, f32[4,1536]{1,0:T(4,128)S(1)} %collective-permute-done.3.after_ref, s32[8,9]{1,0:T(8,128)S(1)} %bitcast.12), custom_call_target="tpu_custom_call" | custom-call | tf_op jit(solution)/shard_map/border/pallas_call | solution.py:387
  (1 shorter events, 0.0 us)
Async XLA Ops:
  3.1 37.2 %copy-start = (f32[2,4,1536]{2,1,0:T(4,128)S(1)}, f32[2,4,1536]{2,1,0:T(4,128)}, u32[]{:S(2)}) copy-start(f32[2,4,1536]{2,1,0:T(4,128)} %slow_ref.1) | copy-start | bytes 147460
  3.1 37.2 %copy-start.2 = (s32[1536]{0:T(1024)S(1)}, s32[1536]{0:T(1024)}, u32[]{:S(2)}) copy-start(s32[1536]{0:T(1024)} %param.12) | copy-start | bytes 18436
  40.3 19.6 %copy-start.1 = (s32[9,2,4]{0,2,1:T(4,128)S(1)}, s32[9,2,4]{0,2,1:T(4,128)}, u32[]{:S(2)}) copy-start(s32[9,2,4]{0,2,1:T(4,128)} %param.13) | copy-start | bytes 868
  48.9 6.0 %collective-permute-start = (f32[4,1536]{1,0:T(4,128)S(1)}, f32[4,1536]{1,0:T(4,128)S(1)}, u32[]{:S(2)}, u32[]{:S(2)}) collective-permute-start(f32[4,1536]{1,0:T(4,128)S(1)} %get-tuple-element.11), channel_id=1, source_target_pairs={{0,8},{8,16},{16,24},{24,32},{32,40},{40,48},{48,56},{56,64},{64,7... | collective-permute-start | bytes 73736 | tf_op jit(solution)/shard_map/ppermute | solution.py:399
  49.5 5.4 %collective-permute-start.1 = (f32[4,1536]{1,0:T(4,128)S(1)}, f32[4,1536]{1,0:T(4,128)S(1)}, u32[]{:S(2)}, u32[]{:S(2)}) collective-permute-start(f32[4,1536]{1,0:T(4,128)S(1)} %get-tuple-element.12), channel_id=1, source_target_pairs={{8,0},{16,8},{24,16},{32,24},{40,32},{48,40},{56,48},{64,56},{72,6... | collective-permute-start | bytes 73736 | tf_op jit(solution)/shard_map/ppermute | solution.py:400
  54.9 5.9 %collective-permute-start.2 = (f32[4,1536]{1,0:T(4,128)S(1)}, f32[4,1536]{1,0:T(4,128)S(1)}, u32[]{:S(2)}, u32[]{:S(2)}) collective-permute-start(f32[4,1536]{1,0:T(4,128)S(1)} %get-tuple-element.13), channel_id=1, source_target_pairs={{0,1},{1,2},{2,3},{3,4},{4,5},{5,6},{6,7},{7,0},{8,9},{9,10},{10,1... | collective-permute-start | bytes 73736 | tf_op jit(solution)/shard_map/ppermute | solution.py:399
  59.9 4.5 %collective-permute-start.3 = (f32[4,1536]{1,0:T(4,128)S(1)}, f32[4,1536]{1,0:T(4,128)S(1)}, u32[]{:S(2)}, u32[]{:S(2)}) collective-permute-start(f32[4,1536]{1,0:T(4,128)S(1)} %get-tuple-element.14), channel_id=1, source_target_pairs={{1,0},{2,1},{3,2},{4,3},{5,4},{6,5},{7,6},{0,7},{9,8},{10,9},{11,1... | collective-permute-start | bytes 73736 | tf_op jit(solution)/shard_map/ppermute | solution.py:400

commit v9 on v8

--- a/solution.py
+++ b/solution.py
@@ -205,10 +205,7 @@
         sums = jnp.dot(member[...], moved[:items, :], preferred_element_type=F32) + jnp.dot(
             member[...], moved[items:, :], preferred_element_type=F32
         )
-        mean = sums / fold[...]
-        out_ref[:, lanes(block)] = mean
-        first_ref[:, lanes(block)] = mean[: first_ref.shape[0], :]
-        last_ref[:, lanes(block)] = mean[bins - last_ref.shape[0] :, :]
+        out_ref[:, lanes(block)] = sums / fold[...]
 
     def interleave(few, many):
         for i, work in enumerate(many):
@@ -236,6 +233,8 @@
             total_up(block - 1, moved[later])
         interleave(ahead, weigh(block, pairs[now], moved[now]))
     total_up(blocks - 1, moved[(blocks - 1) % 2])
+    first_ref[...] = out_ref[: first_ref.shape[0], :]
+    last_ref[...] = out_ref[bins - last_ref.shape[0] :, :]
 
 
 def stack(got, band_start, slowness):

time: 65.5 us -> 65.5 us (level)
  no operation moved by 1% of the time
where the time goes in v9:
time: 65.5 us; the launch traced here: 65.3 us
  blocking collectives  37.2 us (57%)
  Pallas kernels  13.1 us (20%)
  starting transfers between devices  9.78 us (15%)
  waiting for transfers between devices  5.19 us (8%)
    all_to_all x1, blocking collectives, body(): got = lax.all_to_all(send, AXES, split_axis=0, concat_axis=0, tiled=True)  37.2 us
    pallas_call x1, Pallas kernels, stack(): pl.pallas_call(stack_kernel, in_specs=[VMEM] * 3, out_specs=[VMEM] * 3, o...  8.64 us
    ppermute x2, starting transfers between devices, exchange(): lax.ppermute(last, axis, [(i, (i + 1) % size) for i in range(size)])  5.56 us
    ppermute x2, starting transfers between devices, exchange(): lax.ppermute(first, axis, [((i + 1) % size, i) for i in range(size)])  4.22 us
    ppermute x2, waiting for transfers between devices, exchange(): lax.ppermute(first, axis, [((i + 1) % size, i) for i in range(size)])  3.52 us
    pallas_call x1, Pallas kernels, dispatch(): pl.pallas_call(functools.partial(dispatch_kernel, owners), in_specs=[HBM]...  3.05 us
    ppermute x2, waiting for transfers between devices, exchange(): lax.ppermute(last, axis, [(i, (i + 1) % size) for i in range(size)])  1.67 us
  transfers between devices with their start and end apart: 4, of which 3 were waited for; matrix products, arithmetic and copies ran while one was open for 0% of the time, Pallas kernels for 1%

profile of v9, /device:TPU:25, one launch (start us, length us, event | category | flops | bytes accessed | tf_op | source)
XLA Modules:
  0.0 65.3 jit_solution(15532181942412772885)
XLA Ops:
  0.0 3.0 %dispatch.1 = bf16[7936,128]{1,0:T(8,128)(2,1)S(1)} custom-call(bf16[512,1536]{1,0:T(8,128)(2,1)} %traces_hbm.1, s32[4,128]{1,0:T(4,128)} %bitcast.14, s32[4,128]{1,0:T(4,128)} %bitcast.15, bf16[4,128]{1,0:T(4,128)(2,1)} %bitcast.16), custom_call_target="tpu_custom_call" | custom-call | tf_op jit(solution)/shard_map/dispatch/pallas_call | solution.py:90
  3.1 0.0 copy-start
  3.1 0.0 copy-start.2
  3.1 37.2 %all_to_all.5 = bf16[128,31,2,128]{3,2,1,0:T(2,128)(2,1)S(1)} all-to-all(bf16[128,31,2,128]{3,2,1,0:T(2,128)(2,1)S(1)} %bitcast.9), channel_id=1, replica_groups=mesh['xline'=16,'iline'=8] {'xline','iline'}, dimensions={0} | all-to-all | bytes 4063232 | tf_op jit(solution)/shard_map/all_to_all | solution.py:409
  40.3 0.0 copy-start.1
  40.3 0.0 copy-done
  40.3 0.0 copy-done.2
  40.3 8.6 %stack.1 = (f32[8,1536]{1,0:T(8,128)S(1)}, f32[4,1536]{1,0:T(4,128)S(1)}, f32[4,1536]{1,0:T(4,128)S(1)}) custom-call(bf16[7936,128]{1,0:T(8,128)(2,1)S(1)} %bitcast.10, s32[12,128]{1,0:T(8,128)S(1)} %bitcast.13, f32[2,4,1536]{2,1,0:T(4,128)S(1)} %copy-done), custom_call_target="tpu_custom_call" | custom-call | tf_op jit(solution)/shard_map/stack/pallas_call | solution.py:247
  48.9 0.6 collective-permute-start
  49.5 4.2 %collective-permute-start.1 = (f32[4,1536]{1,0:T(4,128)S(1)}, f32[4,1536]{1,0:T(4,128)S(1)}, u32[]{:S(2)}, u32[]{:S(2)}) collective-permute-start(f32[4,1536]{1,0:T(4,128)S(1)} %get-tuple-element.12), channel_id=1, source_target_pairs={{8,0},{16,8},{24,16},{32,24},{40,32},{48,40},{56,48},{64,56},{72,6... | collective-permute-start | bytes 73736 | tf_op jit(solution)/shard_map/ppermute | solution.py:399
  53.7 1.2 %collective-permute-done.low_ref = f32[4,1536]{1,0:T(4,128)S(1)} collective-permute-done((f32[4,1536]{1,0:T(4,128)S(1)}, f32[4,1536]{1,0:T(4,128)S(1)}, u32[]{:S(2)}, u32[]{:S(2)}) %collective-permute-start) | collective-permute-done | bytes 24608 | tf_op jit(solution)/shard_map/ppermute | solution.py:398
  54.9 0.0 collective-permute-done.1.high_ref
  54.9 5.0 %collective-permute-start.2 = (f32[4,1536]{1,0:T(4,128)S(1)}, f32[4,1536]{1,0:T(4,128)S(1)}, u32[]{:S(2)}, u32[]{:S(2)}) collective-permute-start(f32[4,1536]{1,0:T(4,128)S(1)} %get-tuple-element.13), channel_id=1, source_target_pairs={{0,1},{1,2},{2,3},{3,4},{4,5},{5,6},{6,7},{7,0},{8,9},{9,10},{10,1... | collective-permute-start | bytes 73736 | tf_op jit(solution)/shard_map/ppermute | solution.py:398
  59.9 0.0 collective-permute-start.3
  59.9 0.0 copy-done.1
  59.9 0.5 smooth.1.part_ref
  60.4 0.5 collective-permute-done.2.before_ref
  60.9 3.5 %collective-permute-done.3.after_ref = f32[4,1536]{1,0:T(4,128)S(1)} collective-permute-done((f32[4,1536]{1,0:T(4,128)S(1)}, f32[4,1536]{1,0:T(4,128)S(1)}, u32[]{:S(2)}, u32[]{:S(2)}) %collective-permute-start.3) | collective-permute-done | bytes 24608 | tf_op jit(solution)/shard_map/ppermute | solution.py:399
  64.4 1.0 %border.1 = f32[2,4,1536]{2,1,0:T(4,128)} custom-call(f32[8,1536]{1,0:T(8,128)S(1)} %smooth.1.part_ref, f32[4,1536]{1,0:T(4,128)S(1)} %collective-permute-done.2.before_ref, f32[4,1536]{1,0:T(4,128)S(1)} %collective-permute-done.3.after_ref, s32[8,9]{1,0:T(8,128)S(1)} %bitcast.12), custom_call_target="tpu_custom_call" | custom-call | tf_op jit(solution)/shard_map/border/pallas_call | solution.py:386
  (1 shorter events, 0.0 us)
Async XLA Ops:
  3.1 37.2 %copy-start = (f32[2,4,1536]{2,1,0:T(4,128)S(1)}, f32[2,4,1536]{2,1,0:T(4,128)}, u32[]{:S(2)}) copy-start(f32[2,4,1536]{2,1,0:T(4,128)} %slow_ref.1) | copy-start | bytes 147460
  3.1 37.2 %copy-start.2 = (s32[1536]{0:T(1024)S(1)}, s32[1536]{0:T(1024)}, u32[]{:S(2)}) copy-start(s32[1536]{0:T(1024)} %param.12) | copy-start | bytes 18436
  40.3 19.7 %copy-start.1 = (s32[9,2,4]{0,2,1:T(4,128)S(1)}, s32[9,2,4]{0,2,1:T(4,128)}, u32[]{:S(2)}) copy-start(s32[9,2,4]{0,2,1:T(4,128)} %param.13) | copy-start | bytes 868
  48.9 6.0 %collective-permute-start = (f32[4,1536]{1,0:T(4,128)S(1)}, f32[4,1536]{1,0:T(4,128)S(1)}, u32[]{:S(2)}, u32[]{:S(2)}) collective-permute-start(f32[4,1536]{1,0:T(4,128)S(1)} %get-tuple-element.11), channel_id=1, source_target_pairs={{0,8},{8,16},{16,24},{24,32},{32,40},{40,48},{48,56},{56,64},{64,7... | collective-permute-start | bytes 73736 | tf_op jit(solution)/shard_map/ppermute | solution.py:398
  49.5 5.4 %collective-permute-start.1 = (f32[4,1536]{1,0:T(4,128)S(1)}, f32[4,1536]{1,0:T(4,128)S(1)}, u32[]{:S(2)}, u32[]{:S(2)}) collective-permute-start(f32[4,1536]{1,0:T(4,128)S(1)} %get-tuple-element.12), channel_id=1, source_target_pairs={{8,0},{16,8},{24,16},{32,24},{40,32},{48,40},{56,48},{64,56},{72,6... | collective-permute-start | bytes 73736 | tf_op jit(solution)/shard_map/ppermute | solution.py:399
  54.9 5.9 %collective-permute-start.2 = (f32[4,1536]{1,0:T(4,128)S(1)}, f32[4,1536]{1,0:T(4,128)S(1)}, u32[]{:S(2)}, u32[]{:S(2)}) collective-permute-start(f32[4,1536]{1,0:T(4,128)S(1)} %get-tuple-element.13), channel_id=1, source_target_pairs={{0,1},{1,2},{2,3},{3,4},{4,5},{5,6},{6,7},{7,0},{8,9},{9,10},{10,1... | collective-permute-start | bytes 73736 | tf_op jit(solution)/shard_map/ppermute | solution.py:398
  59.9 4.5 %collective-permute-start.3 = (f32[4,1536]{1,0:T(4,128)S(1)}, f32[4,1536]{1,0:T(4,128)S(1)}, u32[]{:S(2)}, u32[]{:S(2)}) collective-permute-start(f32[4,1536]{1,0:T(4,128)S(1)} %get-tuple-element.14), channel_id=1, source_target_pairs={{1,0},{2,1},{3,2},{4,3},{5,4},{6,5},{7,6},{0,7},{9,8},{10,9},{11,1... | collective-permute-start | bytes 73736 | tf_op jit(solution)/shard_map/ppermute | solution.py:399
